TPU v7x, 256 devices: a whole 4x4x8 slice. The times are simulated.
256 devices in a mesh: pair: 2 (over core), virt: 4 (over x), integ: 32 (over y, z).
Axes of the slice: x: 4, y: 4, z: 8, core: 2. Of those that a mesh axis runs over, the one named last changes fastest.
Arguments:
- amplitudes: bfloat16 [2, 32, 256, 256], P('pair', 'integ', 'virt'), may hold values from -4 to 4
- vv_factors: bfloat16 [512, 256, 256], P('integ'), may hold values from -0.25 to 0.25
- ov_factors: bfloat16 [512, 32, 256], P(None, 'integ'), may hold values from -0.75 to 0.75
- occ_energy_i: float32 [2], P('pair'), may hold values from -2 to -0.5
- occ_energy_j: float32 [32], P('integ'), may hold values from -2 to -0.5
- virt_energy: float32 [256], replicated, may hold values from 0.2 to 3
- vv_mask: int32 [2, 2], replicated, may hold values 0 or 1
- pair_domain: int32 [2, 32, 2], P('pair', 'integ'), may hold values 0 or 1
Outputs:
- update: bfloat16 [2, 32, 256, 256], P('pair', 'integ', 'virt')
All inputs are finite; a program needn't handle non-finite values. No bound on the sum of `pair_domain` on one device may be relied on, other than what follows from the above.
Results may differ from a plain program's by a relative error of at most 0.014.
Values may be sent and summed in bfloat16 or wider, within the bound.
No kernel may reach another device: no remote copies, remote signals or barrier semaphores. Data moves between devices by JAX's collectives and lax.ppermute only.
A program may use at most 64 MiB of HBM per device.

v0:
```python
import jax
import jax.numpy as jnp
from jax import lax
from jax.sharding import PartitionSpec as P

TILE_SIZE = 128


def split_halves(values):
    upper = values.astype(jnp.bfloat16)
    lower = (values - upper.astype(jnp.float32)).astype(jnp.bfloat16)
    return (upper, lower)


def body(
    amplitudes,
    vv_factors,
    ov_factors,
    occ_energy_i,
    occ_energy_j,
    virt_energy,
    vv_mask,
    pair_domain,
):
    share = amplitudes.shape[2]
    virt_index = lax.axis_index("virt")
    row_start = virt_index * share
    domain = jnp.repeat(pair_domain[0, 0], TILE_SIZE).astype(jnp.float32)
    domain_rows = lax.dynamic_slice_in_dim(domain, row_start, share, 0)
    masked = (amplitudes[0, 0].astype(jnp.float32) * domain_rows[:, None] * domain[None, :]).astype(
        jnp.bfloat16
    )
    grid = jnp.repeat(jnp.repeat(vv_mask, TILE_SIZE, axis=0), TILE_SIZE, axis=1).astype(
        jnp.bfloat16
    )
    factors = vv_factors * grid[None]
    factor_rows = lax.dynamic_slice_in_dim(factors, row_start, share, 1)
    masked_block = masked[None, None]
    full_rows = lax.all_gather(masked_block, "virt", axis=2, tiled=True)
    own_pair = full_rows[0, 0]
    all_pairs = lax.all_gather(full_rows, "integ", axis=1, tiled=True)[0]
    columns = lax.dynamic_slice_in_dim(own_pair, row_start, share, 1)
    mixed = (2.0 * masked.astype(jnp.float32) - columns.T.astype(jnp.float32)).astype(jnp.bfloat16)
    own_ov = ov_factors[:, 0, :]
    partial_zeta = jnp.einsum("ac,qc->aq", mixed, own_ov, preferred_element_type=jnp.float32)
    pieces = []
    for first in range(0, lax.axis_size("integ") * 1, 8):
        width = min(8, lax.axis_size("integ") * 1 - first)
        block = lax.dynamic_slice_in_dim(all_pairs, first, width, 0)
        weighted = jnp.einsum(
            "qac,jcd->jqad", factor_rows, block, preferred_element_type=jnp.float32
        ).astype(jnp.bfloat16)
        pieces.append(
            jnp.einsum("jqad,qbd->jab", weighted, factors, preferred_element_type=jnp.float32)
        )
    term = jnp.concatenate(pieces, axis=0)
    ladder = lax.psum_scatter(
        term.astype(jnp.bfloat16), "integ", scatter_dimension=0, tiled=True
    ).astype(jnp.float32)[0]
    zeta = lax.psum(partial_zeta, "integ")
    upper, lower = split_halves(zeta)
    cycle = jnp.dot(upper, own_ov, preferred_element_type=jnp.float32)
    cycle = cycle + jnp.dot(lower, own_ov, preferred_element_type=jnp.float32)
    total = ladder + cycle
    energy_rows = lax.dynamic_slice_in_dim(virt_energy, row_start, share, 0)
    denom = energy_rows[:, None] + virt_energy[None, :] - occ_energy_i[0] - occ_energy_j[0]
    update = (total * domain_rows[:, None] * domain[None, :] / denom).astype(jnp.bfloat16)
    return update[None, None]


def solution(mesh):
    placed = (
        P("pair", "integ", "virt", None),
        P("integ", None, None),
        P(None, "integ", None),
        P("pair"),
        P("integ"),
        P(),
        P(),
        P("pair", "integ", None),
    )
    return jax.shard_map(
        body,
        mesh=mesh,
        in_specs=placed,
        out_specs=P("pair", "integ", "virt", None),
        check_vma=False,
    )
```

profile of v0, /device:TPU:4, one launch (start us, length us, event | category | flops | bytes accessed | tf_op | source)
XLA Modules:
  0.0 472.4 jit_solution(15324939264644739411)
XLA Ops:
  6.5 0.0 copy-start
  6.5 0.0 all-gather.2.cloned.1.call-start
  6.5 0.7 convert_bitcast_fusion.2
  7.2 0.1 broadcast_bitcast_fusion
  7.3 0.1 dynamic_slice.32
  7.4 0.8 fusion.92
  8.2 13.0 %all_gather.6 = bf16[1,1,256,256]{3,2,1,0:T(8,128)(2,1)} all-gather(bf16[1,1,64,256]{3,2,1,0:T(8,128)(2,1)S(1)} %fusion.92), channel_id=1, replica_groups=mesh['pair'=2,'virt'=4,'integ'=32] {'virt'}, dimensions={2}, use_global_device_ids=true | all-gather | bytes 163840 | tf_op jit(solution)/shard_map/all_gather | solution.py:39
  21.3 0.0 all-gather.2.cloned.1.call-update
  21.3 0.0 all-reduce.2.cloned.1.call-start
  21.3 0.9 constant_dynamic-slice_fusion
  22.3 0.1 copy.22
  22.4 0.0 copy-done
  22.4 1.6 fusion.89
  24.0 0.0 all-reduce.2.cloned.1.call-update
  24.0 0.0 reduce-scatter.2.cloned.1.call-start
  24.1 0.7 convert_element_type.102
  24.8 0.3 broadcast_in_dim.10
  25.1 1.8 broadcast_multiply_fusion
  26.9 78.7 %all-gather.2.cloned.1.call-done = bf16[1,32,256,256]{3,2,0,1:T(8,128)(2,1)} async-done(((bf16[1,1,256,256]{3,2,0,1:T(8,128)(2,1)}), bf16[1,32,256,256]{3,2,0,1:T(8,128)(2,1)}) %all-gather.2.cloned.1.call-update) | async-done | bytes 4194320 | tf_op jit(solution)/shard_map/all_gather | solution.py:41
  105.6 5.4 %fusion.44 = bf16[8,64,256]{2,1,0:T(8,128)(2,1)S(1)} fusion(bf16[16,256,256]{2,1,0:T(8,128)(2,1)S(1)} %broadcast_multiply_fusion, bf16[1,32,256,256]{3,2,0,1:T(8,128)(2,1)} %all-gather.2.cloned.1.call-done, s32[]{:T(128)S(6)} %select_n.2), kind=kOutput, calls=%fused_computation.24 | convolution fusion | flops 2149711872 | bytes 3932164 | tf_op jit(solution)/shard_map/jqad,qbd->jab/dot_general | solution.py:54
  111.1 5.5 %fusion.49 = bf16[8,64,256]{2,1,0:T(8,128)(2,1)S(1)} fusion(bf16[16,256,256]{2,1,0:T(8,128)(2,1)S(1)} %broadcast_multiply_fusion, bf16[1,32,256,256]{3,2,0,1:T(8,128)(2,1)} %all-gather.2.cloned.1.call-done, s32[]{:T(128)S(6)} %select_n.2), kind=kOutput, calls=%fused_computation.25 | convolution fusion | flops 2149711872 | bytes 3932164 | tf_op jit(solution)/shard_map/jqad,qbd->jab/dot_general | solution.py:54
  116.5 5.5 %fusion.54 = bf16[8,64,256]{2,1,0:T(8,128)(2,1)S(1)} fusion(bf16[16,256,256]{2,1,0:T(8,128)(2,1)S(1)} %broadcast_multiply_fusion, bf16[1,32,256,256]{3,2,0,1:T(8,128)(2,1)} %all-gather.2.cloned.1.call-done, s32[]{:T(128)S(6)} %select_n.2), kind=kOutput, calls=%fused_computation.26 | convolution fusion | flops 2149711872 | bytes 3932164 | tf_op jit(solution)/shard_map/jqad,qbd->jab/dot_general | solution.py:54
  122.0 0.0 copy-start.1
  122.0 5.5 %fusion.59 = bf16[8,64,256]{2,1,0:T(8,128)(2,1)S(1)} fusion(bf16[16,256,256]{2,1,0:T(8,128)(2,1)S(1)} %broadcast_multiply_fusion, bf16[1,32,256,256]{3,2,0,1:T(8,128)(2,1)} %all-gather.2.cloned.1.call-done, s32[]{:T(128)S(6)} %select_n.2), kind=kOutput, calls=%fused_computation.27 | convolution fusion | flops 2149711872 | bytes 3932164 | tf_op jit(solution)/shard_map/jqad,qbd->jab/dot_general | solution.py:54
  127.5 1.1 pad_maximum_fusion
  128.6 0.0 reduce-scatter.2.cloned.1.call-update
  128.6 0.0 copy-done.1
  128.6 0.1 dynamic_slice.43
  130.0 117.1 %all-reduce.2.cloned.1.call-done = f32[64,512]{1,0:T(8,128)} async-done(((f32[64,512]{1,0:T(8,128)}), f32[64,512]{1,0:T(8,128)}) %all-reduce.2.cloned.1.call-update) | async-done | bytes 131088 | tf_op jit(solution)/shard_map/psum | solution.py:60
  247.1 1.1 fusion.87
  248.2 215.9 %reduce-scatter.2.cloned.1.call-done = bf16[1,64,256]{2,1,0:T(8,128)(2,1)} async-done(((bf16[32,64,256]{2,1,0:T(8,128)(2,1)}), bf16[1,64,256]{2,1,0:T(8,128)(2,1)}) %reduce-scatter.2.cloned.1.call-update) | async-done | bytes 32784 | tf_op jit(solution)/shard_map/reduce_scatter | solution.py:57
  464.1 1.8 fusion.69
  (2 shorter events, 0.0 us)
Async XLA Ops:
  6.5 15.8 %copy-start = (bf16[512,1,256]{2,0,1:T(8,128)(2,1)S(1)}, bf16[512,1,256]{2,0,1:T(8,128)(2,1)}, u32[]{:S(2)}) copy-start(bf16[512,1,256]{2,0,1:T(8,128)(2,1)} %param.10) | copy-start | bytes 786436
  6.5 99.1 %all-gather.2.cloned.1.call-start = ((), (), s32[]{:S(2)}) async-start(), calls=%async_computation.1 | async-start | bytes 4325376 | tf_op jit(solution)/shard_map/all_gather | solution.py:41
  21.3 225.8 %all-reduce.2.cloned.1.call-start = ((), (), s32[]{:S(2)}) async-start(), calls=%async_computation.3 | async-start | bytes 262144 | tf_op jit(solution)/shard_map/psum | solution.py:60
  24.0 440.1 %reduce-scatter.2.cloned.1.call-start = ((), (), s32[]{:S(2)}) async-start(), calls=%async_computation.2 | async-start | bytes 1081344 | tf_op jit(solution)/shard_map/reduce_scatter | solution.py:57
  122.0 6.6 %copy-start.1 = (f32[256]{0:T(256)S(1)}, f32[256]{0:T(256)}, u32[]{:S(2)}) copy-start(f32[256]{0:T(256)} %param.13) | copy-start | bytes 3076
Sparse Core Ops, SparseCore 0:
  21.4 84.1 all-gather.1
  109.1 137.9 all-reduce.1
  251.4 212.6 reduce-scatter.1
where the time goes:
time: 473 us; the launch traced here: 472 us
  waiting for transfers between devices  412 us (87%)
  matrix products  26.2 us (6%)
  between operations  14.5 us (3%)
  blocking collectives  13 us (3%)
  other arithmetic  5.11 us (1%)
    reduce_scatter x1, waiting for transfers between devices, body(): lax.psum_scatter(term.astype(jnp.bfloat16), 'integ', scatter_dimension=0,...  216 us
    psum x1, waiting for transfers between devices, body(): zeta = lax.psum(partial_zeta, 'integ')  117 us
    all_gather x1, waiting for transfers between devices, body(): all_pairs = lax.all_gather(full_rows, 'integ', axis=1, tiled=True)[0]  78.7 us
    dot_general x4, matrix products, body(): jnp.einsum('jqad,qbd->jab', weighted, factors, preferred_element_type=jnp...  21.8 us
    all_gather x1, blocking collectives, body(): full_rows = lax.all_gather(masked_block, 'virt', axis=2, tiled=True)  13 us
  transfers between devices with their start and end apart: 3, of which 3 were waited for; matrix products, arithmetic and copies ran while one was open for 6% of the time, Pallas kernels for 0%

commit v1 on v0

v1 whole, which is shorter than its diff:
```python
import jax
import jax.numpy as jnp
from jax import lax
from jax.experimental import pallas as pl
from jax.experimental.pallas import tpu as pltpu
from jax.sharding import Mesh
from jax.sharding import PartitionSpec as P

TILE_SIZE = 128
BF16 = jnp.bfloat16
F32 = jnp.float32
NT = (((1,), (1,)), ((), ()))
TN = (((0,), (0,)), ((), ()))
VIRT = 4
Y = 4
Z = 8


def transposition():
    pairs = []
    for x in range(VIRT):
        for y in range(Y):
            for z in range(Z):
                pairs.append(((x * Y + y) * Z + z, (y * Y + x) * Z + z))
    return pairs


def zeta_kernel(rows_ref, ov_ref, out_ref):
    total = jnp.zeros(out_ref.shape, F32)
    for k in range(Z):
        amp = rows_ref[:, k].reshape(256, 256)
        fac = ov_ref[k]
        direct = lax.dot_general(fac, amp, NT, preferred_element_type=F32)
        swapped = jnp.dot(fac, amp, preferred_element_type=F32)
        total = total + (2.0 * direct - swapped)
    out_ref[...] = total


def ladder_kernel(mask_ref, rows_ref, factors_ref, zeta_ref, ov_ref, out_ref, masked, weighted):
    n_aux = factors_ref.shape[0]

    @pl.when(pl.program_id(0) == 0)
    def _():
        for p in range(2):
            for q in range(2):
                keep = jnp.full((1, TILE_SIZE), mask_ref[p, q], jnp.int32).astype(F32).astype(BF16)
                for aux in range(n_aux):
                    block = factors_ref[aux, p * 128 : (p + 1) * 128, q * 128 : (q + 1) * 128] * keep
                    masked[p * 128 : (p + 1) * 128, aux * 256 + q * 128 : aux * 256 + (q + 1) * 128] = block

    amp = rows_ref[...].reshape(256, 256)
    for aux in range(n_aux):
        cols = slice(aux * 256, (aux + 1) * 256)
        weighted[:, cols] = jnp.dot(masked[:, cols], amp, preferred_element_type=F32).astype(BF16)
    total = lax.dot_general(weighted[...], masked[...], NT, preferred_element_type=F32)
    zeta = zeta_ref[0]
    for other in range(1, VIRT):
        zeta = zeta + zeta_ref[other]
    upper = zeta.astype(BF16)
    lower = (zeta - upper.astype(F32)).astype(BF16)
    fac = ov_ref[0]
    total = total + lax.dot_general(upper, fac, TN, preferred_element_type=F32)
    total = total + lax.dot_general(lower, fac, TN, preferred_element_type=F32)
    out_ref[...] = total.astype(BF16).reshape(out_ref.shape)


def body(
    amplitudes,
    vv_factors,
    ov_factors,
    occ_energy_i,
    occ_energy_j,
    virt_energy,
    vv_mask,
    pair_domain,
):
    share = amplitudes.shape[2]
    virtuals = amplitudes.shape[3]
    n_aux = vv_factors.shape[0]
    virt_index = lax.axis_index("virt")
    row_start = virt_index * share
    domain = jnp.repeat(pair_domain[0, 0], TILE_SIZE).astype(F32)
    domain_rows = lax.dynamic_slice_in_dim(domain, row_start, share, 0)
    masked = (amplitudes[0, 0].astype(F32) * domain_rows[:, None] * domain[None, :]).astype(BF16)
    ov_share = lax.dynamic_slice_in_dim(ov_factors[:, 0, :], virt_index * (n_aux * Z), n_aux * Z, 0)
    swap = transposition()
    payload = jnp.concatenate([masked, ov_share], axis=0)
    payload = lax.ppermute(payload, ("virt", "y", "z"), swap)
    rows = jnp.broadcast_to(payload[None, :share], (Z, share, virtuals))
    parts = payload[share:].reshape(Z, n_aux, virtuals)
    sent = jnp.concatenate([rows, parts], axis=1)
    got = lax.all_to_all(sent, "z", 0, 0, tiled=True)
    rows = got[:, :share]
    ov = got[:, share:]
    rows = lax.all_to_all(jnp.broadcast_to(rows[None], (Y,) + rows.shape), "y", 0, 0, tiled=True)

    zeta = pl.pallas_call(
        zeta_kernel,
        name="zeta",
        out_shape=jax.ShapeDtypeStruct((n_aux, virtuals), F32),
        compiler_params=pltpu.CompilerParams(vmem_limit_bytes=16 << 20),
    )(rows, ov)
    zeta = lax.all_to_all(jnp.broadcast_to(zeta[None], (VIRT, n_aux, virtuals)), "virt", 0, 0, tiled=True)

    partial = pl.pallas_call(
        ladder_kernel,
        name="ladder",
        grid=(Z,),
        in_specs=[
            pl.BlockSpec(memory_space=pltpu.SMEM),
            pl.BlockSpec((Y, 1, share, virtuals), lambda j: (0, j, 0, 0)),
            pl.BlockSpec((n_aux, virtuals, virtuals), lambda j: (0, 0, 0)),
            pl.BlockSpec((VIRT, n_aux, virtuals), lambda j: (0, 0, 0)),
            pl.BlockSpec((1, n_aux, virtuals), lambda j: (j, 0, 0)),
        ],
        out_specs=pl.BlockSpec((Y, 1, share, virtuals), lambda j: (0, j, 0, 0)),
        out_shape=jax.ShapeDtypeStruct((Y, Z, share, virtuals), BF16),
        scratch_shapes=[
            pltpu.VMEM((virtuals, n_aux * virtuals), BF16),
            pltpu.VMEM((virtuals, n_aux * virtuals), BF16),
        ],
        compiler_params=pltpu.CompilerParams(vmem_limit_bytes=40 << 20),
    )(vv_mask, rows, vv_factors, zeta, ov)

    moved = lax.all_to_all(partial, "y", 0, 0, tiled=True)
    summed = jnp.sum(moved.astype(F32), axis=0).astype(BF16)
    moved = lax.all_to_all(summed, "z", 0, 0, tiled=True)
    total = jnp.sum(moved.astype(F32), axis=0).astype(BF16)
    total = lax.ppermute(total, ("virt", "y", "z"), swap).astype(F32)

    energy_rows = lax.dynamic_slice_in_dim(virt_energy, row_start, share, 0)
    denom = energy_rows[:, None] + virt_energy[None, :] - occ_energy_i[0] - occ_energy_j[0]
    update = (total * domain_rows[:, None] * domain[None, :] / denom).astype(BF16)
    return update[None, None]


def solution(mesh):
    fine = Mesh(mesh.devices.reshape(2, VIRT, Y, Z), ("pair", "virt", "y", "z"))
    integ = ("y", "z")
    placed = (
        P("pair", integ, "virt", None),
        P(integ, None, None),
        P(None, integ, None),
        P("pair"),
        P(integ),
        P(),
        P(),
        P("pair", integ, None),
    )
    return jax.shard_map(
        body,
        mesh=fine,
        in_specs=placed,
        out_specs=P("pair", integ, "virt", None),
        check_vma=False,
    )
```

time: 473 us -> 113 us (0.24)
  waiting for transfers between devices: 412 us -> 21.3 us
  blocking collectives: 13 us -> 58.2 us
  matrix products: 26.2 us -> 0 us
  starting transfers between devices: 0.09 us -> 13.4 us
  between operations: 14.5 us -> 1.43 us
  Pallas kernels: 0 us -> 13 us
    reduce_scatter x1 -> x0, waiting for transfers between devices: 216 us -> none  [body(): lax.psum_scatter(term.astype(jnp.bfloat16), 'integ', scatter_dimension=0,...]
    psum x1 -> x0, waiting for transfers between devices: 117 us -> none  [body(): zeta = lax.psum(partial_zeta, 'integ')]
    all_gather x1 -> x0, waiting for transfers between devices: 78.7 us -> none  [body(): all_pairs = lax.all_gather(full_rows, 'integ', axis=1, tiled=True)[0]]
    all_to_all x0 -> x4, blocking collectives: none -> 58.2 us  [the longest x1 20 us: body(): got = lax.all_to_all(sent, 'z', 0, 0, tiled=True)]
    dot_general x7 -> x0, matrix products: 26.2 us -> none  [the longest x4 21.8 us: body(): jnp.einsum('jqad,qbd->jab', weighted, factors, preferred_element_type=jnp...]
    all_gather x1 -> x0, blocking collectives: 13 us -> none  [body(): full_rows = lax.all_gather(masked_block, 'virt', axis=2, tiled=True)]
    pallas_call x0 -> x2, Pallas kernels: none -> 13 us  [the longest x1 12.5 us: body(): pl.pallas_call(ladder_kernel, name='ladder', grid=(Z,), in_specs=[pl.Bloc...]
    all_to_all x0 -> x1, waiting for transfers between devices: none -> 10.8 us  [body(): lax.all_to_all(jnp.broadcast_to(rows[None], (Y,) + rows.shape), 'y', 0, 0...]
  transfers between devices with their start and end apart: 3 -> 3, of which waited for: 3 -> 3; matrix products, arithmetic and copies ran while one was open for 6% -> 1% of each run, Pallas kernels for 0% -> 0%
where the time goes in v1:
time: 113 us
  blocking collectives  58.2 us (52%)
  waiting for transfers between devices  21.3 us (19%)
  starting transfers between devices  13.4 us (12%)
  Pallas kernels  13 us (12%)
  local copies, waits for them, and re-layouts  2.99 us (3%)
  other arithmetic  2.51 us (2%)
  between operations  1.43 us (1%)
    all_to_all x1, blocking collectives, body(): got = lax.all_to_all(sent, 'z', 0, 0, tiled=True)  20 us
    all_to_all x1, blocking collectives, body(): moved = lax.all_to_all(summed, 'z', 0, 0, tiled=True)  16 us
    all_to_all x1, blocking collectives, body(): moved = lax.all_to_all(partial, 'y', 0, 0, tiled=True)  13.3 us
    pallas_call x1, Pallas kernels, body(): pl.pallas_call(ladder_kernel, name='ladder', grid=(Z,), in_specs=[pl.Bloc...  12.5 us
    all_to_all x1, waiting for transfers between devices, body(): lax.all_to_all(jnp.broadcast_to(rows[None], (Y,) + rows.shape), 'y', 0, 0...  10.8 us
    all_to_all x1, blocking collectives, body(): lax.all_to_all(jnp.broadcast_to(zeta[None], (VIRT, n_aux, virtuals)), 'vi...  8.92 us
    ppermute x1, waiting for transfers between devices, body(): payload = lax.ppermute(payload, ('virt', 'y', 'z'), swap)  6.83 us
    ppermute x1, starting transfers between devices, body(): payload = lax.ppermute(payload, ('virt', 'y', 'z'), swap)  5.05 us
  transfers between devices with their start and end apart: 3, of which 3 were waited for; matrix products, arithmetic and copies ran while one was open for 1% of the time, Pallas kernels for 0%

profile of v1, /device:TPU:4, one launch (start us, length us, event | category | flops | bytes accessed | tf_op | source)
XLA Modules:
  0.0 112.8 jit_solution(2128807597678656491)
XLA Ops:
  0.0 0.0 copy-start
  0.0 0.7 convert_bitcast_fusion
  0.7 0.1 broadcast_bitcast_fusion
  0.8 0.1 dynamic_slice.11
  0.9 0.8 fusion.1
  1.7 0.0 copy-done
  1.7 5.0 %collective-permute-start = (bf16[192,256]{1,0:T(8,128)(2,1)S(1)}, bf16[192,256]{1,0:T(8,128)(2,1)S(1)}, u32[]{:S(2)}, u32[]{:S(2)}) collective-permute-start(bf16[192,256]{1,0:T(8,128)(2,1)S(1)} %pad_maximum_fusion.1), channel_id=1, source_target_pairs={{0,0},{1,1},{2,2},{3,3},{4,4},{5,5},{6,6},{7,7},{8,32},{9,33},{10,... | collective-permute-start | bytes 294920 | tf_op jit(solution)/shard_map/ppermute | solution.py:88
  6.8 6.8 %collective-permute-done = bf16[192,256]{1,0:T(8,128)(2,1)S(1)} collective-permute-done((bf16[192,256]{1,0:T(8,128)(2,1)S(1)}, bf16[192,256]{1,0:T(8,128)(2,1)S(1)}, u32[]{:S(2)}, u32[]{:S(2)}) %collective-permute-start) | collective-permute-done | bytes 98336 | tf_op jit(solution)/shard_map/ppermute | solution.py:88
  13.7 20.0 %all_to_all.25 = bf16[8,80,256]{2,1,0:T(8,128)(2,1)S(1)} all-to-all(bf16[8,80,256]{2,1,0:T(8,128)(2,1)S(1)} %pad_maximum_fusion), channel_id=1, replica_groups=mesh['pair'=2,'virt'=4,'y'=4,'z'=8] {'z'}, dimensions={0} | all-to-all | bytes 655360 | tf_op jit(solution)/shard_map/all_to_all | solution.py:92
  33.7 0.0 copy-start.3
  33.7 0.7 copy-done.3
  34.4 1.1 broadcast_in_dim.12
  35.5 0.0 copy-start.1
  35.5 0.0 copy-start.2
  35.5 3.6 %all-to-all-start.1 = ((bf16[4,8,64,256]{3,2,1,0:T(8,128)(2,1)}), bf16[4,8,64,256]{3,2,1,0:T(8,128)(2,1)S(1)}, u32[]{:S(2)}, u32[]{:S(2)}) async-start(bf16[4,8,64,256]{3,2,1,0:T(8,128)(2,1)} %broadcast_in_dim.12), calls=%async_computation.1 | async-start | bytes 2097152 | tf_op jit(solution)/shard_map/all_to_all | solution.py:95
  39.2 0.9 slice.19.ov_ref
  40.0 10.8 %all-to-all-done.1.rows_ref = bf16[4,8,64,256]{3,2,1,0:T(8,128)(2,1)S(1)} async-done(((bf16[4,8,64,256]{3,2,1,0:T(8,128)(2,1)}), bf16[4,8,64,256]{3,2,1,0:T(8,128)(2,1)S(1)}, u32[]{:S(2)}, u32[]{:S(2)}) %all-to-all-start.1) | async-done | bytes 1048608 | tf_op jit(solution)/shard_map/all_to_all | solution.py:95
  50.9 0.5 zeta.1
  51.4 8.9 %all_to_all.26.zeta_ref = f32[4,16,256]{2,1,0:T(8,128)S(1)} all-to-all(f32[4,16,256]{2,1,0:T(8,128)S(1)} %broadcast_in_dim.13), channel_id=1, replica_groups=mesh['pair'=2,'virt'=4,'y'=4,'z'=8] {'virt'}, dimensions={0} | all-to-all | bytes 131072 | tf_op jit(solution)/shard_map/all_to_all | solution.py:103
  60.3 0.0 copy-done.1
  60.3 0.0 copy-done.2
  60.3 12.5 %ladder.1 = bf16[4,8,64,256]{3,2,1,0:T(8,128)(2,1)S(1)} custom-call(s32[2,2]{1,0:T(2,128)S(1)} %copy-done.2, bf16[4,8,64,256]{3,2,1,0:T(8,128)(2,1)S(1)} %all-to-all-done.1.rows_ref, bf16[16,256,256]{2,1,0:T(8,128)(2,1)S(1)} %copy-done.1, f32[4,16,256]{2,1,0:T(8,128)S(1)} %all_to_all.26.zeta_ref, bf16[8,16,256]{2,1,0:T(8,128)(2,1)S(1)} %slice.19.ov_ref), custom_call_target="tpu_custom_call" | custom-call | tf_op jit(solution)/shard_map/ladder/pallas_call | solution.py:105
  72.9 0.0 copy-start.4
  72.9 13.3 %all_to_all.27 = bf16[4,8,64,256]{3,2,1,0:T(8,128)(2,1)S(1)} all-to-all(bf16[4,8,64,256]{3,2,1,0:T(8,128)(2,1)S(1)} %ladder.1), channel_id=1, replica_groups=mesh['pair'=2,'virt'=4,'y'=4,'z'=8] {'y'}, dimensions={0} | all-to-all | bytes 2097152 | tf_op jit(solution)/shard_map/all_to_all | solution.py:125
  86.2 0.2 reduce_sum.24
  86.4 16.0 %all_to_all.28 = bf16[8,64,256]{2,1,0:T(8,128)(2,1)S(1)} all-to-all(bf16[8,64,256]{2,1,0:T(8,128)(2,1)S(1)} %reduce_sum.24), channel_id=1, replica_groups=mesh['pair'=2,'virt'=4,'y'=4,'z'=8] {'z'}, dimensions={0} | all-to-all | bytes 524288 | tf_op jit(solution)/shard_map/all_to_all | solution.py:127
  102.4 4.7 %collective-permute-start.1 = (bf16[64,256]{1,0:T(8,128)(2,1)S(1)}, bf16[64,256]{1,0:T(8,128)(2,1)S(1)}, u32[]{:S(2)}, u32[]{:S(2)}) collective-permute-start(bf16[64,256]{1,0:T(8,128)(2,1)S(1)} %reduce_sum.25), channel_id=1, source_target_pairs={{0,0},{1,1},{2,2},{3,3},{4,4},{5,5},{6,6},{7,7},{8,32},{9,33},{10,... | collective-permute-start | bytes 98312 | tf_op jit(solution)/shard_map/ppermute | solution.py:129
  108.4 0.0 copy-done.4
  108.4 0.1 dynamic_slice.14
  108.5 3.6 %collective-permute-done.1 = bf16[64,256]{1,0:T(8,128)(2,1)S(1)} collective-permute-done((bf16[64,256]{1,0:T(8,128)(2,1)S(1)}, bf16[64,256]{1,0:T(8,128)(2,1)S(1)}, u32[]{:S(2)}, u32[]{:S(2)}) %collective-permute-start.1) | collective-permute-done | bytes 32800 | tf_op jit(solution)/shard_map/ppermute | solution.py:129
  112.1 0.7 fusion.2
  (9 shorter events, 0.2 us)
Async XLA Ops:
  0.0 1.7 %copy-start = (bf16[512,1,256]{2,0,1:T(8,128)(2,1)S(1)}, bf16[512,1,256]{2,0,1:T(8,128)(2,1)}, u32[]{:S(2)}) copy-start(bf16[512,1,256]{2,0,1:T(8,128)(2,1)} %param.10) | copy-start | bytes 786436
  1.7 11.9 %collective-permute-start = (bf16[192,256]{1,0:T(8,128)(2,1)S(1)}, bf16[192,256]{1,0:T(8,128)(2,1)S(1)}, u32[]{:S(2)}, u32[]{:S(2)}) collective-permute-start(bf16[192,256]{1,0:T(8,128)(2,1)S(1)} %pad_maximum_fusion.1), channel_id=1, source_target_pairs={{0,0},{1,1},{2,2},{3,3},{4,4},{5,5},{6,6},{7,7},{8,32},{9,33},{10,... | collective-permute-start | bytes 294920 | tf_op jit(solution)/shard_map/ppermute | solution.py:88
  33.7 0.7 copy-start.3
  35.5 24.8 %copy-start.1 = (bf16[16,256,256]{2,1,0:T(8,128)(2,1)S(1)}, bf16[16,256,256]{2,1,0:T(8,128)(2,1)}, u32[]{:S(2)}) copy-start(bf16[16,256,256]{2,1,0:T(8,128)(2,1)} %factors_ref.1) | copy-start | bytes 6291460
  35.5 24.8 %copy-start.2 = (s32[2,2]{1,0:T(2,128)S(1)}, s32[2,2]{1,0:T(2,128)}, u32[]{:S(2)}) copy-start(s32[2,2]{1,0:T(2,128)} %mask_ref.1) | copy-start | bytes 52
  35.5 15.3 %all-to-all-start.1 = ((bf16[4,8,64,256]{3,2,1,0:T(8,128)(2,1)}), bf16[4,8,64,256]{3,2,1,0:T(8,128)(2,1)S(1)}, u32[]{:S(2)}, u32[]{:S(2)}) async-start(bf16[4,8,64,256]{3,2,1,0:T(8,128)(2,1)} %broadcast_in_dim.12), calls=%async_computation.1 | async-start | bytes 2097152 | tf_op jit(solution)/shard_map/all_to_all | solution.py:95
  72.9 35.5 %copy-start.4 = (f32[256]{0:T(256)S(1)}, f32[256]{0:T(256)}, u32[]{:S(2)}) copy-start(f32[256]{0:T(256)} %param.13) | copy-start | bytes 3076
  102.4 9.7 %collective-permute-start.1 = (bf16[64,256]{1,0:T(8,128)(2,1)S(1)}, bf16[64,256]{1,0:T(8,128)(2,1)S(1)}, u32[]{:S(2)}, u32[]{:S(2)}) collective-permute-start(bf16[64,256]{1,0:T(8,128)(2,1)S(1)} %reduce_sum.25), channel_id=1, source_target_pairs={{0,0},{1,1},{2,2},{3,3},{4,4},{5,5},{6,6},{7,7},{8,32},{9,33},{10,... | collective-permute-start | bytes 98312 | tf_op jit(solution)/shard_map/ppermute | solution.py:129

commit v2 on v0

v2 whole, which is shorter than its diff:
```python
import jax
import jax.numpy as jnp
from jax import lax
from jax.experimental import pallas as pl
from jax.experimental.pallas import tpu as pltpu
from jax.sharding import Mesh
from jax.sharding import PartitionSpec as P

TILE_SIZE = 128
BF16 = jnp.bfloat16
F32 = jnp.float32
NT = (((1,), (1,)), ((), ()))
TN = (((0,), (0,)), ((), ()))
VIRT = 4
Y = 4
Z = 8
ROWS = 64
COLS = 256
AUX = 16


def out_kernel(domain_ref, amp_ref, ov_ref, out_ref):
    x = lax.axis_index("virt")
    z = lax.axis_index("z")
    row_tile = domain_ref[0, 0, x // 2]
    for half in range(2):
        cols = slice(half * TILE_SIZE, (half + 1) * TILE_SIZE)
        keep = (row_tile * domain_ref[0, 0, half]).astype(F32)
        rows = (amp_ref[0, 0, :, cols].astype(F32) * keep).astype(BF16)
        for to in range(Z):
            out_ref[to, :ROWS, cols] = rows
    owner = (x + Y - z % 2) % Y
    start = pl.multiple_of(owner * (Z * AUX), Z * AUX)
    out_ref[:, ROWS:] = ov_ref[pl.ds(start, Z * AUX), :].reshape(Z, AUX, COLS)


def spread_kernel(got_ref, out_ref):
    x = lax.axis_index("virt")
    for to_x in range(VIRT):
        rows = got_ref[2 * to_x : 2 * to_x + 2, :ROWS].reshape(2 * ROWS, COLS)
        for to_y in range(Y):
            out_ref[to_x * Y + to_y, : 2 * ROWS] = rows
            low = (x + Y - to_y) % 2
            out_ref[to_x * Y + to_y, 2 * ROWS :] = got_ref[2 * to_x + low, ROWS:]


def ladder_kernel(mask_ref, rows_ref, factors_ref, out_ref, masked, weighted):
    y = lax.axis_index("y")
    for p in range(2):
        for q in range(2):
            keep = jnp.full((1, TILE_SIZE), mask_ref[p, q], jnp.int32).astype(F32).astype(BF16)
            for aux in range(AUX):
                block = factors_ref[aux, p * 128 : (p + 1) * 128, q * 128 : (q + 1) * 128] * keep
                masked[p * 128 : (p + 1) * 128, aux * 256 + q * 128 : aux * 256 + (q + 1) * 128] = block

    zeta = jnp.zeros((AUX, COLS), F32)
    for at_y in range(Y):
        for low in range(2):
            rows = slice(low * ROWS, (low + 1) * ROWS)
            amp = jnp.concatenate([rows_ref[at_x * Y + at_y, rows] for at_x in range(VIRT)], axis=0)
            fac = rows_ref[((y + low) % Y) * Y + at_y, 2 * ROWS :]
            direct = lax.dot_general(fac, amp, NT, preferred_element_type=F32)
            swapped = jnp.dot(fac, amp, preferred_element_type=F32)
            zeta = zeta + (2.0 * direct - swapped)
            for aux in range(AUX):
                cols = slice(aux * 256, (aux + 1) * 256)
                weighted[:, cols] = jnp.dot(masked[:, cols], amp, preferred_element_type=F32).astype(BF16)
            total = lax.dot_general(weighted[...], masked[...], NT, preferred_element_type=F32).astype(BF16)
            for at_x in range(VIRT):
                out_ref[at_x * Y + at_y, rows] = total[at_x * ROWS : (at_x + 1) * ROWS]
    lane = lax.broadcasted_iota(jnp.int32, (AUX, COLS), 1)
    for at_x in range(VIRT):
        turned = pltpu.roll(zeta, ((y + VIRT - at_x) % VIRT) * ROWS, 1)
        piece = jnp.where(lane // ROWS == y, turned, 0.0).astype(BF16)
        for at_y in range(Y):
            out_ref[at_x * Y + at_y, 2 * ROWS :] = piece


def sum_kernel(got_ref, out_ref):
    for high in range(VIRT):
        for low in range(2):
            rows = slice(low * ROWS, (low + 1) * ROWS)
            total = got_ref[high * Y, rows].astype(F32)
            for at_y in range(1, Y):
                total = total + got_ref[high * Y + at_y, rows].astype(F32)
            out_ref[2 * high + low, :ROWS] = total.astype(BF16)
    zeta = jnp.zeros((AUX, COLS), F32)
    for source in range(VIRT * Y):
        zeta = zeta + got_ref[source, 2 * ROWS :].astype(F32)
    zeta = zeta.astype(BF16)
    for to in range(Z):
        out_ref[to, ROWS:] = zeta


def update_kernel(domain_ref, occ_i_ref, occ_j_ref, virt_ref, got_ref, ov_ref, out_ref):
    x = lax.axis_index("virt")
    total = got_ref[0, :ROWS].astype(F32)
    for source in range(1, Z):
        total = total + got_ref[source, :ROWS].astype(F32)
    zeta = got_ref[:, ROWS:].reshape(Z * AUX, COLS)
    for at_y in range(Y):
        part = zeta[:, at_y * ROWS : (at_y + 1) * ROWS]
        fac = ov_ref[at_y * Z * AUX : (at_y + 1) * Z * AUX, :]
        total = total + lax.dot_general(part, fac, TN, preferred_element_type=F32)
    energy = jnp.broadcast_to(virt_ref[...], (ROWS, COLS))
    row = lax.broadcasted_iota(jnp.int32, (ROWS, COLS), 0) + x * ROWS
    lane = lax.broadcasted_iota(jnp.int32, (ROWS, COLS), 1)
    energy_rows = jnp.sum(jnp.where(row == lane, energy, 0.0), axis=1, keepdims=True)
    denom = energy_rows + energy - occ_i_ref[0] - occ_j_ref[0]
    row_tile = domain_ref[0, 0, x // 2]
    left = (row_tile * domain_ref[0, 0, 0]).astype(F32)
    right = (row_tile * domain_ref[0, 0, 1]).astype(F32)
    keep = jnp.where(lane < TILE_SIZE, left, right)
    out_ref[0, 0] = (total * keep / denom).astype(BF16)


def kernel(function, shape, scalars, arrays, scratch=(), mib=16):
    smem = pl.BlockSpec(memory_space=pltpu.SMEM)
    vmem = pl.BlockSpec(memory_space=pltpu.VMEM)
    call = pl.pallas_call(
        function,
        name=function.__name__,
        in_specs=[smem] * len(scalars) + [vmem] * len(arrays),
        out_specs=vmem,
        out_shape=jax.ShapeDtypeStruct(shape, BF16),
        scratch_shapes=list(scratch),
        compiler_params=pltpu.CompilerParams(vmem_limit_bytes=mib << 20),
    )
    return call(*scalars, *arrays)


def body(
    amplitudes,
    vv_factors,
    ov_factors,
    occ_energy_i,
    occ_energy_j,
    virt_energy,
    vv_mask,
    pair_domain,
):
    ov = ov_factors[:, 0, :]
    sent = kernel(out_kernel, (Z, ROWS + AUX, COLS), (pair_domain,), (amplitudes, ov))
    got = lax.all_to_all(sent, "z", 0, 0, tiled=True)
    sent = kernel(spread_kernel, (VIRT * Y, 2 * ROWS + AUX, COLS), (), (got,))
    got = lax.all_to_all(sent, ("virt", "y"), 0, 0, tiled=True)
    wide = pltpu.VMEM((COLS, AUX * COLS), BF16)
    sent = kernel(ladder_kernel, (VIRT * Y, 2 * ROWS + AUX, COLS), (vv_mask,), (got, vv_factors), (wide, wide), 40)
    got = lax.all_to_all(sent, ("virt", "y"), 0, 0, tiled=True)
    sent = kernel(sum_kernel, (Z, ROWS + AUX, COLS), (), (got,))
    got = lax.all_to_all(sent, "z", 0, 0, tiled=True)
    return kernel(
        update_kernel,
        (1, 1, ROWS, COLS),
        (pair_domain, occ_energy_i, occ_energy_j),
        (virt_energy[None, :], got, ov),
    )


def solution(mesh):
    fine = Mesh(mesh.devices.reshape(2, VIRT, Y, Z), ("pair", "virt", "y", "z"))
    integ = ("y", "z")
    placed = (
        P("pair", integ, "virt", None),
        P(integ, None, None),
        P(None, integ, None),
        P("pair"),
        P(integ),
        P(),
        P(),
        P("pair", integ, None),
    )
    return jax.shard_map(
        body,
        mesh=fine,
        in_specs=placed,
        out_specs=P("pair", integ, "virt", None),
        check_vma=False,
    )
```

time: 473 us -> 94.7 us (0.20)
  waiting for transfers between devices: 412 us -> 9.89 us
  blocking collectives: 13 us -> 62 us
  matrix products: 26.2 us -> 0 us
  between operations: 14.5 us -> 1.35 us
  Pallas kernels: 0 us -> 12.9 us
  other arithmetic: 5.11 us -> 0 us
  starting transfers between devices: 0.09 us -> 5.05 us
    reduce_scatter x1 -> x0, waiting for transfers between devices: 216 us -> none  [body(): lax.psum_scatter(term.astype(jnp.bfloat16), 'integ', scatter_dimension=0,...]
    psum x1 -> x0, waiting for transfers between devices: 117 us -> none  [body(): zeta = lax.psum(partial_zeta, 'integ')]
    all_gather x1 -> x0, waiting for transfers between devices: 78.7 us -> none  [body(): all_pairs = lax.all_gather(full_rows, 'integ', axis=1, tiled=True)[0]]
    all_to_all x0 -> x3, blocking collectives: none -> 62 us  [the longest x2 40.5 us: body(): got = lax.all_to_all(sent, ('virt', 'y'), 0, 0, tiled=True)]
    dot_general x7 -> x0, matrix products: 26.2 us -> none  [the longest x4 21.8 us: body(): jnp.einsum('jqad,qbd->jab', weighted, factors, preferred_element_type=jnp...]
    all_gather x1 -> x0, blocking collectives: 13 us -> none  [body(): full_rows = lax.all_gather(masked_block, 'virt', axis=2, tiled=True)]
    pallas_call x0 -> x5, Pallas kernels: none -> 12.9 us  [kernel(): return call(*scalars, *arrays)]
    all_to_all x0 -> x1, waiting for transfers between devices: none -> 9.89 us  [body(): got = lax.all_to_all(sent, 'z', 0, 0, tiled=True)]
  transfers between devices with their start and end apart: 3 -> 1, of which waited for: 3 -> 1; matrix products, arithmetic and copies ran while one was open for 6% -> 0% of each run, Pallas kernels for 0% -> 0%
where the time goes in v2:
time: 94.7 us; the launch traced here: 93.6 us
  blocking collectives  62 us (65%)
  Pallas kernels  12.9 us (14%)
  waiting for transfers between devices  9.89 us (10%)
  starting transfers between devices  5.05 us (5%)
  local copies, waits for them, and re-layouts  2.39 us (3%)
  between operations  1.35 us (1%)
    all_to_all x2, blocking collectives, body(): got = lax.all_to_all(sent, ('virt', 'y'), 0, 0, tiled=True)  40.5 us
    all_to_all x1, blocking collectives, body(): got = lax.all_to_all(sent, 'z', 0, 0, tiled=True)  21.5 us
    pallas_call x5, Pallas kernels, kernel(): return call(*scalars, *arrays)  12.9 us
    all_to_all x1, waiting for transfers between devices, body(): got = lax.all_to_all(sent, 'z', 0, 0, tiled=True)  9.89 us
    all_to_all x1, starting transfers between devices, body(): got = lax.all_to_all(sent, 'z', 0, 0, tiled=True)  5.05 us
    unnamed x16, local copies, waits for them, and re-layouts  2.39 us
  transfers between devices with their start and end apart: 1, of which 1 were waited for; matrix products, arithmetic and copies ran while one was open for 0% of the time, Pallas kernels for 0%

profile of v2, /device:TPU:4, one launch (start us, length us, event | category | flops | bytes accessed | tf_op | source)
XLA Modules:
  0.0 93.6 jit_solution(9012723270240303986)
XLA Ops:
  0.0 0.0 copy-start.1
  0.0 0.9 %copy-done.1 = bf16[512,1,256]{2,0,1:T(8,128)(2,1)S(1)} copy-done((bf16[512,1,256]{2,0,1:T(8,128)(2,1)S(1)}, bf16[512,1,256]{2,0,1:T(8,128)(2,1)}, u32[]{:S(2)}) %copy-start.1) | copy-done | bytes 262168
  1.0 0.0 copy-start.3
  1.0 0.8 copy-done.3
  1.7 0.0 copy-start.4
  1.7 0.7 copy-done.4
  2.4 0.6 out_kernel.1
  3.0 21.5 %all_to_all.20.got_ref = bf16[8,80,256]{2,1,0:T(8,128)(2,1)S(1)} all-to-all(bf16[8,80,256]{2,1,0:T(8,128)(2,1)S(1)} %out_kernel.1), channel_id=1, replica_groups=mesh['pair'=2,'virt'=4,'y'=4,'z'=8] {'z'}, dimensions={0} | all-to-all | bytes 655360 | tf_op jit(solution)/shard_map/all_to_all | solution.py:144
  24.5 0.1 spread_kernel.1
  24.6 0.0 copy-start
  24.6 0.0 copy-start.6
  24.6 21.8 %all_to_all.21.rows_ref = bf16[16,144,256]{2,1,0:T(8,128)(2,1)S(1)} all-to-all(bf16[16,144,256]{2,1,0:T(8,128)(2,1)S(1)} %spread_kernel.1), channel_id=1, replica_groups=mesh['pair'=2,'virt'=4,'y'=4,'z'=8] {'virt','y'}, dimensions={0} | all-to-all | bytes 2359296 | tf_op jit(solution)/shard_map/all_to_all | solution.py:146
  46.4 0.0 copy-done
  46.4 0.0 copy-done.6
  46.4 9.9 %ladder_kernel.1 = bf16[16,144,256]{2,1,0:T(8,128)(2,1)S(1)} custom-call(s32[2,2]{1,0:T(2,128)S(1)} %copy-done.6, bf16[16,144,256]{2,1,0:T(8,128)(2,1)S(1)} %all_to_all.21.rows_ref, bf16[16,256,256]{2,1,0:T(8,128)(2,1)S(1)} %copy-done), custom_call_target="tpu_custom_call" | custom-call | tf_op jit(solution)/shard_map/ladder_kernel/pallas_call | solution.py:129
  56.3 18.7 %all_to_all.22.got_ref = bf16[16,144,256]{2,1,0:T(8,128)(2,1)S(1)} all-to-all(bf16[16,144,256]{2,1,0:T(8,128)(2,1)S(1)} %ladder_kernel.1), channel_id=1, replica_groups=mesh['pair'=2,'virt'=4,'y'=4,'z'=8] {'virt','y'}, dimensions={0} | all-to-all | bytes 2359296 | tf_op jit(solution)/shard_map/all_to_all | solution.py:149
  75.1 0.0 copy-start.2
  75.1 0.0 copy-start.5
  75.1 0.0 copy-start.7
  75.1 0.9 sum_kernel.1
  75.9 5.0 %all-to-all-start.3 = ((bf16[8,80,256]{2,1,0:T(8,128)(2,1)}), bf16[8,80,256]{2,1,0:T(8,128)(2,1)S(1)}, u32[]{:S(2)}, u32[]{:S(2)}) async-start(bf16[8,80,256]{2,1,0:T(8,128)(2,1)} %sum_kernel.1), calls=%async_computation.3 | async-start | bytes 655360 | tf_op jit(solution)/shard_map/all_to_all | solution.py:151
  82.3 9.9 %all-to-all-done.3.got_ref = bf16[8,80,256]{2,1,0:T(8,128)(2,1)S(1)} async-done(((bf16[8,80,256]{2,1,0:T(8,128)(2,1)}), bf16[8,80,256]{2,1,0:T(8,128)(2,1)S(1)}, u32[]{:S(2)}, u32[]{:S(2)}) %all-to-all-start.3) | async-done | bytes 327712 | tf_op jit(solution)/shard_map/all_to_all | solution.py:151
  92.2 0.0 copy-done.2
  92.2 0.0 copy-done.5
  92.2 0.0 copy-done.7
  92.2 1.4 %update_kernel.1 = bf16[1,1,64,256]{3,2,1,0:T(8,128)(2,1)} custom-call(s32[1,1,2]{2,1,0:T(1,128)S(1)} %copy-done.5, f32[1]{0:T(128)S(6)} %copy.9.occ_i_ref, f32[1]{0:T(128)S(6)} %copy.10.occ_j_ref, f32[1,256]{1,0:T(1,128)S(1)} %bitcast.4, bf16[8,80,256]{2,1,0:T(8,128)(2,1)S(1)} %all-to-all-done.3.got_ref, bf16[512,256]{1,0:T(8,128)(2,1)S(1)} %bitcast.3), custom_call_target="tpu_custom_call" | custom-call | tf_op jit(solution)/shard_map/update_kernel/pallas_call | solution.py:129
Async XLA Ops:
  0.0 0.9 %copy-start.1 = (bf16[512,1,256]{2,0,1:T(8,128)(2,1)S(1)}, bf16[512,1,256]{2,0,1:T(8,128)(2,1)}, u32[]{:S(2)}) copy-start(bf16[512,1,256]{2,0,1:T(8,128)(2,1)} %param.10) | copy-start | bytes 786436
  1.0 0.8 copy-start.3
  1.7 0.7 copy-start.4
  24.6 21.8 %copy-start = (bf16[16,256,256]{2,1,0:T(8,128)(2,1)S(1)}, bf16[16,256,256]{2,1,0:T(8,128)(2,1)}, u32[]{:S(2)}) copy-start(bf16[16,256,256]{2,1,0:T(8,128)(2,1)} %factors_ref.1) | copy-start | bytes 6291460
  24.6 21.8 %copy-start.6 = (s32[2,2]{1,0:T(2,128)S(1)}, s32[2,2]{1,0:T(2,128)}, u32[]{:S(2)}) copy-start(s32[2,2]{1,0:T(2,128)} %mask_ref.1) | copy-start | bytes 52
  75.1 17.1 %copy-start.2 = (bf16[512,1,256]{2,0,1:T(8,128)(2,1)S(1)}, bf16[512,1,256]{2,0,1:T(8,128)(2,1)}, u32[]{:S(2)}) copy-start(bf16[512,1,256]{2,0,1:T(8,128)(2,1)} %param.10) | copy-start | bytes 786436
  75.1 17.1 %copy-start.5 = (s32[1,1,2]{2,1,0:T(1,128)S(1)}, s32[1,1,2]{2,1,0:T(1,128)}, u32[]{:S(2)}) copy-start(s32[1,1,2]{2,1,0:T(1,128)} %domain_ref.3) | copy-start | bytes 28
  75.1 17.1 %copy-start.7 = (f32[256]{0:T(256)S(1)}, f32[256]{0:T(256)}, u32[]{:S(2)}) copy-start(f32[256]{0:T(256)} %param.13) | copy-start | bytes 3076
  75.9 16.2 %all-to-all-start.3 = ((bf16[8,80,256]{2,1,0:T(8,128)(2,1)}), bf16[8,80,256]{2,1,0:T(8,128)(2,1)S(1)}, u32[]{:S(2)}, u32[]{:S(2)}) async-start(bf16[8,80,256]{2,1,0:T(8,128)(2,1)} %sum_kernel.1), calls=%async_computation.3 | async-start | bytes 655360 | tf_op jit(solution)/shard_map/all_to_all | solution.py:151

commit v3 on v2

--- a/solution.py
+++ b/solution.py
@@ -19,19 +19,30 @@
 AUX = 16
 
 
-def out_kernel(domain_ref, amp_ref, ov_ref, out_ref):
+def out_kernel(domain_hbm, amp_hbm, ov_hbm, out_ref, domain, amp, sems):
     x = lax.axis_index("virt")
     z = lax.axis_index("z")
-    row_tile = domain_ref[0, 0, x // 2]
+    owner = (x + Y - z % 2) % Y
+    copies = [
+        pltpu.make_async_copy(domain_hbm.at[0], domain, sems.at[0]),
+        pltpu.make_async_copy(amp_hbm.at[0, 0], amp, sems.at[1]),
+    ]
+    for to in range(Z):
+        start = pl.multiple_of((owner * Z + to) * AUX, AUX)
+        copies.append(pltpu.make_async_copy(ov_hbm.at[pl.ds(start, AUX)], out_ref.at[to, pl.ds(ROWS, AUX)], sems.at[2 + to]))
+    for copy in copies:
+        copy.start()
+    copies[0].wait()
+    copies[1].wait()
+    row_tile = domain[0, x // 2]
     for half in range(2):
         cols = slice(half * TILE_SIZE, (half + 1) * TILE_SIZE)
-        keep = (row_tile * domain_ref[0, 0, half]).astype(F32)
-        rows = (amp_ref[0, 0, :, cols].astype(F32) * keep).astype(BF16)
+        keep = (row_tile * domain[0, half]).astype(F32)
+        rows = (amp[:, cols].astype(F32) * keep).astype(BF16)
         for to in range(Z):
             out_ref[to, :ROWS, cols] = rows
-    owner = (x + Y - z % 2) % Y
-    start = pl.multiple_of(owner * (Z * AUX), Z * AUX)
-    out_ref[:, ROWS:] = ov_ref[pl.ds(start, Z * AUX), :].reshape(Z, AUX, COLS)
+    for copy in copies[2:]:
+        copy.wait()
 
 
 def spread_kernel(got_ref, out_ref):
@@ -140,7 +151,19 @@
     pair_domain,
 ):
     ov = ov_factors[:, 0, :]
-    sent = kernel(out_kernel, (Z, ROWS + AUX, COLS), (pair_domain,), (amplitudes, ov))
+    hbm = pl.BlockSpec(memory_space=pltpu.HBM)
+    sent = pl.pallas_call(
+        out_kernel,
+        name="out_kernel",
+        in_specs=[hbm, hbm, hbm],
+        out_specs=pl.BlockSpec(memory_space=pltpu.VMEM),
+        out_shape=jax.ShapeDtypeStruct((Z, ROWS + AUX, COLS), BF16),
+        scratch_shapes=[
+            pltpu.SMEM((1, 2), jnp.int32),
+            pltpu.VMEM((ROWS, COLS), BF16),
+            pltpu.SemaphoreType.DMA((2 + Z,)),
+        ],
+    )(pair_domain, amplitudes, ov)
     got = lax.all_to_all(sent, "z", 0, 0, tiled=True)
     sent = kernel(spread_kernel, (VIRT * Y, 2 * ROWS + AUX, COLS), (), (got,))
     got = lax.all_to_all(sent, ("virt", "y"), 0, 0, tiled=True)

time: 94.7 us -> 93.5 us (0.987)
  local copies, waits for them, and re-layouts: 2.39 us -> 0.02 us
    unnamed x16 -> x10, local copies, waits for them, and re-layouts: 2.39 us -> 0.02 us
    pallas_call x0 -> x1, Pallas kernels: none -> 1.65 us  [body(): pl.pallas_call(out_kernel, name='out_kernel', in_specs=[hbm, hbm, hbm], o...]
    pallas_call x5 -> x4, Pallas kernels: 12.9 us -> 12.2 us  [kernel(): return call(*scalars, *arrays)]
where the time goes in v3:
time: 93.5 us; the launch traced here: 92.3 us
  blocking collectives  62.2 us (67%)
  Pallas kernels  13.8 us (15%)
  waiting for transfers between devices  9.89 us (11%)
  starting transfers between devices  5.05 us (5%)
  between operations  1.34 us (1%)
    all_to_all x2, blocking collectives, body(): got = lax.all_to_all(sent, ('virt', 'y'), 0, 0, tiled=True)  40.5 us
    all_to_all x1, blocking collectives, body(): got = lax.all_to_all(sent, 'z', 0, 0, tiled=True)  21.8 us
    pallas_call x4, Pallas kernels, kernel(): return call(*scalars, *arrays)  12.2 us
    all_to_all x1, waiting for transfers between devices, body(): got = lax.all_to_all(sent, 'z', 0, 0, tiled=True)  9.89 us
    all_to_all x1, starting transfers between devices, body(): got = lax.all_to_all(sent, 'z', 0, 0, tiled=True)  5.05 us
  transfers between devices with their start and end apart: 1, of which 1 were waited for; matrix products, arithmetic and copies ran while one was open for 0% of the time, Pallas kernels for 0%

profile of v3, /device:TPU:4, one launch (start us, length us, event | category | flops | bytes accessed | tf_op | source)
XLA Modules:
  0.0 92.3 jit_solution(10391837561665122746)
XLA Ops:
  0.0 1.7 %out_kernel.1 = bf16[8,80,256]{2,1,0:T(8,128)(2,1)} custom-call(s32[1,1,2]{2,1,0:T(1,128)} %domain_ref.1, bf16[1,1,64,256]{3,2,1,0:T(8,128)(2,1)} %amp_hbm.1, bf16[512,256]{1,0:T(8,128)(2,1)} %bitcast.2), custom_call_target="tpu_custom_call" | custom-call | tf_op jit(solution)/shard_map/out_kernel/pallas_call | solution.py:155
  1.7 21.8 %all_to_all.20.got_ref = bf16[8,80,256]{2,1,0:T(8,128)(2,1)S(1)} all-to-all(bf16[8,80,256]{2,1,0:T(8,128)(2,1)} %out_kernel.1), channel_id=1, replica_groups=mesh['pair'=2,'virt'=4,'y'=4,'z'=8] {'z'}, dimensions={0} | all-to-all | bytes 655360 | tf_op jit(solution)/shard_map/all_to_all | solution.py:167
  23.4 0.1 spread_kernel.1
  23.5 0.0 copy-start
  23.5 0.0 copy-start.3
  23.5 21.8 %all_to_all.21.rows_ref = bf16[16,144,256]{2,1,0:T(8,128)(2,1)S(1)} all-to-all(bf16[16,144,256]{2,1,0:T(8,128)(2,1)S(1)} %spread_kernel.1), channel_id=1, replica_groups=mesh['pair'=2,'virt'=4,'y'=4,'z'=8] {'virt','y'}, dimensions={0} | all-to-all | bytes 2359296 | tf_op jit(solution)/shard_map/all_to_all | solution.py:169
  45.3 0.0 copy-done
  45.3 0.0 copy-done.3
  45.3 9.8 %ladder_kernel.1 = bf16[16,144,256]{2,1,0:T(8,128)(2,1)S(1)} custom-call(s32[2,2]{1,0:T(2,128)S(1)} %copy-done.3, bf16[16,144,256]{2,1,0:T(8,128)(2,1)S(1)} %all_to_all.21.rows_ref, bf16[16,256,256]{2,1,0:T(8,128)(2,1)S(1)} %copy-done), custom_call_target="tpu_custom_call" | custom-call | tf_op jit(solution)/shard_map/ladder_kernel/pallas_call | solution.py:140
  55.1 18.7 %all_to_all.22.got_ref = bf16[16,144,256]{2,1,0:T(8,128)(2,1)S(1)} all-to-all(bf16[16,144,256]{2,1,0:T(8,128)(2,1)S(1)} %ladder_kernel.1), channel_id=1, replica_groups=mesh['pair'=2,'virt'=4,'y'=4,'z'=8] {'virt','y'}, dimensions={0} | all-to-all | bytes 2359296 | tf_op jit(solution)/shard_map/all_to_all | solution.py:172
  73.8 0.0 copy-start.1
  73.8 0.0 copy-start.2
  73.8 0.0 copy-start.4
  73.8 0.9 sum_kernel.1
  74.7 5.0 %all-to-all-start.3 = ((bf16[8,80,256]{2,1,0:T(8,128)(2,1)}), bf16[8,80,256]{2,1,0:T(8,128)(2,1)S(1)}, u32[]{:S(2)}, u32[]{:S(2)}) async-start(bf16[8,80,256]{2,1,0:T(8,128)(2,1)} %sum_kernel.1), calls=%async_computation.3 | async-start | bytes 655360 | tf_op jit(solution)/shard_map/all_to_all | solution.py:174
  81.0 9.9 %all-to-all-done.3.got_ref = bf16[8,80,256]{2,1,0:T(8,128)(2,1)S(1)} async-done(((bf16[8,80,256]{2,1,0:T(8,128)(2,1)}), bf16[8,80,256]{2,1,0:T(8,128)(2,1)S(1)}, u32[]{:S(2)}, u32[]{:S(2)}) %all-to-all-start.3) | async-done | bytes 327712 | tf_op jit(solution)/shard_map/all_to_all | solution.py:174
  90.9 0.0 copy-done.1
  90.9 0.0 copy-done.2
  90.9 0.0 copy-done.4
  90.9 1.4 %update_kernel.1 = bf16[1,1,64,256]{3,2,1,0:T(8,128)(2,1)} custom-call(s32[1,1,2]{2,1,0:T(1,128)S(1)} %copy-done.2, f32[1]{0:T(128)S(6)} %copy.9.occ_i_ref, f32[1]{0:T(128)S(6)} %copy.10.occ_j_ref, f32[1,256]{1,0:T(1,128)S(1)} %bitcast.4, bf16[8,80,256]{2,1,0:T(8,128)(2,1)S(1)} %all-to-all-done.3.got_ref, bf16[512,256]{1,0:T(8,128)(2,1)S(1)} %bitcast.3), custom_call_target="tpu_custom_call" | custom-call | tf_op jit(solution)/shard_map/update_kernel/pallas_call | solution.py:140
Async XLA Ops:
  23.5 21.8 %copy-start = (bf16[16,256,256]{2,1,0:T(8,128)(2,1)S(1)}, bf16[16,256,256]{2,1,0:T(8,128)(2,1)}, u32[]{:S(2)}) copy-start(bf16[16,256,256]{2,1,0:T(8,128)(2,1)} %factors_ref.1) | copy-start | bytes 6291460
  23.5 21.8 %copy-start.3 = (s32[2,2]{1,0:T(2,128)S(1)}, s32[2,2]{1,0:T(2,128)}, u32[]{:S(2)}) copy-start(s32[2,2]{1,0:T(2,128)} %mask_ref.1) | copy-start | bytes 52
  73.8 17.1 %copy-start.1 = (bf16[512,1,256]{2,0,1:T(8,128)(2,1)S(1)}, bf16[512,1,256]{2,0,1:T(8,128)(2,1)}, u32[]{:S(2)}) copy-start(bf16[512,1,256]{2,0,1:T(8,128)(2,1)} %param.10) | copy-start | bytes 786436
  73.8 17.1 %copy-start.2 = (s32[1,1,2]{2,1,0:T(1,128)S(1)}, s32[1,1,2]{2,1,0:T(1,128)}, u32[]{:S(2)}) copy-start(s32[1,1,2]{2,1,0:T(1,128)} %domain_ref.1) | copy-start | bytes 28
  73.8 17.1 %copy-start.4 = (f32[256]{0:T(256)S(1)}, f32[256]{0:T(256)}, u32[]{:S(2)}) copy-start(f32[256]{0:T(256)} %param.13) | copy-start | bytes 3076
  74.7 16.2 %all-to-all-start.3 = ((bf16[8,80,256]{2,1,0:T(8,128)(2,1)}), bf16[8,80,256]{2,1,0:T(8,128)(2,1)S(1)}, u32[]{:S(2)}, u32[]{:S(2)}) async-start(bf16[8,80,256]{2,1,0:T(8,128)(2,1)} %sum_kernel.1), calls=%async_computation.3 | async-start | bytes 655360 | tf_op jit(solution)/shard_map/all_to_all | solution.py:174

commit v4 on v3

--- a/solution.py
+++ b/solution.py
@@ -17,19 +17,20 @@
 ROWS = 64
 COLS = 256
 AUX = 16
+PART = 8
 
 
 def out_kernel(domain_hbm, amp_hbm, ov_hbm, out_ref, domain, amp, sems):
     x = lax.axis_index("virt")
-    z = lax.axis_index("z")
-    owner = (x + Y - z % 2) % Y
     copies = [
         pltpu.make_async_copy(domain_hbm.at[0], domain, sems.at[0]),
         pltpu.make_async_copy(amp_hbm.at[0, 0], amp, sems.at[1]),
     ]
     for to in range(Z):
-        start = pl.multiple_of((owner * Z + to) * AUX, AUX)
-        copies.append(pltpu.make_async_copy(ov_hbm.at[pl.ds(start, AUX)], out_ref.at[to, pl.ds(ROWS, AUX)], sems.at[2 + to]))
+        for high in range(2):
+            start = pl.multiple_of(((2 * high + x // 2) * Z + to) * AUX + (x % 2) * PART, PART)
+            target = out_ref.at[to, pl.ds(ROWS + high * PART, PART)]
+            copies.append(pltpu.make_async_copy(ov_hbm.at[pl.ds(start, PART)], target, sems.at[2 + 2 * to + high]))
     for copy in copies:
         copy.start()
     copies[0].wait()
@@ -46,59 +47,72 @@
 
 
 def spread_kernel(got_ref, out_ref):
-    x = lax.axis_index("virt")
     for to_x in range(VIRT):
-        rows = got_ref[2 * to_x : 2 * to_x + 2, :ROWS].reshape(2 * ROWS, COLS)
         for to_y in range(Y):
-            out_ref[to_x * Y + to_y, : 2 * ROWS] = rows
-            low = (x + Y - to_y) % 2
-            out_ref[to_x * Y + to_y, 2 * ROWS :] = got_ref[2 * to_x + low, ROWS:]
-
-
-def ladder_kernel(mask_ref, rows_ref, factors_ref, out_ref, masked, weighted):
-    y = lax.axis_index("y")
+            high, low = divmod(to_y, 2)
+            out_ref[to_x * Y + to_y, :ROWS] = got_ref[2 * to_x + low, :ROWS]
+            start = ROWS + high * PART
+            out_ref[to_x * Y + to_y, ROWS:] = got_ref[2 * to_x + low, start : start + PART]
+
+
+def ladder_kernel(mask_ref, rows_ref, own_ref, near_ref, far_ref, out_ref, masked, weighted):
+    sources = [(own_ref, aux) for aux in range(AUX)]
+    sources += [(ref, aux) for ref in (near_ref, far_ref) for aux in range(PART)]
     for p in range(2):
         for q in range(2):
             keep = jnp.full((1, TILE_SIZE), mask_ref[p, q], jnp.int32).astype(F32).astype(BF16)
-            for aux in range(AUX):
-                block = factors_ref[aux, p * 128 : (p + 1) * 128, q * 128 : (q + 1) * 128] * keep
-                masked[p * 128 : (p + 1) * 128, aux * 256 + q * 128 : aux * 256 + (q + 1) * 128] = block
-
-    zeta = jnp.zeros((AUX, COLS), F32)
+            for slot, (ref, aux) in enumerate(sources):
+                block = ref[aux, p * 128 : (p + 1) * 128, q * 128 : (q + 1) * 128] * keep
+                masked[p * 128 : (p + 1) * 128, slot * 256 + q * 128 : slot * 256 + (q + 1) * 128] = block
+
+    zeta = jnp.zeros((2 * AUX, COLS), F32)
     for at_y in range(Y):
+        amp = jnp.concatenate([rows_ref[at_x * Y + at_y, :ROWS] for at_x in range(VIRT)], axis=0)
+        fac = jnp.concatenate([rows_ref[at_x * Y + at_y, ROWS:] for at_x in range(VIRT)], axis=0)
+        direct = lax.dot_general(fac, amp, NT, preferred_element_type=F32)
+        swapped = jnp.dot(fac, amp, preferred_element_type=F32)
+        zeta = zeta + (2.0 * direct - swapped)
+        for slot in range(2 * AUX):
+            cols = slice(slot * 256, (slot + 1) * 256)
+            weighted[:, cols] = jnp.dot(masked[:, cols], amp, preferred_element_type=F32).astype(BF16)
+        total = lax.dot_general(weighted[...], masked[...], NT, preferred_element_type=F32).astype(BF16)
+        for at_x in range(VIRT):
+            out_ref[at_x * Y + at_y, :ROWS] = total[at_x * ROWS : (at_x + 1) * ROWS]
+    group = lax.broadcasted_iota(jnp.int32, (PART, COLS), 1) // ROWS
+    for at_x in range(VIRT):
+        piece = jnp.zeros((PART, COLS), F32)
+        for to in range(4):
+            turned = zeta[to * PART : (to + 1) * PART]
+            if to != at_x:
+                turned = pltpu.roll(turned, ((to - at_x) % 4) * ROWS, 1)
+            piece = jnp.where(group == to, turned, piece)
+        piece = piece.astype(BF16)
+        for at_y in range(Y):
+            out_ref[at_x * Y + at_y, ROWS:] = piece
+
+
+def sum_kernel(got_ref, out_ref):
+    sums = [jnp.zeros((PART, COLS), F32), jnp.zeros((PART, COLS), F32)]
+    for at_x in range(VIRT):
         for low in range(2):
-            rows = slice(low * ROWS, (low + 1) * ROWS)
-            amp = jnp.concatenate([rows_ref[at_x * Y + at_y, rows] for at_x in range(VIRT)], axis=0)
-            fac = rows_ref[((y + low) % Y) * Y + at_y, 2 * ROWS :]
-            direct = lax.dot_general(fac, amp, NT, preferred_element_type=F32)
-            swapped = jnp.dot(fac, amp, preferred_element_type=F32)
-            zeta = zeta + (2.0 * direct - swapped)
-            for aux in range(AUX):
-                cols = slice(aux * 256, (aux + 1) * 256)
-                weighted[:, cols] = jnp.dot(masked[:, cols], amp, preferred_element_type=F32).astype(BF16)
-            total = lax.dot_general(weighted[...], masked[...], NT, preferred_element_type=F32).astype(BF16)
-            for at_x in range(VIRT):
-                out_ref[at_x * Y + at_y, rows] = total[at_x * ROWS : (at_x + 1) * ROWS]
-    lane = lax.broadcasted_iota(jnp.int32, (AUX, COLS), 1)
-    for at_x in range(VIRT):
-        turned = pltpu.roll(zeta, ((y + VIRT - at_x) % VIRT) * ROWS, 1)
-        piece = jnp.where(lane // ROWS == y, turned, 0.0).astype(BF16)
-        for at_y in range(Y):
-            out_ref[at_x * Y + at_y, 2 * ROWS :] = piece
-
-
-def sum_kernel(got_ref, out_ref):
-    for high in range(VIRT):
-        for low in range(2):
-            rows = slice(low * ROWS, (low + 1) * ROWS)
-            total = got_ref[high * Y, rows].astype(F32)
-            for at_y in range(1, Y):
-                total = total + got_ref[high * Y + at_y, rows].astype(F32)
-            out_ref[2 * high + low, :ROWS] = total.astype(BF16)
-    zeta = jnp.zeros((AUX, COLS), F32)
-    for source in range(VIRT * Y):
-        zeta = zeta + got_ref[source, 2 * ROWS :].astype(F32)
-    zeta = zeta.astype(BF16)
+            first = got_ref[at_x * Y + low]
+            second = got_ref[at_x * Y + 2 + low]
+            out_ref[2 * at_x + low, :ROWS] = (first[:ROWS].astype(F32) + second[:ROWS].astype(F32)).astype(BF16)
+            sums[0] = sums[0] + first[ROWS:].astype(F32)
+            sums[1] = sums[1] + second[ROWS:].astype(F32)
+    group = lax.broadcasted_iota(jnp.int32, (PART, COLS), 1) // ROWS
+    halves = []
+    for half in range(2):
+        piece = jnp.zeros((PART, COLS), F32)
+        for high in range(2):
+            for low in range(2):
+                source, to = 2 * low + half, 2 * high + low
+                turned = sums[high]
+                if source != to:
+                    turned = pltpu.roll(turned, ((to - source) % 4) * ROWS, 1)
+                piece = jnp.where(group == to, turned, piece)
+        halves.append(piece)
+    zeta = jnp.concatenate(halves, axis=0).astype(BF16)
     for to in range(Z):
         out_ref[to, ROWS:] = zeta
 
@@ -151,6 +165,7 @@
     pair_domain,
 ):
     ov = ov_factors[:, 0, :]
+    mine = lax.dynamic_slice_in_dim(vv_factors, lax.axis_index("pair") * PART, PART, 0)
     hbm = pl.BlockSpec(memory_space=pltpu.HBM)
     sent = pl.pallas_call(
         out_kernel,
@@ -161,14 +176,23 @@
         scratch_shapes=[
             pltpu.SMEM((1, 2), jnp.int32),
             pltpu.VMEM((ROWS, COLS), BF16),
-            pltpu.SemaphoreType.DMA((2 + Z,)),
+            pltpu.SemaphoreType.DMA((2 + 2 * Z,)),
         ],
     )(pair_domain, amplitudes, ov)
     got = lax.all_to_all(sent, "z", 0, 0, tiled=True)
-    sent = kernel(spread_kernel, (VIRT * Y, 2 * ROWS + AUX, COLS), (), (got,))
+    sent = kernel(spread_kernel, (VIRT * Y, ROWS + PART, COLS), (), (got,))
+    near = lax.ppermute(mine, "y", [(y, y ^ 1) for y in range(Y)])
+    far = lax.ppermute(near, "pair", [(0, 1), (1, 0)])
     got = lax.all_to_all(sent, ("virt", "y"), 0, 0, tiled=True)
-    wide = pltpu.VMEM((COLS, AUX * COLS), BF16)
-    sent = kernel(ladder_kernel, (VIRT * Y, 2 * ROWS + AUX, COLS), (vv_mask,), (got, vv_factors), (wide, wide), 40)
+    wide = pltpu.VMEM((COLS, 2 * AUX * COLS), BF16)
+    sent = kernel(
+        ladder_kernel,
+        (VIRT * Y, ROWS + PART, COLS),
+        (vv_mask,),
+        (got, vv_factors, near, far),
+        (wide, wide),
+        40,
+    )
     got = lax.all_to_all(sent, ("virt", "y"), 0, 0, tiled=True)
     sent = kernel(sum_kernel, (Z, ROWS + AUX, COLS), (), (got,))
     got = lax.all_to_all(sent, "z", 0, 0, tiled=True)

time: 93.5 us -> 94.1 us (level)
  blocking collectives: 62.2 us -> 33.1 us
  waiting for transfers between devices: 9.89 us -> 23.5 us
  starting transfers between devices: 5.05 us -> 18.5 us
  local copies, waits for them, and re-layouts: 0.02 us -> 2.29 us
    all_to_all x1 -> x0, blocking collectives: 21.8 us -> none  [body(): got = lax.all_to_all(sent, 'z', 0, 0, tiled=True)]
    ppermute x0 -> x2, waiting for transfers between devices: none -> 13.3 us  [the longest x1 13.3 us: body(): near = lax.ppermute(mine, 'y', [(y, y ^ 1) for y in range(Y)])]
    all_to_all x1 -> x2, starting transfers between devices: 5.05 us -> 16.9 us  [body(): got = lax.all_to_all(sent, 'z', 0, 0, tiled=True)]
    all_to_all x2, blocking collectives: 40.5 us -> 33.1 us  [body(): got = lax.all_to_all(sent, ('virt', 'y'), 0, 0, tiled=True)]
    dynamic_slice x0 -> x1, local copies, waits for them, and re-layouts: none -> 2.27 us  [body(): lax.dynamic_slice_in_dim(vv_factors, lax.axis_index('pair') * PART, PART, 0)]
    ppermute x0 -> x2, starting transfers between devices: none -> 1.58 us  [the longest x1 1.58 us: body(): near = lax.ppermute(mine, 'y', [(y, y ^ 1) for y in range(Y)])]
    all_to_all x1 -> x2, waiting for transfers between devices: 9.89 us -> 10.2 us  [body(): got = lax.all_to_all(sent, 'z', 0, 0, tiled=True)]
  transfers between devices with their start and end apart: 1 -> 4, of which waited for: 1 -> 2; matrix products, arithmetic and copies ran while one was open for 0% -> 0% of each run, Pallas kernels for 0% -> 2%
where the time goes in v4:
time: 94.1 us; the launch traced here: 93.1 us
  blocking collectives  33.1 us (35%)
  waiting for transfers between devices  23.5 us (25%)
  starting transfers between devices  18.5 us (20%)
  Pallas kernels  14.3 us (15%)
  local copies, waits for them, and re-layouts  2.29 us (2%)
  between operations  1.36 us (1%)
    all_to_all x2, blocking collectives, body(): got = lax.all_to_all(sent, ('virt', 'y'), 0, 0, tiled=True)  33.1 us
    all_to_all x2, starting transfers between devices, body(): got = lax.all_to_all(sent, 'z', 0, 0, tiled=True)  16.9 us
    ppermute x1, waiting for transfers between devices, body(): near = lax.ppermute(mine, 'y', [(y, y ^ 1) for y in range(Y)])  13.3 us
    pallas_call x4, Pallas kernels, kernel(): return call(*scalars, *arrays)  12.6 us
    all_to_all x2, waiting for transfers between devices, body(): got = lax.all_to_all(sent, 'z', 0, 0, tiled=True)  10.2 us
    dynamic_slice x1, local copies, waits for them, and re-layouts, body(): lax.dynamic_slice_in_dim(vv_factors, lax.axis_index('pair') * PART, PART, 0)  2.27 us
  transfers between devices with their start and end apart: 4, of which 2 were waited for; matrix products, arithmetic and copies ran while one was open for 0% of the time, Pallas kernels for 2%

profile of v4, /device:TPU:4, one launch (start us, length us, event | category | flops | bytes accessed | tf_op | source)
XLA Modules:
  0.0 93.1 jit_solution(17622695473088943461)
XLA Ops:
  0.0 2.3 %constant_dynamic-slice_fusion = bf16[8,256,256]{2,1,0:T(8,128)(2,1)} fusion(bf16[16,256,256]{2,1,0:T(8,128)(2,1)} %own_ref.1, s32[]{:T(128)S(6)} %select_n.3), kind=kLoop, calls=%fused_computation | loop fusion | bytes 2097156 | tf_op jit(solution)/shard_map/dynamic_slice | solution.py:168
  2.3 0.0 copy-start
  2.3 0.0 copy-start.3
  2.3 1.6 %collective-permute-start = (bf16[8,256,256]{2,1,0:T(8,128)(2,1)}, bf16[8,256,256]{2,1,0:T(8,128)(2,1)S(1)}, u32[]{:S(2)}, u32[]{:S(2)}) collective-permute-start(bf16[8,256,256]{2,1,0:T(8,128)(2,1)} %constant_dynamic-slice_fusion), channel_id=1, source_target_pairs={{0,8},{8,0},{16,24},{24,16},{1,9},{9,1},{17,25},{25,17},{2,10},{10... | collective-permute-start | bytes 3145736 | tf_op jit(solution)/shard_map/ppermute | solution.py:184
  3.8 1.8 %out_kernel.1 = bf16[8,80,256]{2,1,0:T(8,128)(2,1)} custom-call(s32[1,1,2]{2,1,0:T(1,128)} %domain_ref.1, bf16[1,1,64,256]{3,2,1,0:T(8,128)(2,1)} %amp_hbm.1, bf16[512,256]{1,0:T(8,128)(2,1)} %bitcast.2), custom_call_target="tpu_custom_call" | custom-call | tf_op jit(solution)/shard_map/out_kernel/pallas_call | solution.py:170
  5.6 8.5 %all-to-all-start = ((bf16[8,80,256]{2,1,0:T(8,128)(2,1)}), bf16[8,80,256]{2,1,0:T(8,128)(2,1)S(1)}, u32[]{:S(2)}, u32[]{:S(2)}) async-start(bf16[8,80,256]{2,1,0:T(8,128)(2,1)} %out_kernel.1), calls=%async_computation | async-start | bytes 655360 | tf_op jit(solution)/shard_map/all_to_all | solution.py:182
  14.1 13.3 %collective-permute-done.near_ref = bf16[8,256,256]{2,1,0:T(8,128)(2,1)S(1)} collective-permute-done((bf16[8,256,256]{2,1,0:T(8,128)(2,1)}, bf16[8,256,256]{2,1,0:T(8,128)(2,1)S(1)}, u32[]{:S(2)}, u32[]{:S(2)}) %collective-permute-start) | collective-permute-done | bytes 1048608 | tf_op jit(solution)/shard_map/ppermute | solution.py:184
  27.4 0.0 collective-permute-start.1
  27.4 0.0 all-to-all-done.got_ref
  27.4 18.0 %all_to_all.20.rows_ref = bf16[16,72,256]{2,1,0:T(8,128)(2,1)S(1)} all-to-all(bf16[16,72,256]{2,1,0:T(8,128)(2,1)S(1)} %spread_kernel.1), channel_id=1, replica_groups=mesh['pair'=2,'virt'=4,'y'=4,'z'=8] {'virt','y'}, dimensions={0} | all-to-all | bytes 1179648 | tf_op jit(solution)/shard_map/all_to_all | solution.py:186
  45.4 0.0 collective-permute-done.1.far_ref
  45.4 0.0 copy-done
  45.4 0.0 copy-done.3
  45.4 10.3 %ladder_kernel.1 = bf16[16,72,256]{2,1,0:T(8,128)(2,1)S(1)} custom-call(s32[2,2]{1,0:T(2,128)S(1)} %copy-done.3, bf16[16,72,256]{2,1,0:T(8,128)(2,1)S(1)} %all_to_all.20.rows_ref, bf16[16,256,256]{2,1,0:T(8,128)(2,1)S(1)} %copy-done, bf16[8,256,256]{2,1,0:T(8,128)(2,1)S(1)} %collective-permute-done.near_ref, bf16[8,256,256]{2,1,0:T(8,128)(2,1)} %collective-permute-done.1.far_ref), custom_call_target="tpu_custom_call" | custom-call | tf_op jit(solution)/shard_map/ladder_kernel/pallas_call | solution.py:154
  55.8 0.0 copy-start.1
  55.8 0.0 copy-start.2
  55.8 0.0 copy-start.4
  55.8 15.1 %all_to_all.21.got_ref = bf16[16,72,256]{2,1,0:T(8,128)(2,1)S(1)} all-to-all(bf16[16,72,256]{2,1,0:T(8,128)(2,1)S(1)} %ladder_kernel.1), channel_id=1, replica_groups=mesh['pair'=2,'virt'=4,'y'=4,'z'=8] {'virt','y'}, dimensions={0} | all-to-all | bytes 1179648 | tf_op jit(solution)/shard_map/all_to_all | solution.py:196
  70.9 0.8 sum_kernel.1
  71.7 8.5 %all-to-all-start.3 = ((bf16[8,80,256]{2,1,0:T(8,128)(2,1)}), bf16[8,80,256]{2,1,0:T(8,128)(2,1)S(1)}, u32[]{:S(2)}, u32[]{:S(2)}) async-start(bf16[8,80,256]{2,1,0:T(8,128)(2,1)} %sum_kernel.1), calls=%async_computation.3 | async-start | bytes 655360 | tf_op jit(solution)/shard_map/all_to_all | solution.py:198
  81.5 10.2 %all-to-all-done.3.got_ref = bf16[8,80,256]{2,1,0:T(8,128)(2,1)S(1)} async-done(((bf16[8,80,256]{2,1,0:T(8,128)(2,1)}), bf16[8,80,256]{2,1,0:T(8,128)(2,1)S(1)}, u32[]{:S(2)}, u32[]{:S(2)}) %all-to-all-start.3) | async-done | bytes 327712 | tf_op jit(solution)/shard_map/all_to_all | solution.py:198
  91.6 0.0 copy-done.1
  91.6 0.0 copy-done.2
  91.7 0.0 copy-done.4
  91.7 1.4 %update_kernel.1 = bf16[1,1,64,256]{3,2,1,0:T(8,128)(2,1)} custom-call(s32[1,1,2]{2,1,0:T(1,128)S(1)} %copy-done.2, f32[1]{0:T(128)S(6)} %copy.9.occ_i_ref, f32[1]{0:T(128)S(6)} %copy.10.occ_j_ref, f32[1,256]{1,0:T(1,128)S(1)} %bitcast.4, bf16[8,80,256]{2,1,0:T(8,128)(2,1)S(1)} %all-to-all-done.3.got_ref, bf16[512,256]{1,0:T(8,128)(2,1)S(1)} %bitcast.3), custom_call_target="tpu_custom_call" | custom-call | tf_op jit(solution)/shard_map/update_kernel/pallas_call | solution.py:154
  (1 shorter events, 0.0 us)
Async XLA Ops:
  2.3 43.2 %copy-start = (bf16[16,256,256]{2,1,0:T(8,128)(2,1)S(1)}, bf16[16,256,256]{2,1,0:T(8,128)(2,1)}, u32[]{:S(2)}) copy-start(bf16[16,256,256]{2,1,0:T(8,128)(2,1)} %own_ref.1) | copy-start | bytes 6291460
  2.3 43.2 %copy-start.3 = (s32[2,2]{1,0:T(2,128)S(1)}, s32[2,2]{1,0:T(2,128)}, u32[]{:S(2)}) copy-start(s32[2,2]{1,0:T(2,128)} %mask_ref.1) | copy-start | bytes 52
  2.3 25.1 %collective-permute-start = (bf16[8,256,256]{2,1,0:T(8,128)(2,1)}, bf16[8,256,256]{2,1,0:T(8,128)(2,1)S(1)}, u32[]{:S(2)}, u32[]{:S(2)}) collective-permute-start(bf16[8,256,256]{2,1,0:T(8,128)(2,1)} %constant_dynamic-slice_fusion), channel_id=1, source_target_pairs={{0,8},{8,0},{16,24},{24,16},{1,9},{9,1},{17,25},{25,17},{2,10},{10... | collective-permute-start | bytes 3145736 | tf_op jit(solution)/shard_map/ppermute | solution.py:184
  5.6 21.8 %all-to-all-start = ((bf16[8,80,256]{2,1,0:T(8,128)(2,1)}), bf16[8,80,256]{2,1,0:T(8,128)(2,1)S(1)}, u32[]{:S(2)}, u32[]{:S(2)}) async-start(bf16[8,80,256]{2,1,0:T(8,128)(2,1)} %out_kernel.1), calls=%async_computation | async-start | bytes 655360 | tf_op jit(solution)/shard_map/all_to_all | solution.py:182
  27.4 18.0 %collective-permute-start.1 = (bf16[8,256,256]{2,1,0:T(8,128)(2,1)S(1)}, bf16[8,256,256]{2,1,0:T(8,128)(2,1)}, u32[]{:S(2)}, u32[]{:S(2)}) collective-permute-start(bf16[8,256,256]{2,1,0:T(8,128)(2,1)S(1)} %collective-permute-done.near_ref), channel_id=1, source_target_pairs={{0,128},{128,0},{1,129},{129,1},{2,130},{130,2},{3,131},{131,3},{4... | collective-permute-start | bytes 3145736 | tf_op jit(solution)/shard_map/ppermute | solution.py:185
  55.8 35.9 %copy-start.1 = (bf16[512,1,256]{2,0,1:T(8,128)(2,1)S(1)}, bf16[512,1,256]{2,0,1:T(8,128)(2,1)}, u32[]{:S(2)}) copy-start(bf16[512,1,256]{2,0,1:T(8,128)(2,1)} %param.10) | copy-start | bytes 786436
  55.8 35.9 %copy-start.2 = (s32[1,1,2]{2,1,0:T(1,128)S(1)}, s32[1,1,2]{2,1,0:T(1,128)}, u32[]{:S(2)}) copy-start(s32[1,1,2]{2,1,0:T(1,128)} %domain_ref.1) | copy-start | bytes 28
  55.8 35.9 %copy-start.4 = (f32[256]{0:T(256)S(1)}, f32[256]{0:T(256)}, u32[]{:S(2)}) copy-start(f32[256]{0:T(256)} %param.13) | copy-start | bytes 3076
  71.7 20.0 %all-to-all-start.3 = ((bf16[8,80,256]{2,1,0:T(8,128)(2,1)}), bf16[8,80,256]{2,1,0:T(8,128)(2,1)S(1)}, u32[]{:S(2)}, u32[]{:S(2)}) async-start(bf16[8,80,256]{2,1,0:T(8,128)(2,1)} %sum_kernel.1), calls=%async_computation.3 | async-start | bytes 655360 | tf_op jit(solution)/shard_map/all_to_all | solution.py:198

commit v5 on v4

--- a/solution.py
+++ b/solution.py
@@ -18,19 +18,22 @@
 COLS = 256
 AUX = 16
 PART = 8
-
-
-def out_kernel(domain_hbm, amp_hbm, ov_hbm, out_ref, domain, amp, sems):
+SHARE = 2
+
+
+def out_kernel(domain_hbm, amp_hbm, ov_hbm, factors_hbm, out_ref, share_ref, domain, amp, sems):
     x = lax.axis_index("virt")
+    share = (2 * x + lax.axis_index("pair")) * SHARE
     copies = [
         pltpu.make_async_copy(domain_hbm.at[0], domain, sems.at[0]),
         pltpu.make_async_copy(amp_hbm.at[0, 0], amp, sems.at[1]),
+        pltpu.make_async_copy(factors_hbm.at[pl.ds(share, SHARE)], share_ref, sems.at[2]),
     ]
     for to in range(Z):
         for high in range(2):
             start = pl.multiple_of(((2 * high + x // 2) * Z + to) * AUX + (x % 2) * PART, PART)
             target = out_ref.at[to, pl.ds(ROWS + high * PART, PART)]
-            copies.append(pltpu.make_async_copy(ov_hbm.at[pl.ds(start, PART)], target, sems.at[2 + 2 * to + high]))
+            copies.append(pltpu.make_async_copy(ov_hbm.at[pl.ds(start, PART)], target, sems.at[3 + 2 * to + high]))
     for copy in copies:
         copy.start()
     copies[0].wait()
@@ -55,9 +58,8 @@
             out_ref[to_x * Y + to_y, ROWS:] = got_ref[2 * to_x + low, start : start + PART]
 
 
-def ladder_kernel(mask_ref, rows_ref, own_ref, near_ref, far_ref, out_ref, masked, weighted):
-    sources = [(own_ref, aux) for aux in range(AUX)]
-    sources += [(ref, aux) for ref in (near_ref, far_ref) for aux in range(PART)]
+def ladder_kernel(mask_ref, rows_ref, own_ref, near_ref, out_ref, masked, weighted):
+    sources = [(ref, aux) for ref in (own_ref, near_ref) for aux in range(AUX)]
     for p in range(2):
         for q in range(2):
             keep = jnp.full((1, TILE_SIZE), mask_ref[p, q], jnp.int32).astype(F32).astype(BF16)
@@ -165,31 +167,33 @@
     pair_domain,
 ):
     ov = ov_factors[:, 0, :]
-    mine = lax.dynamic_slice_in_dim(vv_factors, lax.axis_index("pair") * PART, PART, 0)
     hbm = pl.BlockSpec(memory_space=pltpu.HBM)
-    sent = pl.pallas_call(
+    sent, mine = pl.pallas_call(
         out_kernel,
         name="out_kernel",
-        in_specs=[hbm, hbm, hbm],
-        out_specs=pl.BlockSpec(memory_space=pltpu.VMEM),
-        out_shape=jax.ShapeDtypeStruct((Z, ROWS + AUX, COLS), BF16),
+        in_specs=[hbm, hbm, hbm, hbm],
+        out_specs=[pl.BlockSpec(memory_space=pltpu.VMEM)] * 2,
+        out_shape=[
+            jax.ShapeDtypeStruct((Z, ROWS + AUX, COLS), BF16),
+            jax.ShapeDtypeStruct((SHARE, COLS, COLS), BF16),
+        ],
         scratch_shapes=[
             pltpu.SMEM((1, 2), jnp.int32),
             pltpu.VMEM((ROWS, COLS), BF16),
-            pltpu.SemaphoreType.DMA((2 + 2 * Z,)),
+            pltpu.SemaphoreType.DMA((3 + 2 * Z,)),
         ],
-    )(pair_domain, amplitudes, ov)
+    )(pair_domain, amplitudes, ov, vv_factors)
     got = lax.all_to_all(sent, "z", 0, 0, tiled=True)
     sent = kernel(spread_kernel, (VIRT * Y, ROWS + PART, COLS), (), (got,))
     near = lax.ppermute(mine, "y", [(y, y ^ 1) for y in range(Y)])
-    far = lax.ppermute(near, "pair", [(0, 1), (1, 0)])
+    near = lax.all_gather(near, ("virt", "pair"), axis=0, tiled=True)
     got = lax.all_to_all(sent, ("virt", "y"), 0, 0, tiled=True)
     wide = pltpu.VMEM((COLS, 2 * AUX * COLS), BF16)
     sent = kernel(
         ladder_kernel,
         (VIRT * Y, ROWS + PART, COLS),
         (vv_mask,),
-        (got, vv_factors, near, far),
+        (got, vv_factors, near),
         (wide, wide),
         40,
     )

time: 94.1 us -> 111 us (1.18)
  blocking collectives: 33.1 us -> 50.3 us
  between operations: 1.36 us -> 14.8 us
  starting transfers between devices: 18.5 us -> 10.9 us
  waiting for transfers between devices: 23.5 us -> 17.9 us
    all_to_all x0 -> x1, blocking collectives: none -> 20.9 us  [body(): got = lax.all_to_all(sent, 'z', 0, 0, tiled=True)]
    all_to_all x2 -> x1, starting transfers between devices: 16.9 us -> 9.19 us  [body(): got = lax.all_to_all(sent, 'z', 0, 0, tiled=True)]
    ppermute x1, waiting for transfers between devices: 13.3 us -> 6.68 us  [body(): near = lax.ppermute(mine, 'y', [(y, y ^ 1) for y in range(Y)])]
    all_to_all x2, blocking collectives: 33.1 us -> 29.4 us  [body(): got = lax.all_to_all(sent, ('virt', 'y'), 0, 0, tiled=True)]
    unnamed x10 -> x14, local copies, waits for them, and re-layouts: 0.03 us -> 2.33 us
    dynamic_slice x1 -> x0, local copies, waits for them, and re-layouts: 2.27 us -> none  [body(): lax.dynamic_slice_in_dim(vv_factors, lax.axis_index('pair') * PART, PART, 0)]
    all_to_all x2 -> x1, waiting for transfers between devices: 10.2 us -> 11.2 us  [body(): got = lax.all_to_all(sent, 'z', 0, 0, tiled=True)]
  transfers between devices with their start and end apart: 4 -> 3, of which waited for: 2 -> 2; matrix products, arithmetic and copies ran while one was open for 0% -> 0% of each run, Pallas kernels for 2% -> 0%
where the time goes in v5:
time: 111 us; the launch traced here: 110 us
  blocking collectives  50.3 us (45%)
  waiting for transfers between devices  17.9 us (16%)
  between operations  14.8 us (13%)
  Pallas kernels  13.9 us (13%)
  starting transfers between devices  10.9 us (10%)
  local copies, waits for them, and re-layouts  2.33 us (2%)
    all_to_all x2, blocking collectives, body(): got = lax.all_to_all(sent, ('virt', 'y'), 0, 0, tiled=True)  29.4 us
    all_to_all x1, blocking collectives, body(): got = lax.all_to_all(sent, 'z', 0, 0, tiled=True)  20.9 us
    pallas_call x4, Pallas kernels, kernel(): return call(*scalars, *arrays)  11.9 us
    all_to_all x1, waiting for transfers between devices, body(): got = lax.all_to_all(sent, 'z', 0, 0, tiled=True)  11.2 us
    all_to_all x1, starting transfers between devices, body(): got = lax.all_to_all(sent, 'z', 0, 0, tiled=True)  9.19 us
    ppermute x1, waiting for transfers between devices, body(): near = lax.ppermute(mine, 'y', [(y, y ^ 1) for y in range(Y)])  6.68 us
    unnamed x14, local copies, waits for them, and re-layouts  2.33 us
  transfers between devices with their start and end apart: 3, of which 2 were waited for; matrix products, arithmetic and copies ran while one was open for 0% of the time, Pallas kernels for 0%

profile of v5, /device:TPU:4, one launch (start us, length us, event | category | flops | bytes accessed | tf_op | source)
XLA Modules:
  0.0 110.0 jit_solution(125535743398336309)
XLA Ops:
  6.5 0.0 all-gather.2.cloned.1.call-start
  6.5 2.0 %out_kernel.1 = (bf16[8,80,256]{2,1,0:T(8,128)(2,1)}, bf16[2,256,256]{2,1,0:T(8,128)(2,1)}) custom-call(s32[1,1,2]{2,1,0:T(1,128)} %domain_ref.1, bf16[1,1,64,256]{3,2,1,0:T(8,128)(2,1)} %amp_hbm.1, bf16[512,256]{1,0:T(8,128)(2,1)} %bitcast.2, bf16[16,256,256]{2,1,0:T(8,128)(2,1)} %own_ref.1), custom_call_target="tpu_custom_call" | custom-call | tf_op jit(solution)/shard_map/out_kernel/pallas_call | solution.py:171
  8.5 0.0 copy-start
  8.5 0.0 copy-start.4
  8.6 1.7 %collective-permute-start = (bf16[2,256,256]{2,1,0:T(8,128)(2,1)}, bf16[2,256,256]{2,1,0:T(8,128)(2,1)S(1)}, u32[]{:S(2)}, u32[]{:S(2)}) collective-permute-start(bf16[2,256,256]{2,1,0:T(8,128)(2,1)} %get-tuple-element.8), channel_id=1, source_target_pairs={{0,8},{8,0},{16,24},{24,16},{1,9},{9,1},{17,25},{25,17},{2,10},{10... | collective-permute-start | bytes 786440 | tf_op jit(solution)/shard_map/ppermute | solution.py:188
  10.2 6.7 %collective-permute-done = bf16[2,256,256]{2,1,0:T(8,128)(2,1)S(1)} collective-permute-done((bf16[2,256,256]{2,1,0:T(8,128)(2,1)}, bf16[2,256,256]{2,1,0:T(8,128)(2,1)S(1)}, u32[]{:S(2)}, u32[]{:S(2)}) %collective-permute-start) | collective-permute-done | bytes 262176 | tf_op jit(solution)/shard_map/ppermute | solution.py:188
  16.9 0.0 copy-start.6
  16.9 0.7 copy-done.6
  17.6 0.0 all-gather.2.cloned.1.call-update
  17.6 20.9 %all_to_all.20.got_ref = bf16[8,80,256]{2,1,0:T(8,128)(2,1)S(1)} all-to-all(bf16[8,80,256]{2,1,0:T(8,128)(2,1)} %get-tuple-element.7), channel_id=1, replica_groups=mesh['pair'=2,'virt'=4,'y'=4,'z'=8] {'z'}, dimensions={0} | all-to-all | bytes 655360 | tf_op jit(solution)/shard_map/all_to_all | solution.py:186
  38.6 15.6 %all_to_all.21.rows_ref = bf16[16,72,256]{2,1,0:T(8,128)(2,1)S(1)} all-to-all(bf16[16,72,256]{2,1,0:T(8,128)(2,1)S(1)} %spread_kernel.1), channel_id=1, replica_groups=mesh['pair'=2,'virt'=4,'y'=4,'z'=8] {'virt','y'}, dimensions={0} | all-to-all | bytes 1179648 | tf_op jit(solution)/shard_map/all_to_all | solution.py:190
  54.1 0.0 all-gather.2.cloned.1.call-done.near_ref
  54.1 0.0 copy-done
  54.1 0.0 copy-done.4
  54.1 0.0 copy-start.1
  54.1 1.6 %copy-done.1 = bf16[16,256,256]{2,1,0:T(8,128)(2,1)S(1)} copy-done((bf16[16,256,256]{2,1,0:T(8,128)(2,1)S(1)}, bf16[16,256,256]{2,1,0:T(8,128)(2,1)}, u32[]{:S(2)}) %copy-start.1) | copy-done | bytes 2097176
  55.7 9.6 %ladder_kernel.1 = bf16[16,72,256]{2,1,0:T(8,128)(2,1)S(1)} custom-call(s32[2,2]{1,0:T(2,128)S(1)} %copy-done.4, bf16[16,72,256]{2,1,0:T(8,128)(2,1)S(1)} %all_to_all.21.rows_ref, bf16[16,256,256]{2,1,0:T(8,128)(2,1)S(1)} %copy-done, bf16[16,256,256]{2,1,0:T(8,128)(2,1)S(1)} %copy-done.1), custom_call_target="tpu_custom_call" | custom-call | tf_op jit(solution)/shard_map/ladder_kernel/pallas_call | solution.py:156
  65.4 0.0 copy-start.2
  65.4 0.0 copy-start.3
  65.4 0.0 copy-start.5
  65.4 13.8 %all_to_all.22.got_ref = bf16[16,72,256]{2,1,0:T(8,128)(2,1)S(1)} all-to-all(bf16[16,72,256]{2,1,0:T(8,128)(2,1)S(1)} %ladder_kernel.1), channel_id=1, replica_groups=mesh['pair'=2,'virt'=4,'y'=4,'z'=8] {'virt','y'}, dimensions={0} | all-to-all | bytes 1179648 | tf_op jit(solution)/shard_map/all_to_all | solution.py:200
  79.2 0.8 sum_kernel.1
  80.0 9.2 %all-to-all-start.3 = ((bf16[8,80,256]{2,1,0:T(8,128)(2,1)}), bf16[8,80,256]{2,1,0:T(8,128)(2,1)S(1)}, u32[]{:S(2)}, u32[]{:S(2)}) async-start(bf16[8,80,256]{2,1,0:T(8,128)(2,1)} %sum_kernel.1), calls=%async_computation.3 | async-start | bytes 655360 | tf_op jit(solution)/shard_map/all_to_all | solution.py:202
  90.5 11.2 %all-to-all-done.3.got_ref = bf16[8,80,256]{2,1,0:T(8,128)(2,1)S(1)} async-done(((bf16[8,80,256]{2,1,0:T(8,128)(2,1)}), bf16[8,80,256]{2,1,0:T(8,128)(2,1)S(1)}, u32[]{:S(2)}, u32[]{:S(2)}) %all-to-all-start.3) | async-done | bytes 327712 | tf_op jit(solution)/shard_map/all_to_all | solution.py:202
  101.8 0.0 copy-done.2
  101.8 0.0 copy-done.3
  101.8 0.0 copy-done.5
  101.8 1.4 %update_kernel.1 = bf16[1,1,64,256]{3,2,1,0:T(8,128)(2,1)} custom-call(s32[1,1,2]{2,1,0:T(1,128)S(1)} %copy-done.3, f32[1]{0:T(128)S(6)} %copy.9.occ_i_ref, f32[1]{0:T(128)S(6)} %copy.10.occ_j_ref, f32[1,256]{1,0:T(1,128)S(1)} %bitcast.4, bf16[8,80,256]{2,1,0:T(8,128)(2,1)S(1)} %all-to-all-done.3.got_ref, bf16[512,256]{1,0:T(8,128)(2,1)S(1)} %bitcast.3), custom_call_target="tpu_custom_call" | custom-call | tf_op jit(solution)/shard_map/update_kernel/pallas_call | solution.py:156
  (1 shorter events, 0.0 us)
Async XLA Ops:
  6.5 47.6 %all-gather.2.cloned.1.call-start = ((), (), s32[]{:S(2)}) async-start(), calls=%async_computation.4 | async-start | bytes 2359296 | tf_op jit(solution)/shard_map/all_gather | solution.py:189
  8.5 45.6 %copy-start = (bf16[16,256,256]{2,1,0:T(8,128)(2,1)S(1)}, bf16[16,256,256]{2,1,0:T(8,128)(2,1)}, u32[]{:S(2)}) copy-start(bf16[16,256,256]{2,1,0:T(8,128)(2,1)} %own_ref.1) | copy-start | bytes 6291460
  8.5 45.6 %copy-start.4 = (s32[2,2]{1,0:T(2,128)S(1)}, s32[2,2]{1,0:T(2,128)}, u32[]{:S(2)}) copy-start(s32[2,2]{1,0:T(2,128)} %mask_ref.1) | copy-start | bytes 52
  8.6 8.3 %collective-permute-start = (bf16[2,256,256]{2,1,0:T(8,128)(2,1)}, bf16[2,256,256]{2,1,0:T(8,128)(2,1)S(1)}, u32[]{:S(2)}, u32[]{:S(2)}) collective-permute-start(bf16[2,256,256]{2,1,0:T(8,128)(2,1)} %get-tuple-element.8), channel_id=1, source_target_pairs={{0,8},{8,0},{16,24},{24,16},{1,9},{9,1},{17,25},{25,17},{2,10},{10... | collective-permute-start | bytes 786440 | tf_op jit(solution)/shard_map/ppermute | solution.py:188
  16.9 0.7 copy-start.6
  54.1 1.6 %copy-start.1 = (bf16[16,256,256]{2,1,0:T(8,128)(2,1)S(1)}, bf16[16,256,256]{2,1,0:T(8,128)(2,1)}, u32[]{:S(2)}) copy-start(bf16[16,256,256]{2,1,0:T(8,128)(2,1)} %all-gather.2.cloned.1.call-done.near_ref) | copy-start | bytes 6291460
  65.4 36.4 %copy-start.2 = (bf16[512,1,256]{2,0,1:T(8,128)(2,1)S(1)}, bf16[512,1,256]{2,0,1:T(8,128)(2,1)}, u32[]{:S(2)}) copy-start(bf16[512,1,256]{2,0,1:T(8,128)(2,1)} %param.10) | copy-start | bytes 786436
  65.4 36.4 %copy-start.3 = (s32[1,1,2]{2,1,0:T(1,128)S(1)}, s32[1,1,2]{2,1,0:T(1,128)}, u32[]{:S(2)}) copy-start(s32[1,1,2]{2,1,0:T(1,128)} %domain_ref.1) | copy-start | bytes 28
  65.4 36.4 %copy-start.5 = (f32[256]{0:T(256)S(1)}, f32[256]{0:T(256)}, u32[]{:S(2)}) copy-start(f32[256]{0:T(256)} %param.13) | copy-start | bytes 3076
  80.0 21.7 %all-to-all-start.3 = ((bf16[8,80,256]{2,1,0:T(8,128)(2,1)}), bf16[8,80,256]{2,1,0:T(8,128)(2,1)S(1)}, u32[]{:S(2)}, u32[]{:S(2)}) async-start(bf16[8,80,256]{2,1,0:T(8,128)(2,1)} %sum_kernel.1), calls=%async_computation.3 | async-start | bytes 655360 | tf_op jit(solution)/shard_map/all_to_all | solution.py:202
Sparse Core Ops, SparseCore 0:
  17.7 30.4 all-gather.1

commit v6 on v5

--- a/solution.py
+++ b/solution.py
@@ -18,22 +18,23 @@
 COLS = 256
 AUX = 16
 PART = 8
-SHARE = 2
-
-
-def out_kernel(domain_hbm, amp_hbm, ov_hbm, factors_hbm, out_ref, share_ref, domain, amp, sems):
+SHARE = 4
+
+
+def out_kernel(domain_hbm, amp_hbm, ov_hbm, factors_hbm, out_ref, up_ref, down_ref, domain, amp, sems):
     x = lax.axis_index("virt")
-    share = (2 * x + lax.axis_index("pair")) * SHARE
+    share = lax.axis_index("pair") * SHARE
     copies = [
         pltpu.make_async_copy(domain_hbm.at[0], domain, sems.at[0]),
         pltpu.make_async_copy(amp_hbm.at[0, 0], amp, sems.at[1]),
-        pltpu.make_async_copy(factors_hbm.at[pl.ds(share, SHARE)], share_ref, sems.at[2]),
+        pltpu.make_async_copy(factors_hbm.at[pl.ds(share, SHARE)], up_ref, sems.at[2]),
+        pltpu.make_async_copy(factors_hbm.at[pl.ds(2 * SHARE + share, SHARE)], down_ref, sems.at[3]),
     ]
     for to in range(Z):
         for high in range(2):
             start = pl.multiple_of(((2 * high + x // 2) * Z + to) * AUX + (x % 2) * PART, PART)
             target = out_ref.at[to, pl.ds(ROWS + high * PART, PART)]
-            copies.append(pltpu.make_async_copy(ov_hbm.at[pl.ds(start, PART)], target, sems.at[3 + 2 * to + high]))
+            copies.append(pltpu.make_async_copy(ov_hbm.at[pl.ds(start, PART)], target, sems.at[4 + 2 * to + high]))
     for copy in copies:
         copy.start()
     copies[0].wait()
@@ -58,8 +59,9 @@
             out_ref[to_x * Y + to_y, ROWS:] = got_ref[2 * to_x + low, start : start + PART]
 
 
-def ladder_kernel(mask_ref, rows_ref, own_ref, near_ref, out_ref, masked, weighted):
-    sources = [(ref, aux) for ref in (own_ref, near_ref) for aux in range(AUX)]
+def ladder_kernel(mask_ref, rows_ref, own_ref, up_ref, down_ref, up2_ref, down2_ref, out_ref, masked, weighted):
+    sources = [(own_ref, aux) for aux in range(AUX)]
+    sources += [(ref, aux) for ref in (up_ref, down_ref, up2_ref, down2_ref) for aux in range(SHARE)]
     for p in range(2):
         for q in range(2):
             keep = jnp.full((1, TILE_SIZE), mask_ref[p, q], jnp.int32).astype(F32).astype(BF16)
@@ -168,32 +170,35 @@
 ):
     ov = ov_factors[:, 0, :]
     hbm = pl.BlockSpec(memory_space=pltpu.HBM)
-    sent, mine = pl.pallas_call(
+    sent, up, down = pl.pallas_call(
         out_kernel,
         name="out_kernel",
         in_specs=[hbm, hbm, hbm, hbm],
-        out_specs=[pl.BlockSpec(memory_space=pltpu.VMEM)] * 2,
+        out_specs=[pl.BlockSpec(memory_space=pltpu.VMEM), hbm, hbm],
         out_shape=[
             jax.ShapeDtypeStruct((Z, ROWS + AUX, COLS), BF16),
+            jax.ShapeDtypeStruct((SHARE, COLS, COLS), BF16),
             jax.ShapeDtypeStruct((SHARE, COLS, COLS), BF16),
         ],
         scratch_shapes=[
             pltpu.SMEM((1, 2), jnp.int32),
             pltpu.VMEM((ROWS, COLS), BF16),
-            pltpu.SemaphoreType.DMA((3 + 2 * Z,)),
+            pltpu.SemaphoreType.DMA((4 + 2 * Z,)),
         ],
     )(pair_domain, amplitudes, ov, vv_factors)
     got = lax.all_to_all(sent, "z", 0, 0, tiled=True)
     sent = kernel(spread_kernel, (VIRT * Y, ROWS + PART, COLS), (), (got,))
-    near = lax.ppermute(mine, "y", [(y, y ^ 1) for y in range(Y)])
-    near = lax.all_gather(near, ("virt", "pair"), axis=0, tiled=True)
+    swap = [(0, 1), (1, 0)]
+    up = lax.ppermute(up, "y", [(y, (y + 1) % Y) for y in range(Y)])
+    down = lax.ppermute(down, "y", [(y, (y - 1) % Y) for y in range(Y)])
+    extra = (up, down, lax.ppermute(up, "pair", swap), lax.ppermute(down, "pair", swap))
     got = lax.all_to_all(sent, ("virt", "y"), 0, 0, tiled=True)
     wide = pltpu.VMEM((COLS, 2 * AUX * COLS), BF16)
     sent = kernel(
         ladder_kernel,
         (VIRT * Y, ROWS + PART, COLS),
         (vv_mask,),
-        (got, vv_factors, near),
+        (got, vv_factors) + extra,
         (wide, wide),
         40,
     )

time: 111 us -> 117 us (1.054)
  blocking collectives: 50.3 us -> 14 us
  Pallas kernels: 13.9 us -> 47.2 us
  between operations: 14.8 us -> 1.38 us
  starting transfers between devices: 10.9 us -> 23.2 us
  waiting for transfers between devices: 17.9 us -> 25.8 us
  local copies, waits for them, and re-layouts: 2.33 us -> 3.72 us
    pallas_call x1, Pallas kernels: 1.98 us -> 33.8 us  [body(): pl.pallas_call(out_kernel, name='out_kernel', in_specs=[hbm, hbm, hbm, hb...]
    all_to_all x1 -> x0, blocking collectives: 20.9 us -> none  [body(): got = lax.all_to_all(sent, 'z', 0, 0, tiled=True)]
    all_to_all x2 -> x1, blocking collectives: 29.4 us -> 14 us  [body(): got = lax.all_to_all(sent, ('virt', 'y'), 0, 0, tiled=True)]
    all_to_all x1 -> x2, waiting for transfers between devices: 11.2 us -> 19.8 us  [body(): got = lax.all_to_all(sent, 'z', 0, 0, tiled=True)]
    all_to_all x0 -> x1, starting transfers between devices: none -> 7.45 us  [body(): got = lax.all_to_all(sent, ('virt', 'y'), 0, 0, tiled=True)]
    ppermute x1 -> x4, waiting for transfers between devices: 6.68 us -> 1.56 us  [the longest x1 1.4 us: body(): lax.ppermute(up, 'pair', swap)]
    all_to_all x0 -> x1, waiting for transfers between devices: none -> 4.41 us  [body(): got = lax.all_to_all(sent, ('virt', 'y'), 0, 0, tiled=True)]
    all_to_all x1 -> x2, starting transfers between devices: 9.19 us -> 11.9 us  [body(): got = lax.all_to_all(sent, 'z', 0, 0, tiled=True)]
  transfers between devices with their start and end apart: 3 -> 7, of which waited for: 2 -> 5; matrix products, arithmetic and copies ran while one was open for 0% -> 0% of each run, Pallas kernels for 0% -> 1%
where the time goes in v6:
time: 117 us; the launch traced here: 115 us
  Pallas kernels  47.2 us (40%)
  waiting for transfers between devices  25.8 us (22%)
  starting transfers between devices  23.2 us (20%)
  blocking collectives  14 us (12%)
  local copies, waits for them, and re-layouts  3.72 us (3%)
  between operations  1.38 us (1%)
    pallas_call x1, Pallas kernels, body(): pl.pallas_call(out_kernel, name='out_kernel', in_specs=[hbm, hbm, hbm, hb...  33.8 us
    all_to_all x2, waiting for transfers between devices, body(): got = lax.all_to_all(sent, 'z', 0, 0, tiled=True)  19.8 us
    all_to_all x1, blocking collectives, body(): got = lax.all_to_all(sent, ('virt', 'y'), 0, 0, tiled=True)  14 us
    pallas_call x4, Pallas kernels, kernel(): return call(*scalars, *arrays)  13.4 us
    all_to_all x2, starting transfers between devices, body(): got = lax.all_to_all(sent, 'z', 0, 0, tiled=True)  11.9 us
    all_to_all x1, starting transfers between devices, body(): got = lax.all_to_all(sent, ('virt', 'y'), 0, 0, tiled=True)  7.45 us
    all_to_all x1, waiting for transfers between devices, body(): got = lax.all_to_all(sent, ('virt', 'y'), 0, 0, tiled=True)  4.41 us
    unnamed x18, local copies, waits for them, and re-layouts  3.72 us
  transfers between devices with their start and end apart: 7, of which 5 were waited for; matrix products, arithmetic and copies ran while one was open for 0% of the time, Pallas kernels for 1%

profile of v6, /device:TPU:4, one launch (start us, length us, event | category | flops | bytes accessed | tf_op | source)
XLA Modules:
  0.0 115.3 jit_solution(992503402489058683)
XLA Ops:
  0.0 0.0 copy-start
  0.0 0.0 copy-start.7
  0.0 33.8 %out_kernel.1 = (bf16[8,80,256]{2,1,0:T(8,128)(2,1)}, bf16[4,256,256]{2,1,0:T(8,128)(2,1)}, bf16[4,256,256]{2,1,0:T(8,128)(2,1)}) custom-call(s32[1,1,2]{2,1,0:T(1,128)} %domain_ref.1, bf16[1,1,64,256]{3,2,1,0:T(8,128)(2,1)} %amp_hbm.1, bf16[512,256]{1,0:T(8,128)(2,1)} %bitcast.2, bf16[16,256,256]{2,1,0:T(8,128)(2,1)} %own_ref.1), custom_call_target="tpu_custom_call" | custom-call | tf_op jit(solution)/shard_map/out_kernel/pallas_call | solution.py:173
  33.8 8.5 %all-to-all-start = ((bf16[8,80,256]{2,1,0:T(8,128)(2,1)}), bf16[8,80,256]{2,1,0:T(8,128)(2,1)S(1)}, u32[]{:S(2)}, u32[]{:S(2)}) async-start(bf16[8,80,256]{2,1,0:T(8,128)(2,1)} %get-tuple-element.8), calls=%async_computation | async-start | bytes 655360 | tf_op jit(solution)/shard_map/all_to_all | solution.py:189
  42.3 1.6 %collective-permute-start = (bf16[4,256,256]{2,1,0:T(8,128)(2,1)}, bf16[4,256,256]{2,1,0:T(8,128)(2,1)S(1)}, u32[]{:S(2)}, u32[]{:S(2)}) collective-permute-start(bf16[4,256,256]{2,1,0:T(8,128)(2,1)} %get-tuple-element.9), channel_id=1, source_target_pairs={{0,8},{8,16},{16,24},{24,0},{1,9},{9,17},{17,25},{25,1},{2,10},{10... | collective-permute-start | bytes 1572872 | tf_op jit(solution)/shard_map/ppermute | solution.py:192
  43.9 1.7 %collective-permute-start.1 = (bf16[4,256,256]{2,1,0:T(8,128)(2,1)}, bf16[4,256,256]{2,1,0:T(8,128)(2,1)}, u32[]{:S(2)}, u32[]{:S(2)}) collective-permute-start(bf16[4,256,256]{2,1,0:T(8,128)(2,1)} %get-tuple-element.10), channel_id=1, source_target_pairs={{0,24},{8,0},{16,8},{24,16},{1,25},{9,1},{17,9},{25,17},{2,26},{10... | collective-permute-start | bytes 1572872 | tf_op jit(solution)/shard_map/ppermute | solution.py:193
  45.5 10.0 %all-to-all-done.got_ref = bf16[8,80,256]{2,1,0:T(8,128)(2,1)S(1)} async-done(((bf16[8,80,256]{2,1,0:T(8,128)(2,1)}), bf16[8,80,256]{2,1,0:T(8,128)(2,1)S(1)}, u32[]{:S(2)}, u32[]{:S(2)}) %all-to-all-start) | async-done | bytes 327712 | tf_op jit(solution)/shard_map/all_to_all | solution.py:189
  55.6 0.9 spread_kernel.1
  56.4 7.5 %all-to-all-start.1 = ((bf16[16,72,256]{2,1,0:T(8,128)(2,1)}), bf16[16,72,256]{2,1,0:T(8,128)(2,1)S(1)}, u32[]{:S(2)}, u32[]{:S(2)}) async-start(bf16[16,72,256]{2,1,0:T(8,128)(2,1)} %spread_kernel.1), calls=%async_computation.1 | async-start | bytes 1179648 | tf_op jit(solution)/shard_map/all_to_all | solution.py:195
  63.9 0.0 collective-permute-done.up_ref
  63.9 0.1 collective-permute-start.2
  64.0 0.0 collective-permute-done.1.down_ref
  64.0 0.5 collective-permute-start.3
  64.5 1.4 %collective-permute-done.2.up2_ref = bf16[4,256,256]{2,1,0:T(8,128)(2,1)S(1)} collective-permute-done((bf16[4,256,256]{2,1,0:T(8,128)(2,1)S(1)}, bf16[4,256,256]{2,1,0:T(8,128)(2,1)S(1)}, u32[]{:S(2)}, u32[]{:S(2)}) %collective-permute-start.2) | collective-permute-done | bytes 524320 | tf_op jit(solution)/shard_map/ppermute | solution.py:194
  65.9 0.0 copy-start.2
  65.9 0.8 copy-done.2
  66.7 0.2 collective-permute-done.3.down2_ref
  66.9 0.0 copy-start.4
  66.9 0.8 copy-done.4
  67.7 4.4 %all-to-all-done.1.rows_ref = bf16[16,72,256]{2,1,0:T(8,128)(2,1)S(1)} async-done(((bf16[16,72,256]{2,1,0:T(8,128)(2,1)}), bf16[16,72,256]{2,1,0:T(8,128)(2,1)S(1)}, u32[]{:S(2)}, u32[]{:S(2)}) %all-to-all-start.1) | async-done | bytes 589856 | tf_op jit(solution)/shard_map/all_to_all | solution.py:195
  72.1 0.0 copy-done
  72.1 0.0 copy-done.7
  72.1 0.0 copy-start.3
  72.1 1.0 copy-done.3
  73.1 0.0 copy-start.5
  73.1 1.0 copy-done.5
  74.2 10.3 %ladder_kernel.1 = bf16[16,72,256]{2,1,0:T(8,128)(2,1)S(1)} custom-call(s32[2,2]{1,0:T(2,128)S(1)} %copy-done.7, bf16[16,72,256]{2,1,0:T(8,128)(2,1)S(1)} %all-to-all-done.1.rows_ref, bf16[16,256,256]{2,1,0:T(8,128)(2,1)S(1)} %copy-done, bf16[4,256,256]{2,1,0:T(8,128)(2,1)S(1)} %collective-permute-done.up_ref, ...), custom_call_target="tpu_custom_call" | custom-call | tf_op jit(solution)/shard_map/ladder_kernel/pallas_call | solution.py:158
  84.5 0.0 copy-start.1
  84.5 0.0 copy-start.6
  84.5 0.0 copy-start.8
  84.5 14.0 %all_to_all.20.got_ref = bf16[16,72,256]{2,1,0:T(8,128)(2,1)S(1)} all-to-all(bf16[16,72,256]{2,1,0:T(8,128)(2,1)S(1)} %ladder_kernel.1), channel_id=1, replica_groups=mesh['pair'=2,'virt'=4,'y'=4,'z'=8] {'virt','y'}, dimensions={0} | all-to-all | bytes 1179648 | tf_op jit(solution)/shard_map/all_to_all | solution.py:205
  98.5 0.8 sum_kernel.1
  99.3 3.4 %all-to-all-start.3 = ((bf16[8,80,256]{2,1,0:T(8,128)(2,1)}), bf16[8,80,256]{2,1,0:T(8,128)(2,1)S(1)}, u32[]{:S(2)}, u32[]{:S(2)}) async-start(bf16[8,80,256]{2,1,0:T(8,128)(2,1)} %sum_kernel.1), calls=%async_computation.3 | async-start | bytes 655360 | tf_op jit(solution)/shard_map/all_to_all | solution.py:207
  104.1 9.8 %all-to-all-done.3.got_ref = bf16[8,80,256]{2,1,0:T(8,128)(2,1)S(1)} async-done(((bf16[8,80,256]{2,1,0:T(8,128)(2,1)}), bf16[8,80,256]{2,1,0:T(8,128)(2,1)S(1)}, u32[]{:S(2)}, u32[]{:S(2)}) %all-to-all-start.3) | async-done | bytes 327712 | tf_op jit(solution)/shard_map/all_to_all | solution.py:207
  113.9 0.0 copy-done.1
  113.9 0.0 copy-done.6
  113.9 0.0 copy-done.8
  113.9 1.4 %update_kernel.1 = bf16[1,1,64,256]{3,2,1,0:T(8,128)(2,1)} custom-call(s32[1,1,2]{2,1,0:T(1,128)S(1)} %copy-done.6, f32[1]{0:T(128)S(6)} %copy.9.occ_i_ref, f32[1]{0:T(128)S(6)} %copy.10.occ_j_ref, f32[1,256]{1,0:T(1,128)S(1)} %bitcast.4, bf16[8,80,256]{2,1,0:T(8,128)(2,1)S(1)} %all-to-all-done.3.got_ref, bf16[512,256]{1,0:T(8,128)(2,1)S(1)} %bitcast.3), custom_call_target="tpu_custom_call" | custom-call | tf_op jit(solution)/shard_map/update_kernel/pallas_call | solution.py:158
Async XLA Ops:
  0.0 72.1 %copy-start = (bf16[16,256,256]{2,1,0:T(8,128)(2,1)S(1)}, bf16[16,256,256]{2,1,0:T(8,128)(2,1)}, u32[]{:S(2)}) copy-start(bf16[16,256,256]{2,1,0:T(8,128)(2,1)} %own_ref.1) | copy-start | bytes 6291460
  0.0 72.1 %copy-start.7 = (s32[2,2]{1,0:T(2,128)S(1)}, s32[2,2]{1,0:T(2,128)}, u32[]{:S(2)}) copy-start(s32[2,2]{1,0:T(2,128)} %mask_ref.1) | copy-start | bytes 52
  33.8 21.8 %all-to-all-start = ((bf16[8,80,256]{2,1,0:T(8,128)(2,1)}), bf16[8,80,256]{2,1,0:T(8,128)(2,1)S(1)}, u32[]{:S(2)}, u32[]{:S(2)}) async-start(bf16[8,80,256]{2,1,0:T(8,128)(2,1)} %get-tuple-element.8), calls=%async_computation | async-start | bytes 655360 | tf_op jit(solution)/shard_map/all_to_all | solution.py:189
  42.3 21.6 %collective-permute-start = (bf16[4,256,256]{2,1,0:T(8,128)(2,1)}, bf16[4,256,256]{2,1,0:T(8,128)(2,1)S(1)}, u32[]{:S(2)}, u32[]{:S(2)}) collective-permute-start(bf16[4,256,256]{2,1,0:T(8,128)(2,1)} %get-tuple-element.9), channel_id=1, source_target_pairs={{0,8},{8,16},{16,24},{24,0},{1,9},{9,17},{17,25},{25,1},{2,10},{10... | collective-permute-start | bytes 1572872 | tf_op jit(solution)/shard_map/ppermute | solution.py:192
  43.9 20.1 %collective-permute-start.1 = (bf16[4,256,256]{2,1,0:T(8,128)(2,1)}, bf16[4,256,256]{2,1,0:T(8,128)(2,1)}, u32[]{:S(2)}, u32[]{:S(2)}) collective-permute-start(bf16[4,256,256]{2,1,0:T(8,128)(2,1)} %get-tuple-element.10), channel_id=1, source_target_pairs={{0,24},{8,0},{16,8},{24,16},{1,25},{9,1},{17,9},{25,17},{2,26},{10... | collective-permute-start | bytes 1572872 | tf_op jit(solution)/shard_map/ppermute | solution.py:193
  56.4 15.6 %all-to-all-start.1 = ((bf16[16,72,256]{2,1,0:T(8,128)(2,1)}), bf16[16,72,256]{2,1,0:T(8,128)(2,1)S(1)}, u32[]{:S(2)}, u32[]{:S(2)}) async-start(bf16[16,72,256]{2,1,0:T(8,128)(2,1)} %spread_kernel.1), calls=%async_computation.1 | async-start | bytes 1179648 | tf_op jit(solution)/shard_map/all_to_all | solution.py:195
  63.9 2.0 %collective-permute-start.2 = (bf16[4,256,256]{2,1,0:T(8,128)(2,1)S(1)}, bf16[4,256,256]{2,1,0:T(8,128)(2,1)S(1)}, u32[]{:S(2)}, u32[]{:S(2)}) collective-permute-start(bf16[4,256,256]{2,1,0:T(8,128)(2,1)S(1)} %collective-permute-done.up_ref), channel_id=1, source_target_pairs={{0,128},{128,0},{1,129},{129,1},{2,130},{130,2},{3,131},{131,3},{4... | collective-permute-start | bytes 1572872 | tf_op jit(solution)/shard_map/ppermute | solution.py:194
  64.0 2.8 %collective-permute-start.3 = (bf16[4,256,256]{2,1,0:T(8,128)(2,1)}, bf16[4,256,256]{2,1,0:T(8,128)(2,1)S(1)}, u32[]{:S(2)}, u32[]{:S(2)}) collective-permute-start(bf16[4,256,256]{2,1,0:T(8,128)(2,1)} %collective-permute-done.1.down_ref), channel_id=1, source_target_pairs={{0,128},{128,0},{1,129},{129,1},{2,130},{130,2},{3,131},{131,3},{4... | collective-permute-start | bytes 1572872 | tf_op jit(solution)/shard_map/ppermute | solution.py:194
  65.9 0.8 copy-start.2
  66.9 0.8 copy-start.4
  72.1 1.0 copy-start.3
  73.1 1.0 copy-start.5
  84.5 29.4 %copy-start.1 = (bf16[512,1,256]{2,0,1:T(8,128)(2,1)S(1)}, bf16[512,1,256]{2,0,1:T(8,128)(2,1)}, u32[]{:S(2)}) copy-start(bf16[512,1,256]{2,0,1:T(8,128)(2,1)} %param.10) | copy-start | bytes 786436
  84.5 29.4 %copy-start.6 = (s32[1,1,2]{2,1,0:T(1,128)S(1)}, s32[1,1,2]{2,1,0:T(1,128)}, u32[]{:S(2)}) copy-start(s32[1,1,2]{2,1,0:T(1,128)} %domain_ref.1) | copy-start | bytes 28
  84.5 29.4 %copy-start.8 = (f32[256]{0:T(256)S(1)}, f32[256]{0:T(256)}, u32[]{:S(2)}) copy-start(f32[256]{0:T(256)} %param.13) | copy-start | bytes 3076
  99.3 14.5 %all-to-all-start.3 = ((bf16[8,80,256]{2,1,0:T(8,128)(2,1)}), bf16[8,80,256]{2,1,0:T(8,128)(2,1)S(1)}, u32[]{:S(2)}, u32[]{:S(2)}) async-start(bf16[8,80,256]{2,1,0:T(8,128)(2,1)} %sum_kernel.1), calls=%async_computation.3 | async-start | bytes 655360 | tf_op jit(solution)/shard_map/all_to_all | solution.py:207

commit v7 on v4

--- a/solution.py
+++ b/solution.py
@@ -18,6 +18,7 @@
 COLS = 256
 AUX = 16
 PART = 8
+SHARE = 4
 
 
 def out_kernel(domain_hbm, amp_hbm, ov_hbm, out_ref, domain, amp, sems):
@@ -46,6 +47,16 @@
         copy.wait()
 
 
+def share_kernel(factors_hbm, up_ref, down_ref, sems):
+    share = lax.axis_index("pair") * SHARE
+    up = pltpu.make_async_copy(factors_hbm.at[pl.ds(share, SHARE)], up_ref, sems.at[0])
+    down = pltpu.make_async_copy(factors_hbm.at[pl.ds(2 * SHARE + share, SHARE)], down_ref, sems.at[1])
+    up.start()
+    down.start()
+    up.wait()
+    down.wait()
+
+
 def spread_kernel(got_ref, out_ref):
     for to_x in range(VIRT):
         for to_y in range(Y):
@@ -55,16 +66,17 @@
             out_ref[to_x * Y + to_y, ROWS:] = got_ref[2 * to_x + low, start : start + PART]
 
 
-def ladder_kernel(mask_ref, rows_ref, own_ref, near_ref, far_ref, out_ref, masked, weighted):
-    sources = [(own_ref, aux) for aux in range(AUX)]
-    sources += [(ref, aux) for ref in (near_ref, far_ref) for aux in range(PART)]
-    for p in range(2):
-        for q in range(2):
-            keep = jnp.full((1, TILE_SIZE), mask_ref[p, q], jnp.int32).astype(F32).astype(BF16)
-            for slot, (ref, aux) in enumerate(sources):
-                block = ref[aux, p * 128 : (p + 1) * 128, q * 128 : (q + 1) * 128] * keep
-                masked[p * 128 : (p + 1) * 128, slot * 256 + q * 128 : slot * 256 + (q + 1) * 128] = block
-
+def ladder_kernel(
+    mask_ref, rows_ref, own_hbm, up_hbm, down_hbm, up2_hbm, down2_hbm, out_ref, factors, masked, weighted, sems
+):
+    sources = [(own_hbm, aux) for aux in range(AUX)]
+    sources += [(ref, aux) for ref in (up_hbm, down_hbm, up2_hbm, down2_hbm) for aux in range(SHARE)]
+    copies = [
+        pltpu.make_async_copy(ref.at[aux], factors.at[slot], sems.at[slot]) for slot, (ref, aux) in enumerate(sources)
+    ]
+    for copy in copies:
+        copy.start()
+    keep = [[jnp.full((1, TILE_SIZE), mask_ref[p, q], jnp.int32).astype(F32).astype(BF16) for q in range(2)] for p in range(2)]
     zeta = jnp.zeros((2 * AUX, COLS), F32)
     for at_y in range(Y):
         amp = jnp.concatenate([rows_ref[at_x * Y + at_y, :ROWS] for at_x in range(VIRT)], axis=0)
@@ -73,7 +85,15 @@
         swapped = jnp.dot(fac, amp, preferred_element_type=F32)
         zeta = zeta + (2.0 * direct - swapped)
         for slot in range(2 * AUX):
-            cols = slice(slot * 256, (slot + 1) * 256)
+            cols = slice(slot * COLS, (slot + 1) * COLS)
+            if at_y == 0:
+                copies[slot].wait()
+                for p in range(2):
+                    for q in range(2):
+                        rows = slice(p * TILE_SIZE, (p + 1) * TILE_SIZE)
+                        lanes = slice(q * TILE_SIZE, (q + 1) * TILE_SIZE)
+                        left = slot * COLS + q * TILE_SIZE
+                        masked[rows, left : left + TILE_SIZE] = factors[slot, rows, lanes] * keep[p][q]
             weighted[:, cols] = jnp.dot(masked[:, cols], amp, preferred_element_type=F32).astype(BF16)
         total = lax.dot_general(weighted[...], masked[...], NT, preferred_element_type=F32).astype(BF16)
         for at_x in range(VIRT):
@@ -165,7 +185,6 @@
     pair_domain,
 ):
     ov = ov_factors[:, 0, :]
-    mine = lax.dynamic_slice_in_dim(vv_factors, lax.axis_index("pair") * PART, PART, 0)
     hbm = pl.BlockSpec(memory_space=pltpu.HBM)
     sent = pl.pallas_call(
         out_kernel,
@@ -179,20 +198,36 @@
             pltpu.SemaphoreType.DMA((2 + 2 * Z,)),
         ],
     )(pair_domain, amplitudes, ov)
+    up, down = pl.pallas_call(
+        share_kernel,
+        name="share_kernel",
+        in_specs=[hbm],
+        out_specs=[pl.BlockSpec(memory_space=pltpu.VMEM)] * 2,
+        out_shape=[jax.ShapeDtypeStruct((SHARE, COLS, COLS), BF16)] * 2,
+        scratch_shapes=[pltpu.SemaphoreType.DMA((2,))],
+    )(vv_factors)
     got = lax.all_to_all(sent, "z", 0, 0, tiled=True)
     sent = kernel(spread_kernel, (VIRT * Y, ROWS + PART, COLS), (), (got,))
-    near = lax.ppermute(mine, "y", [(y, y ^ 1) for y in range(Y)])
-    far = lax.ppermute(near, "pair", [(0, 1), (1, 0)])
+    swap = [(0, 1), (1, 0)]
+    up = lax.ppermute(up, "y", [(y, (y + 1) % Y) for y in range(Y)])
+    down = lax.ppermute(down, "y", [(y, (y - 1) % Y) for y in range(Y)])
+    extra = (up, down, lax.ppermute(up, "pair", swap), lax.ppermute(down, "pair", swap))
     got = lax.all_to_all(sent, ("virt", "y"), 0, 0, tiled=True)
     wide = pltpu.VMEM((COLS, 2 * AUX * COLS), BF16)
-    sent = kernel(
+    sent = pl.pallas_call(
         ladder_kernel,
-        (VIRT * Y, ROWS + PART, COLS),
-        (vv_mask,),
-        (got, vv_factors, near, far),
-        (wide, wide),
-        40,
-    )
+        name="ladder_kernel",
+        in_specs=[pl.BlockSpec(memory_space=pltpu.SMEM), pl.BlockSpec(memory_space=pltpu.VMEM)] + [hbm] * 5,
+        out_specs=pl.BlockSpec(memory_space=pltpu.VMEM),
+        out_shape=jax.ShapeDtypeStruct((VIRT * Y, ROWS + PART, COLS), BF16),
+        scratch_shapes=[
+            pltpu.VMEM((2 * AUX, COLS, COLS), BF16),
+            wide,
+            wide,
+            pltpu.SemaphoreType.DMA((2 * AUX,)),
+        ],
+        compiler_params=pltpu.CompilerParams(vmem_limit_bytes=40 << 20),
+    )(vv_mask, got, vv_factors, *[pltpu.with_memory_space_constraint(part, pltpu.HBM) for part in extra])
     got = lax.all_to_all(sent, ("virt", "y"), 0, 0, tiled=True)
     sent = kernel(sum_kernel, (Z, ROWS + AUX, COLS), (), (got,))
     got = lax.all_to_all(sent, "z", 0, 0, tiled=True)

time: 94.1 us -> 94.2 us (level)
  blocking collectives: 33.1 us -> 14 us
  Pallas kernels: 14.3 us -> 26.7 us
  starting transfers between devices: 18.5 us -> 24.6 us
  waiting for transfers between devices: 23.5 us -> 25.6 us
  local copies, waits for them, and re-layouts: 2.29 us -> 0.83 us
    pallas_call x0 -> x2, Pallas kernels: none -> 21.9 us  [the longest x1 19.5 us: body(): pl.pallas_call(ladder_kernel, name='ladder_kernel', in_specs=[pl.BlockSpe...]
    all_to_all x2 -> x1, blocking collectives: 33.1 us -> 14 us  [body(): got = lax.all_to_all(sent, ('virt', 'y'), 0, 0, tiled=True)]
    ppermute x2 -> x4, waiting for transfers between devices: 13.3 us -> 1.69 us  [the longest x1 1.4 us: body(): lax.ppermute(up, 'pair', swap)]
    pallas_call x4 -> x3, Pallas kernels: 12.6 us -> 3.08 us  [kernel(): return call(*scalars, *arrays)]
    all_to_all x2, waiting for transfers between devices: 10.2 us -> 18.8 us  [body(): got = lax.all_to_all(sent, 'z', 0, 0, tiled=True)]
    all_to_all x0 -> x1, starting transfers between devices: none -> 7.45 us  [body(): got = lax.all_to_all(sent, ('virt', 'y'), 0, 0, tiled=True)]
    all_to_all x0 -> x1, waiting for transfers between devices: none -> 5.08 us  [body(): got = lax.all_to_all(sent, ('virt', 'y'), 0, 0, tiled=True)]
    all_to_all x2, starting transfers between devices: 16.9 us -> 13.3 us  [body(): got = lax.all_to_all(sent, 'z', 0, 0, tiled=True)]
  transfers between devices with their start and end apart: 4 -> 7, of which waited for: 2 -> 5; matrix products, arithmetic and copies ran while one was open for 0% -> 0% of each run, Pallas kernels for 2% -> 3%
where the time goes in v7:
time: 94.2 us; the launch traced here: 93.1 us
  Pallas kernels  26.7 us (28%)
  waiting for transfers between devices  25.6 us (27%)
  starting transfers between devices  24.6 us (26%)
  blocking collectives  14 us (15%)
  between operations  1.4 us (1%)
    pallas_call x1, Pallas kernels, body(): pl.pallas_call(ladder_kernel, name='ladder_kernel', in_specs=[pl.BlockSpe...  19.5 us
    all_to_all x2, waiting for transfers between devices, body(): got = lax.all_to_all(sent, 'z', 0, 0, tiled=True)  18.8 us
    all_to_all x1, blocking collectives, body(): got = lax.all_to_all(sent, ('virt', 'y'), 0, 0, tiled=True)  14 us
    all_to_all x2, starting transfers between devices, body(): got = lax.all_to_all(sent, 'z', 0, 0, tiled=True)  13.3 us
    all_to_all x1, starting transfers between devices, body(): got = lax.all_to_all(sent, ('virt', 'y'), 0, 0, tiled=True)  7.45 us
    all_to_all x1, waiting for transfers between devices, body(): got = lax.all_to_all(sent, ('virt', 'y'), 0, 0, tiled=True)  5.08 us
    pallas_call x3, Pallas kernels, kernel(): return call(*scalars, *arrays)  3.08 us
    pallas_call x1, Pallas kernels, body(): pl.pallas_call(share_kernel, name='share_kernel', in_specs=[hbm], out_spe...  2.37 us
  transfers between devices with their start and end apart: 7, of which 5 were waited for; matrix products, arithmetic and copies ran while one was open for 0% of the time, Pallas kernels for 3%

profile of v7, /device:TPU:4, one launch (start us, length us, event | category | flops | bytes accessed | tf_op | source)
XLA Modules:
  0.0 93.1 jit_solution(5190305730185080249)
XLA Ops:
  0.0 1.7 %out_kernel.1 = bf16[8,80,256]{2,1,0:T(8,128)(2,1)} custom-call(s32[1,1,2]{2,1,0:T(1,128)} %domain_ref.1, bf16[1,1,64,256]{3,2,1,0:T(8,128)(2,1)} %amp_hbm.1, bf16[512,256]{1,0:T(8,128)(2,1)} %bitcast.2), custom_call_target="tpu_custom_call" | custom-call | tf_op jit(solution)/shard_map/out_kernel/pallas_call | solution.py:189
  1.7 8.5 %all-to-all-start = ((bf16[8,80,256]{2,1,0:T(8,128)(2,1)}), bf16[8,80,256]{2,1,0:T(8,128)(2,1)S(1)}, u32[]{:S(2)}, u32[]{:S(2)}) async-start(bf16[8,80,256]{2,1,0:T(8,128)(2,1)} %out_kernel.1), calls=%async_computation | async-start | bytes 655360 | tf_op jit(solution)/shard_map/all_to_all | solution.py:209
  10.2 0.0 copy-start
  10.2 0.0 copy-start.3
  10.2 2.4 %share_kernel.1 = (bf16[4,256,256]{2,1,0:T(8,128)(2,1)}, bf16[4,256,256]{2,1,0:T(8,128)(2,1)}) custom-call(bf16[16,256,256]{2,1,0:T(8,128)(2,1)} %own_hbm.1), custom_call_target="tpu_custom_call" | custom-call | tf_op jit(solution)/shard_map/share_kernel/pallas_call | solution.py:201
  12.6 1.7 %collective-permute-start = (bf16[4,256,256]{2,1,0:T(8,128)(2,1)}, bf16[4,256,256]{2,1,0:T(8,128)(2,1)S(1)}, u32[]{:S(2)}, u32[]{:S(2)}) collective-permute-start(bf16[4,256,256]{2,1,0:T(8,128)(2,1)} %get-tuple-element.7), channel_id=1, source_target_pairs={{0,8},{8,16},{16,24},{24,0},{1,9},{9,17},{17,25},{25,1},{2,10},{10... | collective-permute-start | bytes 1572872 | tf_op jit(solution)/shard_map/ppermute | solution.py:212
  14.3 1.7 %collective-permute-start.1 = (bf16[4,256,256]{2,1,0:T(8,128)(2,1)}, bf16[4,256,256]{2,1,0:T(8,128)(2,1)}, u32[]{:S(2)}, u32[]{:S(2)}) collective-permute-start(bf16[4,256,256]{2,1,0:T(8,128)(2,1)} %get-tuple-element.8), channel_id=1, source_target_pairs={{0,24},{8,0},{16,8},{24,16},{1,25},{9,1},{17,9},{25,17},{2,26},{10... | collective-permute-start | bytes 1572872 | tf_op jit(solution)/shard_map/ppermute | solution.py:213
  15.9 7.6 %all-to-all-done.got_ref = bf16[8,80,256]{2,1,0:T(8,128)(2,1)S(1)} async-done(((bf16[8,80,256]{2,1,0:T(8,128)(2,1)}), bf16[8,80,256]{2,1,0:T(8,128)(2,1)S(1)}, u32[]{:S(2)}, u32[]{:S(2)}) %all-to-all-start) | async-done | bytes 327712 | tf_op jit(solution)/shard_map/all_to_all | solution.py:209
  23.5 0.9 spread_kernel.1
  24.4 7.5 %all-to-all-start.1 = ((bf16[16,72,256]{2,1,0:T(8,128)(2,1)}), bf16[16,72,256]{2,1,0:T(8,128)(2,1)S(1)}, u32[]{:S(2)}, u32[]{:S(2)}) async-start(bf16[16,72,256]{2,1,0:T(8,128)(2,1)} %spread_kernel.1), calls=%async_computation.1 | async-start | bytes 1179648 | tf_op jit(solution)/shard_map/all_to_all | solution.py:215
  31.8 0.0 collective-permute-done.up_hbm
  31.8 0.0 copy-start.5
  31.8 0.1 collective-permute-start.2
  31.9 0.0 collective-permute-done.1.down_hbm
  31.9 0.5 collective-permute-start.3
  32.4 1.4 %collective-permute-done.2.up2_hbm = bf16[4,256,256]{2,1,0:T(8,128)(2,1)S(1)} collective-permute-done((bf16[4,256,256]{2,1,0:T(8,128)(2,1)S(1)}, bf16[4,256,256]{2,1,0:T(8,128)(2,1)S(1)}, u32[]{:S(2)}, u32[]{:S(2)}) %collective-permute-start.2) | collective-permute-done | bytes 524320 | tf_op jit(solution)/shard_map/ppermute | solution.py:214
  33.8 0.0 copy-start.6
  33.8 0.8 copy-done.6
  34.6 0.3 collective-permute-done.3.down2_hbm
  34.9 5.1 %all-to-all-done.1.rows_ref = bf16[16,72,256]{2,1,0:T(8,128)(2,1)S(1)} async-done(((bf16[16,72,256]{2,1,0:T(8,128)(2,1)}), bf16[16,72,256]{2,1,0:T(8,128)(2,1)S(1)}, u32[]{:S(2)}, u32[]{:S(2)}) %all-to-all-start.1) | async-done | bytes 589856 | tf_op jit(solution)/shard_map/all_to_all | solution.py:215
  40.0 0.0 copy-done.5
  40.0 0.0 copy-done
  40.0 0.0 copy-done.3
  40.0 19.5 %ladder_kernel.1 = bf16[16,72,256]{2,1,0:T(8,128)(2,1)S(1)} custom-call(s32[2,2]{1,0:T(2,128)S(1)} %copy-done.3, bf16[16,72,256]{2,1,0:T(8,128)(2,1)S(1)} %all-to-all-done.1.rows_ref, bf16[16,256,256]{2,1,0:T(8,128)(2,1)S(1)} %copy-done, bf16[4,256,256]{2,1,0:T(8,128)(2,1)} %copy-done.5, bf16[4,256,256]{2,1,0:T(8,128)(2,1)} %collective-permute-done.1.down_hbm, ...), custom_call_target="tpu_custom_call" | custom-call | tf_op jit(solution)/shard_map/ladder_kernel/pallas_call | solution.py:217
  59.5 0.0 copy-start.1
  59.5 0.0 copy-start.2
  59.5 0.0 copy-start.4
  59.5 14.0 %all_to_all.20.got_ref = bf16[16,72,256]{2,1,0:T(8,128)(2,1)S(1)} all-to-all(bf16[16,72,256]{2,1,0:T(8,128)(2,1)S(1)} %ladder_kernel.1), channel_id=1, replica_groups=mesh['pair'=2,'virt'=4,'y'=4,'z'=8] {'virt','y'}, dimensions={0} | all-to-all | bytes 1179648 | tf_op jit(solution)/shard_map/all_to_all | solution.py:231
  73.5 0.8 sum_kernel.1
  74.3 4.8 %all-to-all-start.3 = ((bf16[8,80,256]{2,1,0:T(8,128)(2,1)}), bf16[8,80,256]{2,1,0:T(8,128)(2,1)S(1)}, u32[]{:S(2)}, u32[]{:S(2)}) async-start(bf16[8,80,256]{2,1,0:T(8,128)(2,1)} %sum_kernel.1), calls=%async_computation.3 | async-start | bytes 655360 | tf_op jit(solution)/shard_map/all_to_all | solution.py:233
  80.5 11.2 %all-to-all-done.3.got_ref = bf16[8,80,256]{2,1,0:T(8,128)(2,1)S(1)} async-done(((bf16[8,80,256]{2,1,0:T(8,128)(2,1)}), bf16[8,80,256]{2,1,0:T(8,128)(2,1)S(1)}, u32[]{:S(2)}, u32[]{:S(2)}) %all-to-all-start.3) | async-done | bytes 327712 | tf_op jit(solution)/shard_map/all_to_all | solution.py:233
  91.7 0.0 copy-done.1
  91.7 0.0 copy-done.2
  91.7 0.0 copy-done.4
  91.7 1.4 %update_kernel.1 = bf16[1,1,64,256]{3,2,1,0:T(8,128)(2,1)} custom-call(s32[1,1,2]{2,1,0:T(1,128)S(1)} %copy-done.2, f32[1]{0:T(128)S(6)} %copy.9.occ_i_ref, f32[1]{0:T(128)S(6)} %copy.10.occ_j_ref, f32[1,256]{1,0:T(1,128)S(1)} %bitcast.4, bf16[8,80,256]{2,1,0:T(8,128)(2,1)S(1)} %all-to-all-done.3.got_ref, bf16[512,256]{1,0:T(8,128)(2,1)S(1)} %bitcast.3), custom_call_target="tpu_custom_call" | custom-call | tf_op jit(solution)/shard_map/update_kernel/pallas_call | solution.py:174
Async XLA Ops:
  1.7 21.8 %all-to-all-start = ((bf16[8,80,256]{2,1,0:T(8,128)(2,1)}), bf16[8,80,256]{2,1,0:T(8,128)(2,1)S(1)}, u32[]{:S(2)}, u32[]{:S(2)}) async-start(bf16[8,80,256]{2,1,0:T(8,128)(2,1)} %out_kernel.1), calls=%async_computation | async-start | bytes 655360 | tf_op jit(solution)/shard_map/all_to_all | solution.py:209
  10.2 29.8 %copy-start = (bf16[16,256,256]{2,1,0:T(8,128)(2,1)S(1)}, bf16[16,256,256]{2,1,0:T(8,128)(2,1)}, u32[]{:S(2)}) copy-start(bf16[16,256,256]{2,1,0:T(8,128)(2,1)} %own_hbm.1) | copy-start | bytes 6291460
  10.2 29.8 %copy-start.3 = (s32[2,2]{1,0:T(2,128)S(1)}, s32[2,2]{1,0:T(2,128)}, u32[]{:S(2)}) copy-start(s32[2,2]{1,0:T(2,128)} %mask_ref.1) | copy-start | bytes 52
  12.6 19.2 %collective-permute-start = (bf16[4,256,256]{2,1,0:T(8,128)(2,1)}, bf16[4,256,256]{2,1,0:T(8,128)(2,1)S(1)}, u32[]{:S(2)}, u32[]{:S(2)}) collective-permute-start(bf16[4,256,256]{2,1,0:T(8,128)(2,1)} %get-tuple-element.7), channel_id=1, source_target_pairs={{0,8},{8,16},{16,24},{24,0},{1,9},{9,17},{17,25},{25,1},{2,10},{10... | collective-permute-start | bytes 1572872 | tf_op jit(solution)/shard_map/ppermute | solution.py:212
  14.3 17.7 %collective-permute-start.1 = (bf16[4,256,256]{2,1,0:T(8,128)(2,1)}, bf16[4,256,256]{2,1,0:T(8,128)(2,1)}, u32[]{:S(2)}, u32[]{:S(2)}) collective-permute-start(bf16[4,256,256]{2,1,0:T(8,128)(2,1)} %get-tuple-element.8), channel_id=1, source_target_pairs={{0,24},{8,0},{16,8},{24,16},{1,25},{9,1},{17,9},{25,17},{2,26},{10... | collective-permute-start | bytes 1572872 | tf_op jit(solution)/shard_map/ppermute | solution.py:213
  24.4 15.6 %all-to-all-start.1 = ((bf16[16,72,256]{2,1,0:T(8,128)(2,1)}), bf16[16,72,256]{2,1,0:T(8,128)(2,1)S(1)}, u32[]{:S(2)}, u32[]{:S(2)}) async-start(bf16[16,72,256]{2,1,0:T(8,128)(2,1)} %spread_kernel.1), calls=%async_computation.1 | async-start | bytes 1179648 | tf_op jit(solution)/shard_map/all_to_all | solution.py:215
  31.8 8.2 %copy-start.5 = (bf16[4,256,256]{2,1,0:T(8,128)(2,1)}, bf16[4,256,256]{2,1,0:T(8,128)(2,1)S(1)}, u32[]{:S(2)}) copy-start(bf16[4,256,256]{2,1,0:T(8,128)(2,1)S(1)} %collective-permute-done.up_hbm) | copy-start | bytes 1572868
  31.8 2.0 %collective-permute-start.2 = (bf16[4,256,256]{2,1,0:T(8,128)(2,1)S(1)}, bf16[4,256,256]{2,1,0:T(8,128)(2,1)S(1)}, u32[]{:S(2)}, u32[]{:S(2)}) collective-permute-start(bf16[4,256,256]{2,1,0:T(8,128)(2,1)S(1)} %collective-permute-done.up_hbm), channel_id=1, source_target_pairs={{0,128},{128,0},{1,129},{129,1},{2,130},{130,2},{3,131},{131,3},{4... | collective-permute-start | bytes 1572872 | tf_op jit(solution)/shard_map/ppermute | solution.py:214
  31.9 3.0 %collective-permute-start.3 = (bf16[4,256,256]{2,1,0:T(8,128)(2,1)}, bf16[4,256,256]{2,1,0:T(8,128)(2,1)}, u32[]{:S(2)}, u32[]{:S(2)}) collective-permute-start(bf16[4,256,256]{2,1,0:T(8,128)(2,1)} %collective-permute-done.1.down_hbm), channel_id=1, source_target_pairs={{0,128},{128,0},{1,129},{129,1},{2,130},{130,2},{3,131},{131,3},{4... | collective-permute-start | bytes 1572872 | tf_op jit(solution)/shard_map/ppermute | solution.py:214
  33.8 0.8 copy-start.6
  59.5 32.2 %copy-start.1 = (bf16[512,1,256]{2,0,1:T(8,128)(2,1)S(1)}, bf16[512,1,256]{2,0,1:T(8,128)(2,1)}, u32[]{:S(2)}) copy-start(bf16[512,1,256]{2,0,1:T(8,128)(2,1)} %param.10) | copy-start | bytes 786436
  59.5 32.2 %copy-start.2 = (s32[1,1,2]{2,1,0:T(1,128)S(1)}, s32[1,1,2]{2,1,0:T(1,128)}, u32[]{:S(2)}) copy-start(s32[1,1,2]{2,1,0:T(1,128)} %domain_ref.1) | copy-start | bytes 28
  59.5 32.2 %copy-start.4 = (f32[256]{0:T(256)S(1)}, f32[256]{0:T(256)}, u32[]{:S(2)}) copy-start(f32[256]{0:T(256)} %param.13) | copy-start | bytes 3076
  74.3 17.4 %all-to-all-start.3 = ((bf16[8,80,256]{2,1,0:T(8,128)(2,1)}), bf16[8,80,256]{2,1,0:T(8,128)(2,1)S(1)}, u32[]{:S(2)}, u32[]{:S(2)}) async-start(bf16[8,80,256]{2,1,0:T(8,128)(2,1)} %sum_kernel.1), calls=%async_computation.3 | async-start | bytes 655360 | tf_op jit(solution)/shard_map/all_to_all | solution.py:233

commit v8 on v7

--- a/solution.py
+++ b/solution.py
@@ -67,16 +67,31 @@
 
 
 def ladder_kernel(
-    mask_ref, rows_ref, own_hbm, up_hbm, down_hbm, up2_hbm, down2_hbm, out_ref, factors, masked, weighted, sems
+    mask_ref, rows_ref, own_ref, up_hbm, down_hbm, up2_hbm, down2_hbm, out_ref, factors, masked, weighted, sems
 ):
-    sources = [(own_hbm, aux) for aux in range(AUX)]
-    sources += [(ref, aux) for ref in (up_hbm, down_hbm, up2_hbm, down2_hbm) for aux in range(SHARE)]
     copies = [
-        pltpu.make_async_copy(ref.at[aux], factors.at[slot], sems.at[slot]) for slot, (ref, aux) in enumerate(sources)
+        pltpu.make_async_copy(ref, factors.at[part], sems.at[part])
+        for part, ref in enumerate((up_hbm, down_hbm, up2_hbm, down2_hbm))
     ]
     for copy in copies:
         copy.start()
-    keep = [[jnp.full((1, TILE_SIZE), mask_ref[p, q], jnp.int32).astype(F32).astype(BF16) for q in range(2)] for p in range(2)]
+
+    def mask(slot, matrix):
+        for p in range(2):
+            for q in range(2):
+                keep = jnp.full((1, TILE_SIZE), mask_ref[p, q], jnp.int32).astype(F32).astype(BF16)
+                rows = slice(p * TILE_SIZE, (p + 1) * TILE_SIZE)
+                left = slot * COLS + q * TILE_SIZE
+                block = matrix[rows, q * TILE_SIZE : (q + 1) * TILE_SIZE]
+                masked[rows, left : left + TILE_SIZE] = block * keep
+
+    for aux in range(AUX):
+        mask(aux, own_ref.at[aux])
+    for part, copy in enumerate(copies):
+        copy.wait()
+        for aux in range(SHARE):
+            mask(AUX + part * SHARE + aux, factors.at[part, aux])
+
     zeta = jnp.zeros((2 * AUX, COLS), F32)
     for at_y in range(Y):
         amp = jnp.concatenate([rows_ref[at_x * Y + at_y, :ROWS] for at_x in range(VIRT)], axis=0)
@@ -86,14 +101,6 @@
         zeta = zeta + (2.0 * direct - swapped)
         for slot in range(2 * AUX):
             cols = slice(slot * COLS, (slot + 1) * COLS)
-            if at_y == 0:
-                copies[slot].wait()
-                for p in range(2):
-                    for q in range(2):
-                        rows = slice(p * TILE_SIZE, (p + 1) * TILE_SIZE)
-                        lanes = slice(q * TILE_SIZE, (q + 1) * TILE_SIZE)
-                        left = slot * COLS + q * TILE_SIZE
-                        masked[rows, left : left + TILE_SIZE] = factors[slot, rows, lanes] * keep[p][q]
             weighted[:, cols] = jnp.dot(masked[:, cols], amp, preferred_element_type=F32).astype(BF16)
         total = lax.dot_general(weighted[...], masked[...], NT, preferred_element_type=F32).astype(BF16)
         for at_x in range(VIRT):
@@ -217,14 +224,14 @@
     sent = pl.pallas_call(
         ladder_kernel,
         name="ladder_kernel",
-        in_specs=[pl.BlockSpec(memory_space=pltpu.SMEM), pl.BlockSpec(memory_space=pltpu.VMEM)] + [hbm] * 5,
+        in_specs=[pl.BlockSpec(memory_space=pltpu.SMEM)] + [pl.BlockSpec(memory_space=pltpu.VMEM)] * 2 + [hbm] * 4,
         out_specs=pl.BlockSpec(memory_space=pltpu.VMEM),
         out_shape=jax.ShapeDtypeStruct((VIRT * Y, ROWS + PART, COLS), BF16),
         scratch_shapes=[
-            pltpu.VMEM((2 * AUX, COLS, COLS), BF16),
+            pltpu.VMEM((4, SHARE, COLS, COLS), BF16),
             wide,
             wide,
-            pltpu.SemaphoreType.DMA((2 * AUX,)),
+            pltpu.SemaphoreType.DMA((4,)),
         ],
         compiler_params=pltpu.CompilerParams(vmem_limit_bytes=40 << 20),
     )(vv_mask, got, vv_factors, *[pltpu.with_memory_space_constraint(part, pltpu.HBM) for part in extra])

time: 94.2 us -> 86 us (0.913)
  Pallas kernels: 26.7 us -> 18.4 us
    pallas_call x1, Pallas kernels: 19.5 us -> 11.3 us  [body(): pl.pallas_call(ladder_kernel, name='ladder_kernel', in_specs=[pl.BlockSpe...]
  transfers between devices with their start and end apart: 7 -> 7, of which waited for: 5 -> 5; matrix products, arithmetic and copies ran while one was open for 0% -> 0% of each run, Pallas kernels for 3% -> 4%
where the time goes in v8:
time: 86 us; the launch traced here: 84.9 us
  waiting for transfers between devices  25.6 us (30%)
  starting transfers between devices  24.7 us (29%)
  Pallas kernels  18.4 us (21%)
  blocking collectives  14 us (16%)
  between operations  1.4 us (2%)
    all_to_all x2, waiting for transfers between devices, body(): got = lax.all_to_all(sent, 'z', 0, 0, tiled=True)  18.8 us
    all_to_all x1, blocking collectives, body(): got = lax.all_to_all(sent, ('virt', 'y'), 0, 0, tiled=True)  14 us
    all_to_all x2, starting transfers between devices, body(): got = lax.all_to_all(sent, 'z', 0, 0, tiled=True)  13.3 us
    pallas_call x1, Pallas kernels, body(): pl.pallas_call(ladder_kernel, name='ladder_kernel', in_specs=[pl.BlockSpe...  11.3 us
    all_to_all x1, starting transfers between devices, body(): got = lax.all_to_all(sent, ('virt', 'y'), 0, 0, tiled=True)  7.45 us
    all_to_all x1, waiting for transfers between devices, body(): got = lax.all_to_all(sent, ('virt', 'y'), 0, 0, tiled=True)  5.08 us
    pallas_call x3, Pallas kernels, kernel(): return call(*scalars, *arrays)  3.08 us
    pallas_call x1, Pallas kernels, body(): pl.pallas_call(share_kernel, name='share_kernel', in_specs=[hbm], out_spe...  2.37 us
  transfers between devices with their start and end apart: 7, of which 5 were waited for; matrix products, arithmetic and copies ran while one was open for 0% of the time, Pallas kernels for 4%

profile of v8, /device:TPU:4, one launch (start us, length us, event | category | flops | bytes accessed | tf_op | source)
XLA Modules:
  0.0 84.9 jit_solution(6676466341006561506)
XLA Ops:
  0.0 1.7 %out_kernel.1 = bf16[8,80,256]{2,1,0:T(8,128)(2,1)} custom-call(s32[1,1,2]{2,1,0:T(1,128)} %domain_ref.1, bf16[1,1,64,256]{3,2,1,0:T(8,128)(2,1)} %amp_hbm.1, bf16[512,256]{1,0:T(8,128)(2,1)} %bitcast.2), custom_call_target="tpu_custom_call" | custom-call | tf_op jit(solution)/shard_map/out_kernel/pallas_call | solution.py:196
  1.7 8.5 %all-to-all-start = ((bf16[8,80,256]{2,1,0:T(8,128)(2,1)}), bf16[8,80,256]{2,1,0:T(8,128)(2,1)S(1)}, u32[]{:S(2)}, u32[]{:S(2)}) async-start(bf16[8,80,256]{2,1,0:T(8,128)(2,1)} %out_kernel.1), calls=%async_computation | async-start | bytes 655360 | tf_op jit(solution)/shard_map/all_to_all | solution.py:216
  10.2 0.0 copy-start
  10.2 0.0 copy-start.3
  10.2 2.4 %share_kernel.1 = (bf16[4,256,256]{2,1,0:T(8,128)(2,1)}, bf16[4,256,256]{2,1,0:T(8,128)(2,1)}) custom-call(bf16[16,256,256]{2,1,0:T(8,128)(2,1)} %own_ref.1), custom_call_target="tpu_custom_call" | custom-call | tf_op jit(solution)/shard_map/share_kernel/pallas_call | solution.py:208
  12.6 1.7 %collective-permute-start = (bf16[4,256,256]{2,1,0:T(8,128)(2,1)}, bf16[4,256,256]{2,1,0:T(8,128)(2,1)S(1)}, u32[]{:S(2)}, u32[]{:S(2)}) collective-permute-start(bf16[4,256,256]{2,1,0:T(8,128)(2,1)} %get-tuple-element.7), channel_id=1, source_target_pairs={{0,8},{8,16},{16,24},{24,0},{1,9},{9,17},{17,25},{25,1},{2,10},{10... | collective-permute-start | bytes 1572872 | tf_op jit(solution)/shard_map/ppermute | solution.py:219
  14.3 1.7 %collective-permute-start.1 = (bf16[4,256,256]{2,1,0:T(8,128)(2,1)}, bf16[4,256,256]{2,1,0:T(8,128)(2,1)}, u32[]{:S(2)}, u32[]{:S(2)}) collective-permute-start(bf16[4,256,256]{2,1,0:T(8,128)(2,1)} %get-tuple-element.8), channel_id=1, source_target_pairs={{0,24},{8,0},{16,8},{24,16},{1,25},{9,1},{17,9},{25,17},{2,26},{10... | collective-permute-start | bytes 1572872 | tf_op jit(solution)/shard_map/ppermute | solution.py:220
  15.9 7.6 %all-to-all-done.got_ref = bf16[8,80,256]{2,1,0:T(8,128)(2,1)S(1)} async-done(((bf16[8,80,256]{2,1,0:T(8,128)(2,1)}), bf16[8,80,256]{2,1,0:T(8,128)(2,1)S(1)}, u32[]{:S(2)}, u32[]{:S(2)}) %all-to-all-start) | async-done | bytes 327712 | tf_op jit(solution)/shard_map/all_to_all | solution.py:216
  23.5 0.9 %spread_kernel.1 = bf16[16,72,256]{2,1,0:T(8,128)(2,1)} custom-call(bf16[8,80,256]{2,1,0:T(8,128)(2,1)S(1)} %all-to-all-done.got_ref), custom_call_target="tpu_custom_call" | custom-call | tf_op jit(solution)/shard_map/spread_kernel/pallas_call | solution.py:181
  24.4 7.5 %all-to-all-start.1 = ((bf16[16,72,256]{2,1,0:T(8,128)(2,1)}), bf16[16,72,256]{2,1,0:T(8,128)(2,1)S(1)}, u32[]{:S(2)}, u32[]{:S(2)}) async-start(bf16[16,72,256]{2,1,0:T(8,128)(2,1)} %spread_kernel.1), calls=%async_computation.1 | async-start | bytes 1179648 | tf_op jit(solution)/shard_map/all_to_all | solution.py:222
  31.8 0.0 collective-permute-done.up_hbm
  31.8 0.0 copy-start.5
  31.8 0.1 collective-permute-start.2
  31.9 0.0 collective-permute-done.1.down_hbm
  31.9 0.5 collective-permute-start.3
  32.4 1.4 %collective-permute-done.2.up2_hbm = bf16[4,256,256]{2,1,0:T(8,128)(2,1)S(1)} collective-permute-done((bf16[4,256,256]{2,1,0:T(8,128)(2,1)S(1)}, bf16[4,256,256]{2,1,0:T(8,128)(2,1)S(1)}, u32[]{:S(2)}, u32[]{:S(2)}) %collective-permute-start.2) | collective-permute-done | bytes 524320 | tf_op jit(solution)/shard_map/ppermute | solution.py:221
  33.8 0.0 copy-start.6
  33.8 0.8 copy-done.6
  34.6 0.3 collective-permute-done.3.down2_hbm
  34.9 5.1 %all-to-all-done.1.rows_ref = bf16[16,72,256]{2,1,0:T(8,128)(2,1)S(1)} async-done(((bf16[16,72,256]{2,1,0:T(8,128)(2,1)}), bf16[16,72,256]{2,1,0:T(8,128)(2,1)S(1)}, u32[]{:S(2)}, u32[]{:S(2)}) %all-to-all-start.1) | async-done | bytes 589856 | tf_op jit(solution)/shard_map/all_to_all | solution.py:222
  40.0 0.0 copy-done.5
  40.0 0.0 copy-done
  40.0 0.0 copy-done.3
  40.0 11.3 %ladder_kernel.1 = bf16[16,72,256]{2,1,0:T(8,128)(2,1)S(1)} custom-call(s32[2,2]{1,0:T(2,128)S(1)} %copy-done.3, bf16[16,72,256]{2,1,0:T(8,128)(2,1)S(1)} %all-to-all-done.1.rows_ref, bf16[16,256,256]{2,1,0:T(8,128)(2,1)S(1)} %copy-done, bf16[4,256,256]{2,1,0:T(8,128)(2,1)} %copy-done.5, bf16[4,256,256]{2,1,0:T(8,128)(2,1)} %collective-permute-done.1.down_hbm, ...), custom_call_target="tpu_custom_call" | custom-call | tf_op jit(solution)/shard_map/ladder_kernel/pallas_call | solution.py:224
  51.3 0.0 copy-start.1
  51.3 0.0 copy-start.2
  51.3 0.0 copy-start.4
  51.3 14.0 %all_to_all.20.got_ref = bf16[16,72,256]{2,1,0:T(8,128)(2,1)S(1)} all-to-all(bf16[16,72,256]{2,1,0:T(8,128)(2,1)S(1)} %ladder_kernel.1), channel_id=1, replica_groups=mesh['pair'=2,'virt'=4,'y'=4,'z'=8] {'virt','y'}, dimensions={0} | all-to-all | bytes 1179648 | tf_op jit(solution)/shard_map/all_to_all | solution.py:238
  65.3 0.8 sum_kernel.1
  66.1 4.8 %all-to-all-start.3 = ((bf16[8,80,256]{2,1,0:T(8,128)(2,1)}), bf16[8,80,256]{2,1,0:T(8,128)(2,1)S(1)}, u32[]{:S(2)}, u32[]{:S(2)}) async-start(bf16[8,80,256]{2,1,0:T(8,128)(2,1)} %sum_kernel.1), calls=%async_computation.3 | async-start | bytes 655360 | tf_op jit(solution)/shard_map/all_to_all | solution.py:240
  72.2 11.2 %all-to-all-done.3.got_ref = bf16[8,80,256]{2,1,0:T(8,128)(2,1)S(1)} async-done(((bf16[8,80,256]{2,1,0:T(8,128)(2,1)}), bf16[8,80,256]{2,1,0:T(8,128)(2,1)S(1)}, u32[]{:S(2)}, u32[]{:S(2)}) %all-to-all-start.3) | async-done | bytes 327712 | tf_op jit(solution)/shard_map/all_to_all | solution.py:240
  83.5 0.0 copy-done.1
  83.5 0.0 copy-done.2
  83.5 0.0 copy-done.4
  83.5 1.4 %update_kernel.1 = bf16[1,1,64,256]{3,2,1,0:T(8,128)(2,1)} custom-call(s32[1,1,2]{2,1,0:T(1,128)S(1)} %copy-done.2, f32[1]{0:T(128)S(6)} %copy.9.occ_i_ref, f32[1]{0:T(128)S(6)} %copy.10.occ_j_ref, f32[1,256]{1,0:T(1,128)S(1)} %bitcast.4, bf16[8,80,256]{2,1,0:T(8,128)(2,1)S(1)} %all-to-all-done.3.got_ref, bf16[512,256]{1,0:T(8,128)(2,1)S(1)} %bitcast.3), custom_call_target="tpu_custom_call" | custom-call | tf_op jit(solution)/shard_map/update_kernel/pallas_call | solution.py:181
Async XLA Ops:
  1.7 21.8 %all-to-all-start = ((bf16[8,80,256]{2,1,0:T(8,128)(2,1)}), bf16[8,80,256]{2,1,0:T(8,128)(2,1)S(1)}, u32[]{:S(2)}, u32[]{:S(2)}) async-start(bf16[8,80,256]{2,1,0:T(8,128)(2,1)} %out_kernel.1), calls=%async_computation | async-start | bytes 655360 | tf_op jit(solution)/shard_map/all_to_all | solution.py:216
  10.2 29.8 %copy-start = (bf16[16,256,256]{2,1,0:T(8,128)(2,1)S(1)}, bf16[16,256,256]{2,1,0:T(8,128)(2,1)}, u32[]{:S(2)}) copy-start(bf16[16,256,256]{2,1,0:T(8,128)(2,1)} %own_ref.1) | copy-start | bytes 6291460
  10.2 29.8 %copy-start.3 = (s32[2,2]{1,0:T(2,128)S(1)}, s32[2,2]{1,0:T(2,128)}, u32[]{:S(2)}) copy-start(s32[2,2]{1,0:T(2,128)} %mask_ref.1) | copy-start | bytes 52
  12.6 19.2 %collective-permute-start = (bf16[4,256,256]{2,1,0:T(8,128)(2,1)}, bf16[4,256,256]{2,1,0:T(8,128)(2,1)S(1)}, u32[]{:S(2)}, u32[]{:S(2)}) collective-permute-start(bf16[4,256,256]{2,1,0:T(8,128)(2,1)} %get-tuple-element.7), channel_id=1, source_target_pairs={{0,8},{8,16},{16,24},{24,0},{1,9},{9,17},{17,25},{25,1},{2,10},{10... | collective-permute-start | bytes 1572872 | tf_op jit(solution)/shard_map/ppermute | solution.py:219
  14.3 17.7 %collective-permute-start.1 = (bf16[4,256,256]{2,1,0:T(8,128)(2,1)}, bf16[4,256,256]{2,1,0:T(8,128)(2,1)}, u32[]{:S(2)}, u32[]{:S(2)}) collective-permute-start(bf16[4,256,256]{2,1,0:T(8,128)(2,1)} %get-tuple-element.8), channel_id=1, source_target_pairs={{0,24},{8,0},{16,8},{24,16},{1,25},{9,1},{17,9},{25,17},{2,26},{10... | collective-permute-start | bytes 1572872 | tf_op jit(solution)/shard_map/ppermute | solution.py:220
  24.4 15.6 %all-to-all-start.1 = ((bf16[16,72,256]{2,1,0:T(8,128)(2,1)}), bf16[16,72,256]{2,1,0:T(8,128)(2,1)S(1)}, u32[]{:S(2)}, u32[]{:S(2)}) async-start(bf16[16,72,256]{2,1,0:T(8,128)(2,1)} %spread_kernel.1), calls=%async_computation.1 | async-start | bytes 1179648 | tf_op jit(solution)/shard_map/all_to_all | solution.py:222
  31.8 8.2 %copy-start.5 = (bf16[4,256,256]{2,1,0:T(8,128)(2,1)}, bf16[4,256,256]{2,1,0:T(8,128)(2,1)S(1)}, u32[]{:S(2)}) copy-start(bf16[4,256,256]{2,1,0:T(8,128)(2,1)S(1)} %collective-permute-done.up_hbm) | copy-start | bytes 1572868
  31.8 2.0 %collective-permute-start.2 = (bf16[4,256,256]{2,1,0:T(8,128)(2,1)S(1)}, bf16[4,256,256]{2,1,0:T(8,128)(2,1)S(1)}, u32[]{:S(2)}, u32[]{:S(2)}) collective-permute-start(bf16[4,256,256]{2,1,0:T(8,128)(2,1)S(1)} %collective-permute-done.up_hbm), channel_id=1, source_target_pairs={{0,128},{128,0},{1,129},{129,1},{2,130},{130,2},{3,131},{131,3},{4... | collective-permute-start | bytes 1572872 | tf_op jit(solution)/shard_map/ppermute | solution.py:221
  31.9 3.0 %collective-permute-start.3 = (bf16[4,256,256]{2,1,0:T(8,128)(2,1)}, bf16[4,256,256]{2,1,0:T(8,128)(2,1)}, u32[]{:S(2)}, u32[]{:S(2)}) collective-permute-start(bf16[4,256,256]{2,1,0:T(8,128)(2,1)} %collective-permute-done.1.down_hbm), channel_id=1, source_target_pairs={{0,128},{128,0},{1,129},{129,1},{2,130},{130,2},{3,131},{131,3},{4... | collective-permute-start | bytes 1572872 | tf_op jit(solution)/shard_map/ppermute | solution.py:221
  33.8 0.8 copy-start.6
  51.3 32.2 %copy-start.1 = (bf16[512,1,256]{2,0,1:T(8,128)(2,1)S(1)}, bf16[512,1,256]{2,0,1:T(8,128)(2,1)}, u32[]{:S(2)}) copy-start(bf16[512,1,256]{2,0,1:T(8,128)(2,1)} %param.10) | copy-start | bytes 786436
  51.3 32.2 %copy-start.2 = (s32[1,1,2]{2,1,0:T(1,128)S(1)}, s32[1,1,2]{2,1,0:T(1,128)}, u32[]{:S(2)}) copy-start(s32[1,1,2]{2,1,0:T(1,128)} %domain_ref.1) | copy-start | bytes 28
  51.3 32.2 %copy-start.4 = (f32[256]{0:T(256)S(1)}, f32[256]{0:T(256)}, u32[]{:S(2)}) copy-start(f32[256]{0:T(256)} %param.13) | copy-start | bytes 3076
  66.1 17.4 %all-to-all-start.3 = ((bf16[8,80,256]{2,1,0:T(8,128)(2,1)}), bf16[8,80,256]{2,1,0:T(8,128)(2,1)S(1)}, u32[]{:S(2)}, u32[]{:S(2)}) async-start(bf16[8,80,256]{2,1,0:T(8,128)(2,1)} %sum_kernel.1), calls=%async_computation.3 | async-start | bytes 655360 | tf_op jit(solution)/shard_map/all_to_all | solution.py:240

commit v9 on v7

--- a/solution.py
+++ b/solution.py
@@ -66,17 +66,23 @@
             out_ref[to_x * Y + to_y, ROWS:] = got_ref[2 * to_x + low, start : start + PART]
 
 
-def ladder_kernel(
-    mask_ref, rows_ref, own_hbm, up_hbm, down_hbm, up2_hbm, down2_hbm, out_ref, factors, masked, weighted, sems
-):
-    sources = [(own_hbm, aux) for aux in range(AUX)]
-    sources += [(ref, aux) for ref in (up_hbm, down_hbm, up2_hbm, down2_hbm) for aux in range(SHARE)]
-    copies = [
-        pltpu.make_async_copy(ref.at[aux], factors.at[slot], sems.at[slot]) for slot, (ref, aux) in enumerate(sources)
-    ]
-    for copy in copies:
-        copy.start()
-    keep = [[jnp.full((1, TILE_SIZE), mask_ref[p, q], jnp.int32).astype(F32).astype(BF16) for q in range(2)] for p in range(2)]
+def mask_kernel(mask_ref, *refs):
+    out_ref = refs[-1]
+    sources = [(ref, aux) for ref in refs[:-1] for aux in range(ref.shape[0])]
+    for p in range(2):
+        rows = slice(p * TILE_SIZE, (p + 1) * TILE_SIZE)
+        for q in range(2):
+            keep = jnp.full((1, TILE_SIZE), mask_ref[p, q], jnp.int32).astype(F32).astype(BF16)
+            for slot, (ref, aux) in enumerate(sources):
+                left = slot * COLS + q * TILE_SIZE
+                block = ref[aux, rows, q * TILE_SIZE : (q + 1) * TILE_SIZE]
+                out_ref[rows, left : left + TILE_SIZE] = block * keep
+
+
+def ladder_kernel(mask_ref, rows_ref, own_ref, extra_hbm, out_ref, own, extra, weighted, sem):
+    copy = pltpu.make_async_copy(extra_hbm, extra, sem)
+    copy.start()
+    mask_kernel(mask_ref, own_ref, own)
     zeta = jnp.zeros((2 * AUX, COLS), F32)
     for at_y in range(Y):
         amp = jnp.concatenate([rows_ref[at_x * Y + at_y, :ROWS] for at_x in range(VIRT)], axis=0)
@@ -84,18 +90,16 @@
         direct = lax.dot_general(fac, amp, NT, preferred_element_type=F32)
         swapped = jnp.dot(fac, amp, preferred_element_type=F32)
         zeta = zeta + (2.0 * direct - swapped)
-        for slot in range(2 * AUX):
-            cols = slice(slot * COLS, (slot + 1) * COLS)
-            if at_y == 0:
-                copies[slot].wait()
-                for p in range(2):
-                    for q in range(2):
-                        rows = slice(p * TILE_SIZE, (p + 1) * TILE_SIZE)
-                        lanes = slice(q * TILE_SIZE, (q + 1) * TILE_SIZE)
-                        left = slot * COLS + q * TILE_SIZE
-                        masked[rows, left : left + TILE_SIZE] = factors[slot, rows, lanes] * keep[p][q]
-            weighted[:, cols] = jnp.dot(masked[:, cols], amp, preferred_element_type=F32).astype(BF16)
-        total = lax.dot_general(weighted[...], masked[...], NT, preferred_element_type=F32).astype(BF16)
+        total = jnp.zeros((COLS, COLS), F32)
+        for half, masked in enumerate((own, extra)):
+            if at_y == 0 and half == 1:
+                copy.wait()
+            for slot in range(AUX):
+                cols = slice(slot * COLS, (slot + 1) * COLS)
+                piece = jnp.dot(masked[:, cols], amp, preferred_element_type=F32).astype(BF16)
+                weighted[half, :, cols] = piece
+            total = total + lax.dot_general(weighted[half], masked[...], NT, preferred_element_type=F32)
+        total = total.astype(BF16)
         for at_x in range(VIRT):
             out_ref[at_x * Y + at_y, :ROWS] = total[at_x * ROWS : (at_x + 1) * ROWS]
     group = lax.broadcasted_iota(jnp.int32, (PART, COLS), 1) // ROWS
@@ -137,8 +141,20 @@
         out_ref[to, ROWS:] = zeta
 
 
-def update_kernel(domain_ref, occ_i_ref, occ_j_ref, virt_ref, got_ref, ov_ref, out_ref):
+def scale_kernel(domain_ref, occ_i_ref, occ_j_ref, virt_ref, out_ref):
     x = lax.axis_index("virt")
+    energy = jnp.broadcast_to(virt_ref[...], (ROWS, COLS))
+    row = lax.broadcasted_iota(jnp.int32, (ROWS, COLS), 0) + x * ROWS
+    lane = lax.broadcasted_iota(jnp.int32, (ROWS, COLS), 1)
+    energy_rows = jnp.sum(jnp.where(row == lane, energy, 0.0), axis=1, keepdims=True)
+    denom = energy_rows + energy - occ_i_ref[0] - occ_j_ref[0]
+    row_tile = domain_ref[0, 0, x // 2]
+    left = (row_tile * domain_ref[0, 0, 0]).astype(F32)
+    right = (row_tile * domain_ref[0, 0, 1]).astype(F32)
+    out_ref[...] = jnp.where(lane < TILE_SIZE, left, right) / denom
+
+
+def update_kernel(got_ref, ov_ref, scale_ref, out_ref):
     total = got_ref[0, :ROWS].astype(F32)
     for source in range(1, Z):
         total = total + got_ref[source, :ROWS].astype(F32)
@@ -147,19 +163,10 @@
         part = zeta[:, at_y * ROWS : (at_y + 1) * ROWS]
         fac = ov_ref[at_y * Z * AUX : (at_y + 1) * Z * AUX, :]
         total = total + lax.dot_general(part, fac, TN, preferred_element_type=F32)
-    energy = jnp.broadcast_to(virt_ref[...], (ROWS, COLS))
-    row = lax.broadcasted_iota(jnp.int32, (ROWS, COLS), 0) + x * ROWS
-    lane = lax.broadcasted_iota(jnp.int32, (ROWS, COLS), 1)
-    energy_rows = jnp.sum(jnp.where(row == lane, energy, 0.0), axis=1, keepdims=True)
-    denom = energy_rows + energy - occ_i_ref[0] - occ_j_ref[0]
-    row_tile = domain_ref[0, 0, x // 2]
-    left = (row_tile * domain_ref[0, 0, 0]).astype(F32)
-    right = (row_tile * domain_ref[0, 0, 1]).astype(F32)
-    keep = jnp.where(lane < TILE_SIZE, left, right)
-    out_ref[0, 0] = (total * keep / denom).astype(BF16)
-
-
-def kernel(function, shape, scalars, arrays, scratch=(), mib=16):
+    out_ref[0, 0] = (total * scale_ref[...]).astype(BF16)
+
+
+def kernel(function, shape, scalars, arrays, scratch=(), mib=16, dtype=BF16):
     smem = pl.BlockSpec(memory_space=pltpu.SMEM)
     vmem = pl.BlockSpec(memory_space=pltpu.VMEM)
     call = pl.pallas_call(
@@ -167,7 +174,7 @@
         name=function.__name__,
         in_specs=[smem] * len(scalars) + [vmem] * len(arrays),
         out_specs=vmem,
-        out_shape=jax.ShapeDtypeStruct(shape, BF16),
+        out_shape=jax.ShapeDtypeStruct(shape, dtype),
         scratch_shapes=list(scratch),
         compiler_params=pltpu.CompilerParams(vmem_limit_bytes=mib << 20),
     )
@@ -213,30 +220,29 @@
     down = lax.ppermute(down, "y", [(y, (y - 1) % Y) for y in range(Y)])
     extra = (up, down, lax.ppermute(up, "pair", swap), lax.ppermute(down, "pair", swap))
     got = lax.all_to_all(sent, ("virt", "y"), 0, 0, tiled=True)
-    wide = pltpu.VMEM((COLS, 2 * AUX * COLS), BF16)
+    packed = (COLS, AUX * COLS)
+    extra = kernel(mask_kernel, packed, (vv_mask,), extra)
+    smem, vmem = pl.BlockSpec(memory_space=pltpu.SMEM), pl.BlockSpec(memory_space=pltpu.VMEM)
     sent = pl.pallas_call(
         ladder_kernel,
         name="ladder_kernel",
-        in_specs=[pl.BlockSpec(memory_space=pltpu.SMEM), pl.BlockSpec(memory_space=pltpu.VMEM)] + [hbm] * 5,
-        out_specs=pl.BlockSpec(memory_space=pltpu.VMEM),
+        in_specs=[smem, vmem, vmem, hbm],
+        out_specs=vmem,
         out_shape=jax.ShapeDtypeStruct((VIRT * Y, ROWS + PART, COLS), BF16),
         scratch_shapes=[
-            pltpu.VMEM((2 * AUX, COLS, COLS), BF16),
-            wide,
-            wide,
-            pltpu.SemaphoreType.DMA((2 * AUX,)),
+            pltpu.VMEM(packed, BF16),
+            pltpu.VMEM(packed, BF16),
+            pltpu.VMEM((2,) + packed, BF16),
+            pltpu.SemaphoreType.DMA,
         ],
         compiler_params=pltpu.CompilerParams(vmem_limit_bytes=40 << 20),
-    )(vv_mask, got, vv_factors, *[pltpu.with_memory_space_constraint(part, pltpu.HBM) for part in extra])
+    )(vv_mask, got, vv_factors, pltpu.with_memory_space_constraint(extra, pltpu.HBM))
     got = lax.all_to_all(sent, ("virt", "y"), 0, 0, tiled=True)
     sent = kernel(sum_kernel, (Z, ROWS + AUX, COLS), (), (got,))
     got = lax.all_to_all(sent, "z", 0, 0, tiled=True)
-    return kernel(
-        update_kernel,
-        (1, 1, ROWS, COLS),
-        (pair_domain, occ_energy_i, occ_energy_j),
-        (virt_energy[None, :], got, ov),
-    )
+    scalars = (pair_domain, occ_energy_i, occ_energy_j)
+    scale = kernel(scale_kernel, (ROWS, COLS), scalars, (virt_energy[None, :],), dtype=F32)
+    return kernel(update_kernel, (1, 1, ROWS, COLS), (), (got, ov, scale))
 
 
 def solution(mesh):

time: 94.2 us -> 87.9 us (0.933)
  Pallas kernels: 26.7 us -> 21.1 us
  waiting for transfers between devices: 25.6 us -> 23 us
  blocking collectives: 14 us -> 15.2 us
    pallas_call x1, Pallas kernels: 19.5 us -> 12.5 us  [body(): pl.pallas_call(ladder_kernel, name='ladder_kernel', in_specs=[smem, vmem,...]
    all_to_all x1, waiting for transfers between devices: 5.08 us -> 2.29 us  [body(): got = lax.all_to_all(sent, ('virt', 'y'), 0, 0, tiled=True)]
    pallas_call x3 -> x5, Pallas kernels: 3.08 us -> 4.76 us  [kernel(): return call(*scalars, *arrays)]
    all_to_all x1, blocking collectives: 14 us -> 15.2 us  [body(): got = lax.all_to_all(sent, ('virt', 'y'), 0, 0, tiled=True)]
  transfers between devices with their start and end apart: 7 -> 7, of which waited for: 5 -> 5; matrix products, arithmetic and copies ran while one was open for 0% -> 0% of each run, Pallas kernels for 3% -> 6%
where the time goes in v9:
time: 87.9 us; the launch traced here: 86.8 us
  starting transfers between devices  24.7 us (28%)
  waiting for transfers between devices  23 us (26%)
  Pallas kernels  21.1 us (24%)
  blocking collectives  15.2 us (17%)
  between operations  1.42 us (2%)
  local copies, waits for them, and re-layouts  1.35 us (2%)
    all_to_all x2, waiting for transfers between devices, body(): got = lax.all_to_all(sent, 'z', 0, 0, tiled=True)  18.3 us
    all_to_all x1, blocking collectives, body(): got = lax.all_to_all(sent, ('virt', 'y'), 0, 0, tiled=True)  15.2 us
    all_to_all x2, starting transfers between devices, body(): got = lax.all_to_all(sent, 'z', 0, 0, tiled=True)  13.4 us
    pallas_call x1, Pallas kernels, body(): pl.pallas_call(ladder_kernel, name='ladder_kernel', in_specs=[smem, vmem,...  12.5 us
    all_to_all x1, starting transfers between devices, body(): got = lax.all_to_all(sent, ('virt', 'y'), 0, 0, tiled=True)  7.45 us
    pallas_call x5, Pallas kernels, kernel(): return call(*scalars, *arrays)  4.76 us
    all_to_all x1, waiting for transfers between devices, body(): got = lax.all_to_all(sent, ('virt', 'y'), 0, 0, tiled=True)  2.29 us
    pallas_call x1, Pallas kernels, body(): pl.pallas_call(share_kernel, name='share_kernel', in_specs=[hbm], out_spe...  2.2 us
  transfers between devices with their start and end apart: 7, of which 5 were waited for; matrix products, arithmetic and copies ran while one was open for 0% of the time, Pallas kernels for 6%

profile of v9, /device:TPU:4, one launch (start us, length us, event | category | flops | bytes accessed | tf_op | source)
XLA Modules:
  0.0 86.8 jit_solution(17670573169794911665)
XLA Ops:
  0.0 1.7 %out_kernel.1 = bf16[8,80,256]{2,1,0:T(8,128)(2,1)} custom-call(s32[1,1,2]{2,1,0:T(1,128)} %domain_ref.1, bf16[1,1,64,256]{3,2,1,0:T(8,128)(2,1)} %amp_hbm.1, bf16[512,256]{1,0:T(8,128)(2,1)} %bitcast.2), custom_call_target="tpu_custom_call" | custom-call | tf_op jit(solution)/shard_map/out_kernel/pallas_call | solution.py:196
  1.7 8.5 %all-to-all-start = ((bf16[8,80,256]{2,1,0:T(8,128)(2,1)}), bf16[8,80,256]{2,1,0:T(8,128)(2,1)S(1)}, u32[]{:S(2)}, u32[]{:S(2)}) async-start(bf16[8,80,256]{2,1,0:T(8,128)(2,1)} %out_kernel.1), calls=%async_computation | async-start | bytes 655360 | tf_op jit(solution)/shard_map/all_to_all | solution.py:216
  10.2 0.0 copy-start.3
  10.2 2.2 %share_kernel.1 = (bf16[4,256,256]{2,1,0:T(8,128)(2,1)}, bf16[4,256,256]{2,1,0:T(8,128)(2,1)}) custom-call(bf16[16,256,256]{2,1,0:T(8,128)(2,1)} %own_ref.1), custom_call_target="tpu_custom_call" | custom-call | tf_op jit(solution)/shard_map/share_kernel/pallas_call | solution.py:208
  12.4 1.7 %collective-permute-start = (bf16[4,256,256]{2,1,0:T(8,128)(2,1)}, bf16[4,256,256]{2,1,0:T(8,128)(2,1)S(1)}, u32[]{:S(2)}, u32[]{:S(2)}) collective-permute-start(bf16[4,256,256]{2,1,0:T(8,128)(2,1)} %get-tuple-element.7), channel_id=1, source_target_pairs={{0,8},{8,16},{16,24},{24,0},{1,9},{9,17},{17,25},{25,1},{2,10},{10... | collective-permute-start | bytes 1572872 | tf_op jit(solution)/shard_map/ppermute | solution.py:219
  14.1 1.7 %collective-permute-start.1 = (bf16[4,256,256]{2,1,0:T(8,128)(2,1)}, bf16[4,256,256]{2,1,0:T(8,128)(2,1)}, u32[]{:S(2)}, u32[]{:S(2)}) collective-permute-start(bf16[4,256,256]{2,1,0:T(8,128)(2,1)} %get-tuple-element.8), channel_id=1, source_target_pairs={{0,24},{8,0},{16,8},{24,16},{1,25},{9,1},{17,9},{25,17},{2,26},{10... | collective-permute-start | bytes 1572872 | tf_op jit(solution)/shard_map/ppermute | solution.py:220
  15.7 7.8 %all-to-all-done.got_ref = bf16[8,80,256]{2,1,0:T(8,128)(2,1)S(1)} async-done(((bf16[8,80,256]{2,1,0:T(8,128)(2,1)}), bf16[8,80,256]{2,1,0:T(8,128)(2,1)S(1)}, u32[]{:S(2)}, u32[]{:S(2)}) %all-to-all-start) | async-done | bytes 327712 | tf_op jit(solution)/shard_map/all_to_all | solution.py:216
  23.5 0.9 spread_kernel.1
  24.4 7.5 %all-to-all-start.1 = ((bf16[16,72,256]{2,1,0:T(8,128)(2,1)}), bf16[16,72,256]{2,1,0:T(8,128)(2,1)S(1)}, u32[]{:S(2)}, u32[]{:S(2)}) async-start(bf16[16,72,256]{2,1,0:T(8,128)(2,1)} %spread_kernel.1), calls=%async_computation.1 | async-start | bytes 1179648 | tf_op jit(solution)/shard_map/all_to_all | solution.py:222
  31.8 0.0 copy-start.1
  31.8 0.0 collective-permute-done.refs_0_
  31.8 0.1 collective-permute-start.2
  31.9 0.0 collective-permute-done.1.refs_1_
  31.9 0.5 collective-permute-start.3
  32.4 1.4 %collective-permute-done.2.refs_2_ = bf16[4,256,256]{2,1,0:T(8,128)(2,1)S(1)} collective-permute-done((bf16[4,256,256]{2,1,0:T(8,128)(2,1)S(1)}, bf16[4,256,256]{2,1,0:T(8,128)(2,1)S(1)}, u32[]{:S(2)}, u32[]{:S(2)}) %collective-permute-start.2) | collective-permute-done | bytes 524320 | tf_op jit(solution)/shard_map/ppermute | solution.py:221
  33.8 1.0 %collective-permute-done.3.refs_3_ = bf16[4,256,256]{2,1,0:T(8,128)(2,1)S(1)} collective-permute-done((bf16[4,256,256]{2,1,0:T(8,128)(2,1)}, bf16[4,256,256]{2,1,0:T(8,128)(2,1)S(1)}, u32[]{:S(2)}, u32[]{:S(2)}) %collective-permute-start.3) | collective-permute-done | bytes 524320 | tf_op jit(solution)/shard_map/ppermute | solution.py:221
  34.8 0.0 copy-done.3
  34.8 1.6 %mask_kernel.1.extra_hbm = bf16[256,4096]{1,0:T(8,128)(2,1)S(1)} custom-call(s32[2,2]{1,0:T(2,128)S(1)} %copy-done.3, bf16[4,256,256]{2,1,0:T(8,128)(2,1)S(1)} %collective-permute-done.refs_0_, bf16[4,256,256]{2,1,0:T(8,128)(2,1)} %collective-permute-done.1.refs_1_, bf16[4,256,256]{2,1,0:T(8,128)(2,1)S(1)} %collective-permute-done.2.refs_2_, ...), custom_call_target="tpu_custom_call" | custom-call | tf_op jit(solution)/shard_map/mask_kernel/pallas_call | solution.py:181
  36.4 0.0 copy-start
  36.4 1.3 %copy-done = bf16[256,4096]{1,0:T(8,128)(2,1)} copy-done((bf16[256,4096]{1,0:T(8,128)(2,1)}, bf16[256,4096]{1,0:T(8,128)(2,1)S(1)}, u32[]{:S(2)}) %copy-start) | copy-done | bytes 2097176
  37.7 2.3 %all-to-all-done.1.rows_ref = bf16[16,72,256]{2,1,0:T(8,128)(2,1)S(1)} async-done(((bf16[16,72,256]{2,1,0:T(8,128)(2,1)}), bf16[16,72,256]{2,1,0:T(8,128)(2,1)S(1)}, u32[]{:S(2)}, u32[]{:S(2)}) %all-to-all-start.1) | async-done | bytes 589856 | tf_op jit(solution)/shard_map/all_to_all | solution.py:222
  40.0 0.0 copy-done.1
  40.0 12.5 %ladder_kernel.1 = bf16[16,72,256]{2,1,0:T(8,128)(2,1)S(1)} custom-call(s32[2,2]{1,0:T(2,128)S(1)} %copy-done.3, bf16[16,72,256]{2,1,0:T(8,128)(2,1)S(1)} %all-to-all-done.1.rows_ref, bf16[16,256,256]{2,1,0:T(8,128)(2,1)S(1)} %copy-done.1, bf16[256,4096]{1,0:T(8,128)(2,1)} %copy-done), custom_call_target="tpu_custom_call" | custom-call | tf_op jit(solution)/shard_map/ladder_kernel/pallas_call | solution.py:226
  52.5 0.0 copy-start.4
  52.5 0.0 copy-start.5
  52.5 0.0 copy-start.2
  52.5 15.2 %all_to_all.20.got_ref = bf16[16,72,256]{2,1,0:T(8,128)(2,1)S(1)} all-to-all(bf16[16,72,256]{2,1,0:T(8,128)(2,1)S(1)} %ladder_kernel.1), channel_id=1, replica_groups=mesh['pair'=2,'virt'=4,'y'=4,'z'=8] {'virt','y'}, dimensions={0} | all-to-all | bytes 1179648 | tf_op jit(solution)/shard_map/all_to_all | solution.py:240
  67.7 0.8 sum_kernel.1
  68.5 4.9 %all-to-all-start.3 = ((bf16[8,80,256]{2,1,0:T(8,128)(2,1)}), bf16[8,80,256]{2,1,0:T(8,128)(2,1)S(1)}, u32[]{:S(2)}, u32[]{:S(2)}) async-start(bf16[8,80,256]{2,1,0:T(8,128)(2,1)} %sum_kernel.1), calls=%async_computation.3 | async-start | bytes 655360 | tf_op jit(solution)/shard_map/all_to_all | solution.py:242
  74.7 0.0 copy-done.4
  74.7 0.0 copy-done.5
  74.7 0.6 scale_kernel.1.scale_ref
  75.3 10.6 %all-to-all-done.3.got_ref = bf16[8,80,256]{2,1,0:T(8,128)(2,1)S(1)} async-done(((bf16[8,80,256]{2,1,0:T(8,128)(2,1)}), bf16[8,80,256]{2,1,0:T(8,128)(2,1)S(1)}, u32[]{:S(2)}, u32[]{:S(2)}) %all-to-all-start.3) | async-done | bytes 327712 | tf_op jit(solution)/shard_map/all_to_all | solution.py:242
  85.9 0.0 copy-done.2
  85.9 0.9 %update_kernel.1 = bf16[1,1,64,256]{3,2,1,0:T(8,128)(2,1)} custom-call(bf16[8,80,256]{2,1,0:T(8,128)(2,1)S(1)} %all-to-all-done.3.got_ref, bf16[512,256]{1,0:T(8,128)(2,1)S(1)} %bitcast.3, f32[64,256]{1,0:T(8,128)S(1)} %scale_kernel.1.scale_ref), custom_call_target="tpu_custom_call" | custom-call | tf_op jit(solution)/shard_map/update_kernel/pallas_call | solution.py:181
Async XLA Ops:
  1.7 21.8 %all-to-all-start = ((bf16[8,80,256]{2,1,0:T(8,128)(2,1)}), bf16[8,80,256]{2,1,0:T(8,128)(2,1)S(1)}, u32[]{:S(2)}, u32[]{:S(2)}) async-start(bf16[8,80,256]{2,1,0:T(8,128)(2,1)} %out_kernel.1), calls=%async_computation | async-start | bytes 655360 | tf_op jit(solution)/shard_map/all_to_all | solution.py:216
  10.2 24.6 %copy-start.3 = (s32[2,2]{1,0:T(2,128)S(1)}, s32[2,2]{1,0:T(2,128)}, u32[]{:S(2)}) copy-start(s32[2,2]{1,0:T(2,128)} %mask_ref.3) | copy-start | bytes 52
  12.4 19.4 %collective-permute-start = (bf16[4,256,256]{2,1,0:T(8,128)(2,1)}, bf16[4,256,256]{2,1,0:T(8,128)(2,1)S(1)}, u32[]{:S(2)}, u32[]{:S(2)}) collective-permute-start(bf16[4,256,256]{2,1,0:T(8,128)(2,1)} %get-tuple-element.7), channel_id=1, source_target_pairs={{0,8},{8,16},{16,24},{24,0},{1,9},{9,17},{17,25},{25,1},{2,10},{10... | collective-permute-start | bytes 1572872 | tf_op jit(solution)/shard_map/ppermute | solution.py:219
  14.1 17.8 %collective-permute-start.1 = (bf16[4,256,256]{2,1,0:T(8,128)(2,1)}, bf16[4,256,256]{2,1,0:T(8,128)(2,1)}, u32[]{:S(2)}, u32[]{:S(2)}) collective-permute-start(bf16[4,256,256]{2,1,0:T(8,128)(2,1)} %get-tuple-element.8), channel_id=1, source_target_pairs={{0,24},{8,0},{16,8},{24,16},{1,25},{9,1},{17,9},{25,17},{2,26},{10... | collective-permute-start | bytes 1572872 | tf_op jit(solution)/shard_map/ppermute | solution.py:220
  24.4 15.6 %all-to-all-start.1 = ((bf16[16,72,256]{2,1,0:T(8,128)(2,1)}), bf16[16,72,256]{2,1,0:T(8,128)(2,1)S(1)}, u32[]{:S(2)}, u32[]{:S(2)}) async-start(bf16[16,72,256]{2,1,0:T(8,128)(2,1)} %spread_kernel.1), calls=%async_computation.1 | async-start | bytes 1179648 | tf_op jit(solution)/shard_map/all_to_all | solution.py:222
  31.8 8.2 %copy-start.1 = (bf16[16,256,256]{2,1,0:T(8,128)(2,1)S(1)}, bf16[16,256,256]{2,1,0:T(8,128)(2,1)}, u32[]{:S(2)}) copy-start(bf16[16,256,256]{2,1,0:T(8,128)(2,1)} %own_ref.1) | copy-start | bytes 6291460
  31.8 2.0 %collective-permute-start.2 = (bf16[4,256,256]{2,1,0:T(8,128)(2,1)S(1)}, bf16[4,256,256]{2,1,0:T(8,128)(2,1)S(1)}, u32[]{:S(2)}, u32[]{:S(2)}) collective-permute-start(bf16[4,256,256]{2,1,0:T(8,128)(2,1)S(1)} %collective-permute-done.refs_0_), channel_id=1, source_target_pairs={{0,128},{128,0},{1,129},{129,1},{2,130},{130,2},{3,131},{131,3},{4... | collective-permute-start | bytes 1572872 | tf_op jit(solution)/shard_map/ppermute | solution.py:221
  31.9 2.8 %collective-permute-start.3 = (bf16[4,256,256]{2,1,0:T(8,128)(2,1)}, bf16[4,256,256]{2,1,0:T(8,128)(2,1)S(1)}, u32[]{:S(2)}, u32[]{:S(2)}) collective-permute-start(bf16[4,256,256]{2,1,0:T(8,128)(2,1)} %collective-permute-done.1.refs_1_), channel_id=1, source_target_pairs={{0,128},{128,0},{1,129},{129,1},{2,130},{130,2},{3,131},{131,3},{4... | collective-permute-start | bytes 1572872 | tf_op jit(solution)/shard_map/ppermute | solution.py:221
  36.4 1.3 %copy-start = (bf16[256,4096]{1,0:T(8,128)(2,1)}, bf16[256,4096]{1,0:T(8,128)(2,1)S(1)}, u32[]{:S(2)}) copy-start(bf16[256,4096]{1,0:T(8,128)(2,1)S(1)} %mask_kernel.1.extra_hbm) | copy-start | bytes 6291460
  52.5 22.2 %copy-start.4 = (s32[1,1,2]{2,1,0:T(1,128)S(1)}, s32[1,1,2]{2,1,0:T(1,128)}, u32[]{:S(2)}) copy-start(s32[1,1,2]{2,1,0:T(1,128)} %domain_ref.1) | copy-start | bytes 28
  52.5 22.2 %copy-start.5 = (f32[256]{0:T(256)S(1)}, f32[256]{0:T(256)}, u32[]{:S(2)}) copy-start(f32[256]{0:T(256)} %param.13) | copy-start | bytes 3076
  52.5 33.4 %copy-start.2 = (bf16[512,1,256]{2,0,1:T(8,128)(2,1)S(1)}, bf16[512,1,256]{2,0,1:T(8,128)(2,1)}, u32[]{:S(2)}) copy-start(bf16[512,1,256]{2,0,1:T(8,128)(2,1)} %param.10) | copy-start | bytes 786436
  68.5 17.4 %all-to-all-start.3 = ((bf16[8,80,256]{2,1,0:T(8,128)(2,1)}), bf16[8,80,256]{2,1,0:T(8,128)(2,1)S(1)}, u32[]{:S(2)}, u32[]{:S(2)}) async-start(bf16[8,80,256]{2,1,0:T(8,128)(2,1)} %sum_kernel.1), calls=%async_computation.3 | async-start | bytes 655360 | tf_op jit(solution)/shard_map/all_to_all | solution.py:242

commit v10 on v9

--- a/solution.py
+++ b/solution.py
@@ -66,42 +66,57 @@
             out_ref[to_x * Y + to_y, ROWS:] = got_ref[2 * to_x + low, start : start + PART]
 
 
-def mask_kernel(mask_ref, *refs):
-    out_ref = refs[-1]
-    sources = [(ref, aux) for ref in refs[:-1] for aux in range(ref.shape[0])]
+def mask_into(masked, slot, matrix, mask_ref):
     for p in range(2):
-        rows = slice(p * TILE_SIZE, (p + 1) * TILE_SIZE)
         for q in range(2):
             keep = jnp.full((1, TILE_SIZE), mask_ref[p, q], jnp.int32).astype(F32).astype(BF16)
-            for slot, (ref, aux) in enumerate(sources):
-                left = slot * COLS + q * TILE_SIZE
-                block = ref[aux, rows, q * TILE_SIZE : (q + 1) * TILE_SIZE]
-                out_ref[rows, left : left + TILE_SIZE] = block * keep
-
-
-def ladder_kernel(mask_ref, rows_ref, own_ref, extra_hbm, out_ref, own, extra, weighted, sem):
-    copy = pltpu.make_async_copy(extra_hbm, extra, sem)
-    copy.start()
-    mask_kernel(mask_ref, own_ref, own)
+            rows = slice(p * TILE_SIZE, (p + 1) * TILE_SIZE)
+            left = slot * COLS + q * TILE_SIZE
+            block = matrix[rows, q * TILE_SIZE : (q + 1) * TILE_SIZE]
+            masked[rows, left : left + TILE_SIZE] = block * keep
+
+
+def gather_rows(rows_ref, at_y, rows):
+    return jnp.concatenate([rows_ref[at_x * Y + at_y, rows] for at_x in range(VIRT)], axis=0)
+
+
+def ladder_sum(masked, weighted, amp):
+    for slot in range(masked.shape[1] // COLS):
+        cols = slice(slot * COLS, (slot + 1) * COLS)
+        weighted[:, cols] = jnp.dot(masked[:, cols], amp, preferred_element_type=F32).astype(BF16)
+    return lax.dot_general(weighted[...], masked[...], NT, preferred_element_type=F32)
+
+
+def first_kernel(mask_ref, rows_ref, own_ref, up_hbm, down_hbm, sums_ref, zeta_ref, factors, masked, weighted, sems):
+    copies = [
+        pltpu.make_async_copy(ref, factors.at[part], sems.at[part]) for part, ref in enumerate((up_hbm, down_hbm))
+    ]
+    for copy in copies:
+        copy.start()
+    for aux in range(AUX):
+        mask_into(masked, aux, own_ref.at[aux], mask_ref)
+    for part, copy in enumerate(copies):
+        copy.wait()
+        for aux in range(SHARE):
+            mask_into(masked, AUX + part * SHARE + aux, factors.at[part, aux], mask_ref)
     zeta = jnp.zeros((2 * AUX, COLS), F32)
     for at_y in range(Y):
-        amp = jnp.concatenate([rows_ref[at_x * Y + at_y, :ROWS] for at_x in range(VIRT)], axis=0)
-        fac = jnp.concatenate([rows_ref[at_x * Y + at_y, ROWS:] for at_x in range(VIRT)], axis=0)
+        amp = gather_rows(rows_ref, at_y, slice(0, ROWS))
+        fac = gather_rows(rows_ref, at_y, slice(ROWS, ROWS + PART))
         direct = lax.dot_general(fac, amp, NT, preferred_element_type=F32)
         swapped = jnp.dot(fac, amp, preferred_element_type=F32)
         zeta = zeta + (2.0 * direct - swapped)
-        total = jnp.zeros((COLS, COLS), F32)
-        for half, masked in enumerate((own, extra)):
-            if at_y == 0 and half == 1:
-                copy.wait()
-            for slot in range(AUX):
-                cols = slice(slot * COLS, (slot + 1) * COLS)
-                piece = jnp.dot(masked[:, cols], amp, preferred_element_type=F32).astype(BF16)
-                weighted[half, :, cols] = piece
-            total = total + lax.dot_general(weighted[half], masked[...], NT, preferred_element_type=F32)
-        total = total.astype(BF16)
-        for at_x in range(VIRT):
-            out_ref[at_x * Y + at_y, :ROWS] = total[at_x * ROWS : (at_x + 1) * ROWS]
+        sums_ref[at_y] = ladder_sum(masked, weighted, amp)
+    zeta_ref[...] = zeta
+
+
+def second_kernel(mask_ref, rows_ref, zeta_ref, sums_ref, up_hbm, down_hbm, out_ref, factors, masked, weighted, sems):
+    copies = [
+        pltpu.make_async_copy(ref, factors.at[part], sems.at[part]) for part, ref in enumerate((up_hbm, down_hbm))
+    ]
+    for copy in copies:
+        copy.start()
+    zeta = zeta_ref[...]
     group = lax.broadcasted_iota(jnp.int32, (PART, COLS), 1) // ROWS
     for at_x in range(VIRT):
         piece = jnp.zeros((PART, COLS), F32)
@@ -113,6 +128,15 @@
         piece = piece.astype(BF16)
         for at_y in range(Y):
             out_ref[at_x * Y + at_y, ROWS:] = piece
+    for part in range(2):
+        copies[part].wait()
+        for aux in range(SHARE):
+            mask_into(masked, part * SHARE + aux, factors.at[part, aux], mask_ref)
+    for at_y in range(Y):
+        amp = gather_rows(rows_ref, at_y, slice(0, ROWS))
+        total = (sums_ref[at_y] + ladder_sum(masked, weighted, amp)).astype(BF16)
+        for at_x in range(VIRT):
+            out_ref[at_x * Y + at_y, :ROWS] = total[at_x * ROWS : (at_x + 1) * ROWS]
 
 
 def sum_kernel(got_ref, out_ref):
@@ -164,6 +188,10 @@
         fac = ov_ref[at_y * Z * AUX : (at_y + 1) * Z * AUX, :]
         total = total + lax.dot_general(part, fac, TN, preferred_element_type=F32)
     out_ref[0, 0] = (total * scale_ref[...]).astype(BF16)
+
+
+def in_hbm(array):
+    return pltpu.with_memory_space_constraint(array, pltpu.HBM)
 
 
 def kernel(function, shape, scalars, arrays, scratch=(), mib=16, dtype=BF16):
@@ -218,25 +246,40 @@
     swap = [(0, 1), (1, 0)]
     up = lax.ppermute(up, "y", [(y, (y + 1) % Y) for y in range(Y)])
     down = lax.ppermute(down, "y", [(y, (y - 1) % Y) for y in range(Y)])
-    extra = (up, down, lax.ppermute(up, "pair", swap), lax.ppermute(down, "pair", swap))
     got = lax.all_to_all(sent, ("virt", "y"), 0, 0, tiled=True)
-    packed = (COLS, AUX * COLS)
-    extra = kernel(mask_kernel, packed, (vv_mask,), extra)
+    up2 = lax.ppermute(up, "pair", swap)
+    down2 = lax.ppermute(down, "pair", swap)
     smem, vmem = pl.BlockSpec(memory_space=pltpu.SMEM), pl.BlockSpec(memory_space=pltpu.VMEM)
+    shares = pltpu.VMEM((2, SHARE, COLS, COLS), BF16)
+    all_sums = (Y, COLS, COLS)
+    sums, zeta = pl.pallas_call(
+        first_kernel,
+        name="first_kernel",
+        in_specs=[smem, vmem, vmem, hbm, hbm],
+        out_specs=[vmem, vmem],
+        out_shape=[jax.ShapeDtypeStruct(all_sums, F32), jax.ShapeDtypeStruct((2 * AUX, COLS), F32)],
+        scratch_shapes=[
+            shares,
+            pltpu.VMEM((COLS, 3 * PART * COLS), BF16),
+            pltpu.VMEM((COLS, 3 * PART * COLS), BF16),
+            pltpu.SemaphoreType.DMA((2,)),
+        ],
+        compiler_params=pltpu.CompilerParams(vmem_limit_bytes=32 << 20),
+    )(vv_mask, got, vv_factors, in_hbm(up), in_hbm(down))
     sent = pl.pallas_call(
-        ladder_kernel,
-        name="ladder_kernel",
-        in_specs=[smem, vmem, vmem, hbm],
+        second_kernel,
+        name="second_kernel",
+        in_specs=[smem, vmem, vmem, vmem, hbm, hbm],
         out_specs=vmem,
         out_shape=jax.ShapeDtypeStruct((VIRT * Y, ROWS + PART, COLS), BF16),
         scratch_shapes=[
-            pltpu.VMEM(packed, BF16),
-            pltpu.VMEM(packed, BF16),
-            pltpu.VMEM((2,) + packed, BF16),
-            pltpu.SemaphoreType.DMA,
+            shares,
+            pltpu.VMEM((COLS, PART * COLS), BF16),
+            pltpu.VMEM((COLS, PART * COLS), BF16),
+            pltpu.SemaphoreType.DMA((2,)),
         ],
-        compiler_params=pltpu.CompilerParams(vmem_limit_bytes=40 << 20),
-    )(vv_mask, got, vv_factors, pltpu.with_memory_space_constraint(extra, pltpu.HBM))
+        compiler_params=pltpu.CompilerParams(vmem_limit_bytes=32 << 20),
+    )(vv_mask, got, zeta, sums, in_hbm(up2), in_hbm(down2))
     got = lax.all_to_all(sent, ("virt", "y"), 0, 0, tiled=True)
     sent = kernel(sum_kernel, (Z, ROWS + AUX, COLS), (), (got,))
     got = lax.all_to_all(sent, "z", 0, 0, tiled=True)

time: 87.9 us -> 84.7 us (0.964)
  starting transfers between devices: 24.7 us -> 23.3 us
  local copies, waits for them, and re-layouts: 1.35 us -> 0.03 us
  waiting for transfers between devices: 23 us -> 24.3 us
  blocking collectives: 15.2 us -> 14 us
    all_to_all x1, waiting for transfers between devices: 2.29 us -> 7.57 us  [body(): got = lax.all_to_all(sent, ('virt', 'y'), 0, 0, tiled=True)]
    ppermute x2, waiting for transfers between devices: 2.36 us -> 0.01 us  [the longest x1 0.01 us: body(): up2 = lax.ppermute(up, 'pair', swap)]
    all_to_all x2, waiting for transfers between devices: 18.3 us -> 16.7 us  [body(): got = lax.all_to_all(sent, 'z', 0, 0, tiled=True)]
    pallas_call x5 -> x4, Pallas kernels: 4.76 us -> 3.19 us  [kernel(): return call(*scalars, *arrays)]
    all_to_all x2, starting transfers between devices: 13.4 us -> 11.9 us  [body(): got = lax.all_to_all(sent, 'z', 0, 0, tiled=True)]
    unnamed x12, local copies, waits for them, and re-layouts: 1.35 us -> 0.03 us
    all_to_all x1, blocking collectives: 15.2 us -> 14 us  [body(): got = lax.all_to_all(sent, ('virt', 'y'), 0, 0, tiled=True)]
    pallas_call x1 -> x2, Pallas kernels: 12.5 us -> 13 us  [the longest x1 8.73 us: body(): pl.pallas_call(first_kernel, name='first_kernel', in_specs=[smem, vmem, v...]
  transfers between devices with their start and end apart: 7 -> 7, of which waited for: 5 -> 3; matrix products, arithmetic and copies ran while one was open for 0% -> 0% of each run, Pallas kernels for 6% -> 15%
where the time goes in v10:
time: 84.7 us; the launch traced here: 83.3 us
  waiting for transfers between devices  24.3 us (29%)
  starting transfers between devices  23.3 us (28%)
  Pallas kernels  20.3 us (24%)
  blocking collectives  14 us (17%)
  between operations  1.44 us (2%)
    all_to_all x2, waiting for transfers between devices, body(): got = lax.all_to_all(sent, 'z', 0, 0, tiled=True)  16.7 us
    all_to_all x1, blocking collectives, body(): got = lax.all_to_all(sent, ('virt', 'y'), 0, 0, tiled=True)  14 us
    all_to_all x2, starting transfers between devices, body(): got = lax.all_to_all(sent, 'z', 0, 0, tiled=True)  11.9 us
    pallas_call x1, Pallas kernels, body(): pl.pallas_call(first_kernel, name='first_kernel', in_specs=[smem, vmem, v...  8.73 us
    all_to_all x1, waiting for transfers between devices, body(): got = lax.all_to_all(sent, ('virt', 'y'), 0, 0, tiled=True)  7.57 us
    all_to_all x1, starting transfers between devices, body(): got = lax.all_to_all(sent, ('virt', 'y'), 0, 0, tiled=True)  7.45 us
    pallas_call x1, Pallas kernels, body(): pl.pallas_call(second_kernel, name='second_kernel', in_specs=[smem, vmem,...  4.26 us
    pallas_call x4, Pallas kernels, kernel(): return call(*scalars, *arrays)  3.19 us
  transfers between devices with their start and end apart: 7, of which 3 were waited for; matrix products, arithmetic and copies ran while one was open for 0% of the time, Pallas kernels for 15%

profile of v10, /device:TPU:4, one launch (start us, length us, event | category | flops | bytes accessed | tf_op | source)
XLA Modules:
  0.0 83.3 jit_solution(8473310452316535226)
XLA Ops:
  0.0 1.7 %out_kernel.1 = bf16[8,80,256]{2,1,0:T(8,128)(2,1)} custom-call(s32[1,1,2]{2,1,0:T(1,128)} %domain_ref.1, bf16[1,1,64,256]{3,2,1,0:T(8,128)(2,1)} %amp_hbm.1, bf16[512,256]{1,0:T(8,128)(2,1)} %bitcast.2), custom_call_target="tpu_custom_call" | custom-call | tf_op jit(solution)/shard_map/out_kernel/pallas_call | solution.py:224
  1.7 8.5 %all-to-all-start = ((bf16[8,80,256]{2,1,0:T(8,128)(2,1)}), bf16[8,80,256]{2,1,0:T(8,128)(2,1)S(1)}, u32[]{:S(2)}, u32[]{:S(2)}) async-start(bf16[8,80,256]{2,1,0:T(8,128)(2,1)} %out_kernel.1), calls=%async_computation | async-start | bytes 655360 | tf_op jit(solution)/shard_map/all_to_all | solution.py:244
  10.2 0.0 copy-start
  10.2 0.0 copy-start.2
  10.2 2.4 %share_kernel.1 = (bf16[4,256,256]{2,1,0:T(8,128)(2,1)}, bf16[4,256,256]{2,1,0:T(8,128)(2,1)}) custom-call(bf16[16,256,256]{2,1,0:T(8,128)(2,1)} %own_ref.1), custom_call_target="tpu_custom_call" | custom-call | tf_op jit(solution)/shard_map/share_kernel/pallas_call | solution.py:236
  12.6 1.7 %collective-permute-start = (bf16[4,256,256]{2,1,0:T(8,128)(2,1)}, bf16[4,256,256]{2,1,0:T(8,128)(2,1)S(1)}, u32[]{:S(2)}, u32[]{:S(2)}) collective-permute-start(bf16[4,256,256]{2,1,0:T(8,128)(2,1)} %get-tuple-element.9), channel_id=1, source_target_pairs={{0,8},{8,16},{16,24},{24,0},{1,9},{9,17},{17,25},{25,1},{2,10},{10... | collective-permute-start | bytes 1572872 | tf_op jit(solution)/shard_map/ppermute | solution.py:247
  14.3 1.7 %collective-permute-start.1 = (bf16[4,256,256]{2,1,0:T(8,128)(2,1)}, bf16[4,256,256]{2,1,0:T(8,128)(2,1)}, u32[]{:S(2)}, u32[]{:S(2)}) collective-permute-start(bf16[4,256,256]{2,1,0:T(8,128)(2,1)} %get-tuple-element.10), channel_id=1, source_target_pairs={{0,24},{8,0},{16,8},{24,16},{1,25},{9,1},{17,9},{25,17},{2,26},{10... | collective-permute-start | bytes 1572872 | tf_op jit(solution)/shard_map/ppermute | solution.py:248
  15.9 7.6 %all-to-all-done.got_ref = bf16[8,80,256]{2,1,0:T(8,128)(2,1)S(1)} async-done(((bf16[8,80,256]{2,1,0:T(8,128)(2,1)}), bf16[8,80,256]{2,1,0:T(8,128)(2,1)S(1)}, u32[]{:S(2)}, u32[]{:S(2)}) %all-to-all-start) | async-done | bytes 327712 | tf_op jit(solution)/shard_map/all_to_all | solution.py:244
  23.5 0.9 %spread_kernel.1 = bf16[16,72,256]{2,1,0:T(8,128)(2,1)} custom-call(bf16[8,80,256]{2,1,0:T(8,128)(2,1)S(1)} %all-to-all-done.got_ref), custom_call_target="tpu_custom_call" | custom-call | tf_op jit(solution)/shard_map/spread_kernel/pallas_call | solution.py:209
  24.4 7.5 %all-to-all-start.1 = ((bf16[16,72,256]{2,1,0:T(8,128)(2,1)}), bf16[16,72,256]{2,1,0:T(8,128)(2,1)S(1)}, u32[]{:S(2)}, u32[]{:S(2)}) async-start(bf16[16,72,256]{2,1,0:T(8,128)(2,1)} %spread_kernel.1), calls=%async_computation.1 | async-start | bytes 1179648 | tf_op jit(solution)/shard_map/all_to_all | solution.py:249
  31.8 0.0 collective-permute-done.up_hbm
  31.8 0.0 copy-start.5
  31.8 0.1 collective-permute-start.2
  31.9 0.0 collective-permute-done.1.down_hbm
  31.9 0.5 collective-permute-start.3
  32.4 7.6 %all-to-all-done.1.rows_ref = bf16[16,72,256]{2,1,0:T(8,128)(2,1)S(1)} async-done(((bf16[16,72,256]{2,1,0:T(8,128)(2,1)}), bf16[16,72,256]{2,1,0:T(8,128)(2,1)S(1)}, u32[]{:S(2)}, u32[]{:S(2)}) %all-to-all-start.1) | async-done | bytes 589856 | tf_op jit(solution)/shard_map/all_to_all | solution.py:249
  40.0 0.0 copy-done.5
  40.0 0.0 copy-done
  40.0 0.0 copy-done.2
  40.0 8.7 %first_kernel.1 = (f32[4,256,256]{2,1,0:T(8,128)S(1)}, f32[32,256]{1,0:T(8,128)S(1)}) custom-call(s32[2,2]{1,0:T(2,128)S(1)} %copy-done.2, bf16[16,72,256]{2,1,0:T(8,128)(2,1)S(1)} %all-to-all-done.1.rows_ref, bf16[16,256,256]{2,1,0:T(8,128)(2,1)S(1)} %copy-done, bf16[4,256,256]{2,1,0:T(8,128)(2,1)} %copy-done.5, ...), custom_call_target="tpu_custom_call" | custom-call | tf_op jit(solution)/shard_map/first_kernel/pallas_call | solution.py:255
  48.8 0.0 collective-permute-done.2.up_hbm
  48.8 0.0 collective-permute-done.3.down_hbm
  48.8 4.3 %second_kernel.1 = bf16[16,72,256]{2,1,0:T(8,128)(2,1)S(1)} custom-call(s32[2,2]{1,0:T(2,128)S(1)} %copy-done.2, bf16[16,72,256]{2,1,0:T(8,128)(2,1)S(1)} %all-to-all-done.1.rows_ref, f32[32,256]{1,0:T(8,128)S(1)} %get-tuple-element.11.zeta_ref, f32[4,256,256]{2,1,0:T(8,128)S(1)} %get-tuple-element.12.sums_ref, ...), custom_call_target="tpu_custom_call" | custom-call | tf_op jit(solution)/shard_map/second_kernel/pallas_call | solution.py:269
  53.0 0.0 copy-start.3
  53.1 0.0 copy-start.4
  53.1 0.0 copy-start.1
  53.1 14.0 %all_to_all.20.got_ref = bf16[16,72,256]{2,1,0:T(8,128)(2,1)S(1)} all-to-all(bf16[16,72,256]{2,1,0:T(8,128)(2,1)S(1)} %second_kernel.1), channel_id=1, replica_groups=mesh['pair'=2,'virt'=4,'y'=4,'z'=8] {'virt','y'}, dimensions={0} | all-to-all | bytes 1179648 | tf_op jit(solution)/shard_map/all_to_all | solution.py:283
  67.1 0.8 sum_kernel.1
  67.9 3.4 %all-to-all-start.3 = ((bf16[8,80,256]{2,1,0:T(8,128)(2,1)}), bf16[8,80,256]{2,1,0:T(8,128)(2,1)S(1)}, u32[]{:S(2)}, u32[]{:S(2)}) async-start(bf16[8,80,256]{2,1,0:T(8,128)(2,1)} %sum_kernel.1), calls=%async_computation.3 | async-start | bytes 655360 | tf_op jit(solution)/shard_map/all_to_all | solution.py:285
  72.6 0.0 copy-done.3
  72.6 0.0 copy-done.4
  72.6 0.6 scale_kernel.1.scale_ref
  73.3 9.1 %all-to-all-done.3.got_ref = bf16[8,80,256]{2,1,0:T(8,128)(2,1)S(1)} async-done(((bf16[8,80,256]{2,1,0:T(8,128)(2,1)}), bf16[8,80,256]{2,1,0:T(8,128)(2,1)S(1)}, u32[]{:S(2)}, u32[]{:S(2)}) %all-to-all-start.3) | async-done | bytes 327712 | tf_op jit(solution)/shard_map/all_to_all | solution.py:285
  82.4 0.0 copy-done.1
  82.4 0.9 %update_kernel.1 = bf16[1,1,64,256]{3,2,1,0:T(8,128)(2,1)} custom-call(bf16[8,80,256]{2,1,0:T(8,128)(2,1)S(1)} %all-to-all-done.3.got_ref, bf16[512,256]{1,0:T(8,128)(2,1)S(1)} %bitcast.3, f32[64,256]{1,0:T(8,128)S(1)} %scale_kernel.1.scale_ref), custom_call_target="tpu_custom_call" | custom-call | tf_op jit(solution)/shard_map/update_kernel/pallas_call | solution.py:209
Async XLA Ops:
  1.7 21.8 %all-to-all-start = ((bf16[8,80,256]{2,1,0:T(8,128)(2,1)}), bf16[8,80,256]{2,1,0:T(8,128)(2,1)S(1)}, u32[]{:S(2)}, u32[]{:S(2)}) async-start(bf16[8,80,256]{2,1,0:T(8,128)(2,1)} %out_kernel.1), calls=%async_computation | async-start | bytes 655360 | tf_op jit(solution)/shard_map/all_to_all | solution.py:244
  10.2 29.8 %copy-start = (bf16[16,256,256]{2,1,0:T(8,128)(2,1)S(1)}, bf16[16,256,256]{2,1,0:T(8,128)(2,1)}, u32[]{:S(2)}) copy-start(bf16[16,256,256]{2,1,0:T(8,128)(2,1)} %own_ref.1) | copy-start | bytes 6291460
  10.2 29.8 %copy-start.2 = (s32[2,2]{1,0:T(2,128)S(1)}, s32[2,2]{1,0:T(2,128)}, u32[]{:S(2)}) copy-start(s32[2,2]{1,0:T(2,128)} %mask_ref.3) | copy-start | bytes 52
  12.6 19.2 %collective-permute-start = (bf16[4,256,256]{2,1,0:T(8,128)(2,1)}, bf16[4,256,256]{2,1,0:T(8,128)(2,1)S(1)}, u32[]{:S(2)}, u32[]{:S(2)}) collective-permute-start(bf16[4,256,256]{2,1,0:T(8,128)(2,1)} %get-tuple-element.9), channel_id=1, source_target_pairs={{0,8},{8,16},{16,24},{24,0},{1,9},{9,17},{17,25},{25,1},{2,10},{10... | collective-permute-start | bytes 1572872 | tf_op jit(solution)/shard_map/ppermute | solution.py:247
  14.3 17.7 %collective-permute-start.1 = (bf16[4,256,256]{2,1,0:T(8,128)(2,1)}, bf16[4,256,256]{2,1,0:T(8,128)(2,1)}, u32[]{:S(2)}, u32[]{:S(2)}) collective-permute-start(bf16[4,256,256]{2,1,0:T(8,128)(2,1)} %get-tuple-element.10), channel_id=1, source_target_pairs={{0,24},{8,0},{16,8},{24,16},{1,25},{9,1},{17,9},{25,17},{2,26},{10... | collective-permute-start | bytes 1572872 | tf_op jit(solution)/shard_map/ppermute | solution.py:248
  24.4 15.6 %all-to-all-start.1 = ((bf16[16,72,256]{2,1,0:T(8,128)(2,1)}), bf16[16,72,256]{2,1,0:T(8,128)(2,1)S(1)}, u32[]{:S(2)}, u32[]{:S(2)}) async-start(bf16[16,72,256]{2,1,0:T(8,128)(2,1)} %spread_kernel.1), calls=%async_computation.1 | async-start | bytes 1179648 | tf_op jit(solution)/shard_map/all_to_all | solution.py:249
  31.8 8.2 %copy-start.5 = (bf16[4,256,256]{2,1,0:T(8,128)(2,1)}, bf16[4,256,256]{2,1,0:T(8,128)(2,1)S(1)}, u32[]{:S(2)}) copy-start(bf16[4,256,256]{2,1,0:T(8,128)(2,1)S(1)} %collective-permute-done.up_hbm) | copy-start | bytes 1572868
  31.8 16.9 %collective-permute-start.2 = (bf16[4,256,256]{2,1,0:T(8,128)(2,1)S(1)}, bf16[4,256,256]{2,1,0:T(8,128)(2,1)}, u32[]{:S(2)}, u32[]{:S(2)}) collective-permute-start(bf16[4,256,256]{2,1,0:T(8,128)(2,1)S(1)} %collective-permute-done.up_hbm), channel_id=1, source_target_pairs={{0,128},{128,0},{1,129},{129,1},{2,130},{130,2},{3,131},{131,3},{4... | collective-permute-start | bytes 1572872 | tf_op jit(solution)/shard_map/ppermute | solution.py:250
  31.9 16.8 %collective-permute-start.3 = (bf16[4,256,256]{2,1,0:T(8,128)(2,1)}, bf16[4,256,256]{2,1,0:T(8,128)(2,1)}, u32[]{:S(2)}, u32[]{:S(2)}) collective-permute-start(bf16[4,256,256]{2,1,0:T(8,128)(2,1)} %collective-permute-done.1.down_hbm), channel_id=1, source_target_pairs={{0,128},{128,0},{1,129},{129,1},{2,130},{130,2},{3,131},{131,3},{4... | collective-permute-start | bytes 1572872 | tf_op jit(solution)/shard_map/ppermute | solution.py:251
  53.0 19.6 %copy-start.3 = (s32[1,1,2]{2,1,0:T(1,128)S(1)}, s32[1,1,2]{2,1,0:T(1,128)}, u32[]{:S(2)}) copy-start(s32[1,1,2]{2,1,0:T(1,128)} %domain_ref.1) | copy-start | bytes 28
  53.1 19.6 %copy-start.4 = (f32[256]{0:T(256)S(1)}, f32[256]{0:T(256)}, u32[]{:S(2)}) copy-start(f32[256]{0:T(256)} %param.13) | copy-start | bytes 3076
  53.1 29.4 %copy-start.1 = (bf16[512,1,256]{2,0,1:T(8,128)(2,1)S(1)}, bf16[512,1,256]{2,0,1:T(8,128)(2,1)}, u32[]{:S(2)}) copy-start(bf16[512,1,256]{2,0,1:T(8,128)(2,1)} %param.10) | copy-start | bytes 786436
  67.9 14.5 %all-to-all-start.3 = ((bf16[8,80,256]{2,1,0:T(8,128)(2,1)}), bf16[8,80,256]{2,1,0:T(8,128)(2,1)S(1)}, u32[]{:S(2)}, u32[]{:S(2)}) async-start(bf16[8,80,256]{2,1,0:T(8,128)(2,1)} %sum_kernel.1), calls=%async_computation.3 | async-start | bytes 655360 | tf_op jit(solution)/shard_map/all_to_all | solution.py:285

commit v11 on v8

--- a/solution.py
+++ b/solution.py
@@ -21,17 +21,20 @@
 SHARE = 4
 
 
-def out_kernel(domain_hbm, amp_hbm, ov_hbm, out_ref, domain, amp, sems):
+def out_kernel(domain_hbm, amp_hbm, ov_hbm, factors_hbm, out_ref, up_ref, down_ref, domain, amp, sems):
     x = lax.axis_index("virt")
+    share = lax.axis_index("pair") * SHARE
     copies = [
         pltpu.make_async_copy(domain_hbm.at[0], domain, sems.at[0]),
         pltpu.make_async_copy(amp_hbm.at[0, 0], amp, sems.at[1]),
+        pltpu.make_async_copy(factors_hbm.at[pl.ds(share, SHARE)], up_ref, sems.at[2]),
+        pltpu.make_async_copy(factors_hbm.at[pl.ds(2 * SHARE + share, SHARE)], down_ref, sems.at[3]),
     ]
     for to in range(Z):
         for high in range(2):
             start = pl.multiple_of(((2 * high + x // 2) * Z + to) * AUX + (x % 2) * PART, PART)
             target = out_ref.at[to, pl.ds(ROWS + high * PART, PART)]
-            copies.append(pltpu.make_async_copy(ov_hbm.at[pl.ds(start, PART)], target, sems.at[2 + 2 * to + high]))
+            copies.append(pltpu.make_async_copy(ov_hbm.at[pl.ds(start, PART)], target, sems.at[4 + 2 * to + high]))
     for copy in copies:
         copy.start()
     copies[0].wait()
@@ -45,16 +48,6 @@
             out_ref[to, :ROWS, cols] = rows
     for copy in copies[2:]:
         copy.wait()
-
-
-def share_kernel(factors_hbm, up_ref, down_ref, sems):
-    share = lax.axis_index("pair") * SHARE
-    up = pltpu.make_async_copy(factors_hbm.at[pl.ds(share, SHARE)], up_ref, sems.at[0])
-    down = pltpu.make_async_copy(factors_hbm.at[pl.ds(2 * SHARE + share, SHARE)], down_ref, sems.at[1])
-    up.start()
-    down.start()
-    up.wait()
-    down.wait()
 
 
 def spread_kernel(got_ref, out_ref):
@@ -144,8 +137,20 @@
         out_ref[to, ROWS:] = zeta
 
 
-def update_kernel(domain_ref, occ_i_ref, occ_j_ref, virt_ref, got_ref, ov_ref, out_ref):
+def scale_kernel(domain_ref, occ_i_ref, occ_j_ref, virt_ref, out_ref):
     x = lax.axis_index("virt")
+    energy = jnp.broadcast_to(virt_ref[...], (ROWS, COLS))
+    row = lax.broadcasted_iota(jnp.int32, (ROWS, COLS), 0) + x * ROWS
+    lane = lax.broadcasted_iota(jnp.int32, (ROWS, COLS), 1)
+    energy_rows = jnp.sum(jnp.where(row == lane, energy, 0.0), axis=1, keepdims=True)
+    denom = energy_rows + energy - occ_i_ref[0] - occ_j_ref[0]
+    row_tile = domain_ref[0, 0, x // 2]
+    left = (row_tile * domain_ref[0, 0, 0]).astype(F32)
+    right = (row_tile * domain_ref[0, 0, 1]).astype(F32)
+    out_ref[...] = jnp.where(lane < TILE_SIZE, left, right) / denom
+
+
+def update_kernel(got_ref, ov_ref, scale_ref, out_ref):
     total = got_ref[0, :ROWS].astype(F32)
     for source in range(1, Z):
         total = total + got_ref[source, :ROWS].astype(F32)
@@ -154,19 +159,10 @@
         part = zeta[:, at_y * ROWS : (at_y + 1) * ROWS]
         fac = ov_ref[at_y * Z * AUX : (at_y + 1) * Z * AUX, :]
         total = total + lax.dot_general(part, fac, TN, preferred_element_type=F32)
-    energy = jnp.broadcast_to(virt_ref[...], (ROWS, COLS))
-    row = lax.broadcasted_iota(jnp.int32, (ROWS, COLS), 0) + x * ROWS
-    lane = lax.broadcasted_iota(jnp.int32, (ROWS, COLS), 1)
-    energy_rows = jnp.sum(jnp.where(row == lane, energy, 0.0), axis=1, keepdims=True)
-    denom = energy_rows + energy - occ_i_ref[0] - occ_j_ref[0]
-    row_tile = domain_ref[0, 0, x // 2]
-    left = (row_tile * domain_ref[0, 0, 0]).astype(F32)
-    right = (row_tile * domain_ref[0, 0, 1]).astype(F32)
-    keep = jnp.where(lane < TILE_SIZE, left, right)
-    out_ref[0, 0] = (total * keep / denom).astype(BF16)
-
-
-def kernel(function, shape, scalars, arrays, scratch=(), mib=16):
+    out_ref[0, 0] = (total * scale_ref[...]).astype(BF16)
+
+
+def kernel(function, shape, scalars, arrays, scratch=(), mib=16, dtype=BF16):
     smem = pl.BlockSpec(memory_space=pltpu.SMEM)
     vmem = pl.BlockSpec(memory_space=pltpu.VMEM)
     call = pl.pallas_call(
@@ -174,7 +170,7 @@
         name=function.__name__,
         in_specs=[smem] * len(scalars) + [vmem] * len(arrays),
         out_specs=vmem,
-        out_shape=jax.ShapeDtypeStruct(shape, BF16),
+        out_shape=jax.ShapeDtypeStruct(shape, dtype),
         scratch_shapes=list(scratch),
         compiler_params=pltpu.CompilerParams(vmem_limit_bytes=mib << 20),
     )
@@ -193,26 +189,20 @@
 ):
     ov = ov_factors[:, 0, :]
     hbm = pl.BlockSpec(memory_space=pltpu.HBM)
-    sent = pl.pallas_call(
+    vmem = pl.BlockSpec(memory_space=pltpu.VMEM)
+    share = jax.ShapeDtypeStruct((SHARE, COLS, COLS), BF16)
+    sent, up, down = pl.pallas_call(
         out_kernel,
         name="out_kernel",
-        in_specs=[hbm, hbm, hbm],
-        out_specs=pl.BlockSpec(memory_space=pltpu.VMEM),
-        out_shape=jax.ShapeDtypeStruct((Z, ROWS + AUX, COLS), BF16),
+        in_specs=[hbm, hbm, hbm, hbm],
+        out_specs=[vmem, vmem, vmem],
+        out_shape=[jax.ShapeDtypeStruct((Z, ROWS + AUX, COLS), BF16), share, share],
         scratch_shapes=[
             pltpu.SMEM((1, 2), jnp.int32),
             pltpu.VMEM((ROWS, COLS), BF16),
-            pltpu.SemaphoreType.DMA((2 + 2 * Z,)),
+            pltpu.SemaphoreType.DMA((4 + 2 * Z,)),
         ],
-    )(pair_domain, amplitudes, ov)
-    up, down = pl.pallas_call(
-        share_kernel,
-        name="share_kernel",
-        in_specs=[hbm],
-        out_specs=[pl.BlockSpec(memory_space=pltpu.VMEM)] * 2,
-        out_shape=[jax.ShapeDtypeStruct((SHARE, COLS, COLS), BF16)] * 2,
-        scratch_shapes=[pltpu.SemaphoreType.DMA((2,))],
-    )(vv_factors)
+    )(pair_domain, amplitudes, ov, vv_factors)
     got = lax.all_to_all(sent, "z", 0, 0, tiled=True)
     sent = kernel(spread_kernel, (VIRT * Y, ROWS + PART, COLS), (), (got,))
     swap = [(0, 1), (1, 0)]
@@ -238,12 +228,9 @@
     got = lax.all_to_all(sent, ("virt", "y"), 0, 0, tiled=True)
     sent = kernel(sum_kernel, (Z, ROWS + AUX, COLS), (), (got,))
     got = lax.all_to_all(sent, "z", 0, 0, tiled=True)
-    return kernel(
-        update_kernel,
-        (1, 1, ROWS, COLS),
-        (pair_domain, occ_energy_i, occ_energy_j),
-        (virt_energy[None, :], got, ov),
-    )
+    scalars = (pair_domain, occ_energy_i, occ_energy_j)
+    scale = kernel(scale_kernel, (ROWS, COLS), scalars, (virt_energy[None, :],), dtype=F32)
+    return kernel(update_kernel, (1, 1, ROWS, COLS), (), (got, ov, scale))
 
 
 def solution(mesh):

time: 86 us -> 83.8 us (0.974)
  starting transfers between devices: 24.7 us -> 23.2 us
  Pallas kernels: 18.4 us -> 17.1 us
    pallas_call x2 -> x1, Pallas kernels: 4.1 us -> 2.68 us  [body(): pl.pallas_call(out_kernel, name='out_kernel', in_specs=[hbm, hbm, hbm, hb...]
    all_to_all x2, starting transfers between devices: 13.3 us -> 11.9 us  [body(): got = lax.all_to_all(sent, 'z', 0, 0, tiled=True)]
    pallas_call x3 -> x4, Pallas kernels: 3.08 us -> 3.19 us  [kernel(): return call(*scalars, *arrays)]
  transfers between devices with their start and end apart: 7 -> 7, of which waited for: 5 -> 5; matrix products, arithmetic and copies ran while one was open for 0% -> 0% of each run, Pallas kernels for 4% -> 2%
where the time goes in v11:
time: 83.8 us; the launch traced here: 82.5 us
  waiting for transfers between devices  25.9 us (31%)
  starting transfers between devices  23.2 us (28%)
  Pallas kernels  17.1 us (20%)
  blocking collectives  14 us (17%)
  between operations  1.4 us (2%)
    all_to_all x2, waiting for transfers between devices, body(): got = lax.all_to_all(sent, 'z', 0, 0, tiled=True)  19.2 us
    all_to_all x1, blocking collectives, body(): got = lax.all_to_all(sent, ('virt', 'y'), 0, 0, tiled=True)  14 us
    all_to_all x2, starting transfers between devices, body(): got = lax.all_to_all(sent, 'z', 0, 0, tiled=True)  11.9 us
    pallas_call x1, Pallas kernels, body(): pl.pallas_call(ladder_kernel, name='ladder_kernel', in_specs=[pl.BlockSpe...  11.3 us
    all_to_all x1, starting transfers between devices, body(): got = lax.all_to_all(sent, ('virt', 'y'), 0, 0, tiled=True)  7.45 us
    all_to_all x1, waiting for transfers between devices, body(): got = lax.all_to_all(sent, ('virt', 'y'), 0, 0, tiled=True)  5.08 us
    pallas_call x4, Pallas kernels, kernel(): return call(*scalars, *arrays)  3.19 us
    pallas_call x1, Pallas kernels, body(): pl.pallas_call(out_kernel, name='out_kernel', in_specs=[hbm, hbm, hbm, hb...  2.68 us
  transfers between devices with their start and end apart: 7, of which 5 were waited for; matrix products, arithmetic and copies ran while one was open for 0% of the time, Pallas kernels for 2%

profile of v11, /device:TPU:4, one launch (start us, length us, event | category | flops | bytes accessed | tf_op | source)
XLA Modules:
  0.0 82.5 jit_solution(1087292124729966182)
XLA Ops:
  0.0 0.0 copy-start
  0.0 0.0 copy-start.3
  0.0 2.7 %out_kernel.1 = (bf16[8,80,256]{2,1,0:T(8,128)(2,1)}, bf16[4,256,256]{2,1,0:T(8,128)(2,1)}, bf16[4,256,256]{2,1,0:T(8,128)(2,1)}) custom-call(s32[1,1,2]{2,1,0:T(1,128)} %domain_ref.1, bf16[1,1,64,256]{3,2,1,0:T(8,128)(2,1)} %amp_hbm.1, bf16[512,256]{1,0:T(8,128)(2,1)} %bitcast.2, bf16[16,256,256]{2,1,0:T(8,128)(2,1)} %own_ref.1), custom_call_target="tpu_custom_call" | custom-call | tf_op jit(solution)/shard_map/out_kernel/pallas_call | solution.py:194
  2.7 8.5 %all-to-all-start = ((bf16[8,80,256]{2,1,0:T(8,128)(2,1)}), bf16[8,80,256]{2,1,0:T(8,128)(2,1)S(1)}, u32[]{:S(2)}, u32[]{:S(2)}) async-start(bf16[8,80,256]{2,1,0:T(8,128)(2,1)} %get-tuple-element.8), calls=%async_computation | async-start | bytes 655360 | tf_op jit(solution)/shard_map/all_to_all | solution.py:206
  11.2 1.6 %collective-permute-start = (bf16[4,256,256]{2,1,0:T(8,128)(2,1)}, bf16[4,256,256]{2,1,0:T(8,128)(2,1)S(1)}, u32[]{:S(2)}, u32[]{:S(2)}) collective-permute-start(bf16[4,256,256]{2,1,0:T(8,128)(2,1)} %get-tuple-element.9), channel_id=1, source_target_pairs={{0,8},{8,16},{16,24},{24,0},{1,9},{9,17},{17,25},{25,1},{2,10},{10... | collective-permute-start | bytes 1572872 | tf_op jit(solution)/shard_map/ppermute | solution.py:209
  12.7 1.7 %collective-permute-start.1 = (bf16[4,256,256]{2,1,0:T(8,128)(2,1)}, bf16[4,256,256]{2,1,0:T(8,128)(2,1)}, u32[]{:S(2)}, u32[]{:S(2)}) collective-permute-start(bf16[4,256,256]{2,1,0:T(8,128)(2,1)} %get-tuple-element.10), channel_id=1, source_target_pairs={{0,24},{8,0},{16,8},{24,16},{1,25},{9,1},{17,9},{25,17},{2,26},{10... | collective-permute-start | bytes 1572872 | tf_op jit(solution)/shard_map/ppermute | solution.py:210
  14.4 10.0 %all-to-all-done.got_ref = bf16[8,80,256]{2,1,0:T(8,128)(2,1)S(1)} async-done(((bf16[8,80,256]{2,1,0:T(8,128)(2,1)}), bf16[8,80,256]{2,1,0:T(8,128)(2,1)S(1)}, u32[]{:S(2)}, u32[]{:S(2)}) %all-to-all-start) | async-done | bytes 327712 | tf_op jit(solution)/shard_map/all_to_all | solution.py:206
  24.4 0.9 %spread_kernel.1 = bf16[16,72,256]{2,1,0:T(8,128)(2,1)} custom-call(bf16[8,80,256]{2,1,0:T(8,128)(2,1)S(1)} %all-to-all-done.got_ref), custom_call_target="tpu_custom_call" | custom-call | tf_op jit(solution)/shard_map/spread_kernel/pallas_call | solution.py:177
  25.3 7.5 %all-to-all-start.1 = ((bf16[16,72,256]{2,1,0:T(8,128)(2,1)}), bf16[16,72,256]{2,1,0:T(8,128)(2,1)S(1)}, u32[]{:S(2)}, u32[]{:S(2)}) async-start(bf16[16,72,256]{2,1,0:T(8,128)(2,1)} %spread_kernel.1), calls=%async_computation.1 | async-start | bytes 1179648 | tf_op jit(solution)/shard_map/all_to_all | solution.py:212
  32.8 0.0 collective-permute-done.up_hbm
  32.8 0.0 copy-start.5
  32.8 0.1 collective-permute-start.2
  32.9 0.0 collective-permute-done.1.down_hbm
  32.9 0.5 collective-permute-start.3
  33.4 1.4 %collective-permute-done.2.up2_hbm = bf16[4,256,256]{2,1,0:T(8,128)(2,1)S(1)} collective-permute-done((bf16[4,256,256]{2,1,0:T(8,128)(2,1)S(1)}, bf16[4,256,256]{2,1,0:T(8,128)(2,1)S(1)}, u32[]{:S(2)}, u32[]{:S(2)}) %collective-permute-start.2) | collective-permute-done | bytes 524320 | tf_op jit(solution)/shard_map/ppermute | solution.py:211
  34.8 0.0 copy-start.6
  34.8 0.8 copy-done.6
  35.6 0.3 collective-permute-done.3.down2_hbm
  35.9 5.1 %all-to-all-done.1.rows_ref = bf16[16,72,256]{2,1,0:T(8,128)(2,1)S(1)} async-done(((bf16[16,72,256]{2,1,0:T(8,128)(2,1)}), bf16[16,72,256]{2,1,0:T(8,128)(2,1)S(1)}, u32[]{:S(2)}, u32[]{:S(2)}) %all-to-all-start.1) | async-done | bytes 589856 | tf_op jit(solution)/shard_map/all_to_all | solution.py:212
  41.0 0.0 copy-done.5
  41.0 0.0 copy-done
  41.0 0.0 copy-done.3
  41.0 11.3 %ladder_kernel.1 = bf16[16,72,256]{2,1,0:T(8,128)(2,1)S(1)} custom-call(s32[2,2]{1,0:T(2,128)S(1)} %copy-done.3, bf16[16,72,256]{2,1,0:T(8,128)(2,1)S(1)} %all-to-all-done.1.rows_ref, bf16[16,256,256]{2,1,0:T(8,128)(2,1)S(1)} %copy-done, bf16[4,256,256]{2,1,0:T(8,128)(2,1)} %copy-done.5, bf16[4,256,256]{2,1,0:T(8,128)(2,1)} %collective-permute-done.1.down_hbm, ...), custom_call_target="tpu_custom_call" | custom-call | tf_op jit(solution)/shard_map/ladder_kernel/pallas_call | solution.py:214
  52.2 0.0 copy-start.2
  52.3 0.0 copy-start.4
  52.3 0.0 copy-start.1
  52.3 14.0 %all_to_all.20.got_ref = bf16[16,72,256]{2,1,0:T(8,128)(2,1)S(1)} all-to-all(bf16[16,72,256]{2,1,0:T(8,128)(2,1)S(1)} %ladder_kernel.1), channel_id=1, replica_groups=mesh['pair'=2,'virt'=4,'y'=4,'z'=8] {'virt','y'}, dimensions={0} | all-to-all | bytes 1179648 | tf_op jit(solution)/shard_map/all_to_all | solution.py:228
  66.3 0.8 sum_kernel.1
  67.1 3.4 %all-to-all-start.3 = ((bf16[8,80,256]{2,1,0:T(8,128)(2,1)}), bf16[8,80,256]{2,1,0:T(8,128)(2,1)S(1)}, u32[]{:S(2)}, u32[]{:S(2)}) async-start(bf16[8,80,256]{2,1,0:T(8,128)(2,1)} %sum_kernel.1), calls=%async_computation.3 | async-start | bytes 655360 | tf_op jit(solution)/shard_map/all_to_all | solution.py:230
  71.8 0.0 copy-done.2
  71.8 0.0 copy-done.4
  71.8 0.6 scale_kernel.1.scale_ref
  72.5 9.1 %all-to-all-done.3.got_ref = bf16[8,80,256]{2,1,0:T(8,128)(2,1)S(1)} async-done(((bf16[8,80,256]{2,1,0:T(8,128)(2,1)}), bf16[8,80,256]{2,1,0:T(8,128)(2,1)S(1)}, u32[]{:S(2)}, u32[]{:S(2)}) %all-to-all-start.3) | async-done | bytes 327712 | tf_op jit(solution)/shard_map/all_to_all | solution.py:230
  81.6 0.0 copy-done.1
  81.6 0.9 %update_kernel.1 = bf16[1,1,64,256]{3,2,1,0:T(8,128)(2,1)} custom-call(bf16[8,80,256]{2,1,0:T(8,128)(2,1)S(1)} %all-to-all-done.3.got_ref, bf16[512,256]{1,0:T(8,128)(2,1)S(1)} %bitcast.3, f32[64,256]{1,0:T(8,128)S(1)} %scale_kernel.1.scale_ref), custom_call_target="tpu_custom_call" | custom-call | tf_op jit(solution)/shard_map/update_kernel/pallas_call | solution.py:177
Async XLA Ops:
  0.0 41.0 %copy-start = (bf16[16,256,256]{2,1,0:T(8,128)(2,1)S(1)}, bf16[16,256,256]{2,1,0:T(8,128)(2,1)}, u32[]{:S(2)}) copy-start(bf16[16,256,256]{2,1,0:T(8,128)(2,1)} %own_ref.1) | copy-start | bytes 6291460
  0.0 41.0 %copy-start.3 = (s32[2,2]{1,0:T(2,128)S(1)}, s32[2,2]{1,0:T(2,128)}, u32[]{:S(2)}) copy-start(s32[2,2]{1,0:T(2,128)} %mask_ref.1) | copy-start | bytes 52
  2.7 21.8 %all-to-all-start = ((bf16[8,80,256]{2,1,0:T(8,128)(2,1)}), bf16[8,80,256]{2,1,0:T(8,128)(2,1)S(1)}, u32[]{:S(2)}, u32[]{:S(2)}) async-start(bf16[8,80,256]{2,1,0:T(8,128)(2,1)} %get-tuple-element.8), calls=%async_computation | async-start | bytes 655360 | tf_op jit(solution)/shard_map/all_to_all | solution.py:206
  11.2 21.6 %collective-permute-start = (bf16[4,256,256]{2,1,0:T(8,128)(2,1)}, bf16[4,256,256]{2,1,0:T(8,128)(2,1)S(1)}, u32[]{:S(2)}, u32[]{:S(2)}) collective-permute-start(bf16[4,256,256]{2,1,0:T(8,128)(2,1)} %get-tuple-element.9), channel_id=1, source_target_pairs={{0,8},{8,16},{16,24},{24,0},{1,9},{9,17},{17,25},{25,1},{2,10},{10... | collective-permute-start | bytes 1572872 | tf_op jit(solution)/shard_map/ppermute | solution.py:209
  12.7 20.1 %collective-permute-start.1 = (bf16[4,256,256]{2,1,0:T(8,128)(2,1)}, bf16[4,256,256]{2,1,0:T(8,128)(2,1)}, u32[]{:S(2)}, u32[]{:S(2)}) collective-permute-start(bf16[4,256,256]{2,1,0:T(8,128)(2,1)} %get-tuple-element.10), channel_id=1, source_target_pairs={{0,24},{8,0},{16,8},{24,16},{1,25},{9,1},{17,9},{25,17},{2,26},{10... | collective-permute-start | bytes 1572872 | tf_op jit(solution)/shard_map/ppermute | solution.py:210
  25.3 15.6 %all-to-all-start.1 = ((bf16[16,72,256]{2,1,0:T(8,128)(2,1)}), bf16[16,72,256]{2,1,0:T(8,128)(2,1)S(1)}, u32[]{:S(2)}, u32[]{:S(2)}) async-start(bf16[16,72,256]{2,1,0:T(8,128)(2,1)} %spread_kernel.1), calls=%async_computation.1 | async-start | bytes 1179648 | tf_op jit(solution)/shard_map/all_to_all | solution.py:212
  32.8 8.2 %copy-start.5 = (bf16[4,256,256]{2,1,0:T(8,128)(2,1)}, bf16[4,256,256]{2,1,0:T(8,128)(2,1)S(1)}, u32[]{:S(2)}) copy-start(bf16[4,256,256]{2,1,0:T(8,128)(2,1)S(1)} %collective-permute-done.up_hbm) | copy-start | bytes 1572868
  32.8 2.0 %collective-permute-start.2 = (bf16[4,256,256]{2,1,0:T(8,128)(2,1)S(1)}, bf16[4,256,256]{2,1,0:T(8,128)(2,1)S(1)}, u32[]{:S(2)}, u32[]{:S(2)}) collective-permute-start(bf16[4,256,256]{2,1,0:T(8,128)(2,1)S(1)} %collective-permute-done.up_hbm), channel_id=1, source_target_pairs={{0,128},{128,0},{1,129},{129,1},{2,130},{130,2},{3,131},{131,3},{4... | collective-permute-start | bytes 1572872 | tf_op jit(solution)/shard_map/ppermute | solution.py:211
  32.9 3.0 %collective-permute-start.3 = (bf16[4,256,256]{2,1,0:T(8,128)(2,1)}, bf16[4,256,256]{2,1,0:T(8,128)(2,1)}, u32[]{:S(2)}, u32[]{:S(2)}) collective-permute-start(bf16[4,256,256]{2,1,0:T(8,128)(2,1)} %collective-permute-done.1.down_hbm), channel_id=1, source_target_pairs={{0,128},{128,0},{1,129},{129,1},{2,130},{130,2},{3,131},{131,3},{4... | collective-permute-start | bytes 1572872 | tf_op jit(solution)/shard_map/ppermute | solution.py:211
  34.8 0.8 copy-start.6
  52.2 19.6 %copy-start.2 = (s32[1,1,2]{2,1,0:T(1,128)S(1)}, s32[1,1,2]{2,1,0:T(1,128)}, u32[]{:S(2)}) copy-start(s32[1,1,2]{2,1,0:T(1,128)} %domain_ref.1) | copy-start | bytes 28
  52.3 19.6 %copy-start.4 = (f32[256]{0:T(256)S(1)}, f32[256]{0:T(256)}, u32[]{:S(2)}) copy-start(f32[256]{0:T(256)} %param.13) | copy-start | bytes 3076
  52.3 29.4 %copy-start.1 = (bf16[512,1,256]{2,0,1:T(8,128)(2,1)S(1)}, bf16[512,1,256]{2,0,1:T(8,128)(2,1)}, u32[]{:S(2)}) copy-start(bf16[512,1,256]{2,0,1:T(8,128)(2,1)} %param.10) | copy-start | bytes 786436
  67.1 14.5 %all-to-all-start.3 = ((bf16[8,80,256]{2,1,0:T(8,128)(2,1)}), bf16[8,80,256]{2,1,0:T(8,128)(2,1)S(1)}, u32[]{:S(2)}, u32[]{:S(2)}) async-start(bf16[8,80,256]{2,1,0:T(8,128)(2,1)} %sum_kernel.1), calls=%async_computation.3 | async-start | bytes 655360 | tf_op jit(solution)/shard_map/all_to_all | solution.py:230

commit v12 on v11

--- a/solution.py
+++ b/solution.py
@@ -225,11 +225,12 @@
         ],
         compiler_params=pltpu.CompilerParams(vmem_limit_bytes=40 << 20),
     )(vv_mask, got, vv_factors, *[pltpu.with_memory_space_constraint(part, pltpu.HBM) for part in extra])
+    scalars = (pair_domain, occ_energy_i, occ_energy_j)
+    scale = kernel(scale_kernel, (ROWS, COLS), scalars, (virt_energy[None, :],), dtype=F32)
+    sent, scale = lax.optimization_barrier((sent, scale))
     got = lax.all_to_all(sent, ("virt", "y"), 0, 0, tiled=True)
     sent = kernel(sum_kernel, (Z, ROWS + AUX, COLS), (), (got,))
     got = lax.all_to_all(sent, "z", 0, 0, tiled=True)
-    scalars = (pair_domain, occ_energy_i, occ_energy_j)
-    scale = kernel(scale_kernel, (ROWS, COLS), scalars, (virt_energy[None, :],), dtype=F32)
     return kernel(update_kernel, (1, 1, ROWS, COLS), (), (got, ov, scale))
 
 

time: 83.8 us -> 82.5 us (0.984)
  blocking collectives: 14 us -> 28 us
  waiting for transfers between devices: 25.9 us -> 14.8 us
  starting transfers between devices: 23.2 us -> 19.7 us
    all_to_all x0 -> x1, blocking collectives: none -> 14 us  [body(): got = lax.all_to_all(sent, 'z', 0, 0, tiled=True)]
    all_to_all x2 -> x1, waiting for transfers between devices: 19.2 us -> 10 us  [body(): got = lax.all_to_all(sent, 'z', 0, 0, tiled=True)]
    all_to_all x2 -> x1, starting transfers between devices: 11.9 us -> 8.48 us  [body(): got = lax.all_to_all(sent, 'z', 0, 0, tiled=True)]
    ppermute x1, waiting for transfers between devices: 1.4 us -> 0.01 us  [body(): lax.ppermute(up, 'pair', swap)]
  transfers between devices with their start and end apart: 7 -> 6, of which waited for: 5 -> 2; matrix products, arithmetic and copies ran while one was open for 0% -> 0% of each run, Pallas kernels for 2% -> 2%
where the time goes in v12:
time: 82.5 us; the launch traced here: 81.3 us
  blocking collectives  28 us (34%)
  starting transfers between devices  19.7 us (24%)
  Pallas kernels  16.4 us (20%)
  waiting for transfers between devices  14.8 us (18%)
  between operations  1.41 us (2%)
  local copies, waits for them, and re-layouts  0.83 us (1%)
    all_to_all x1, blocking collectives, body(): got = lax.all_to_all(sent, 'z', 0, 0, tiled=True)  14 us
    all_to_all x1, blocking collectives, body(): got = lax.all_to_all(sent, ('virt', 'y'), 0, 0, tiled=True)  14 us
    pallas_call x1, Pallas kernels, body(): pl.pallas_call(ladder_kernel, name='ladder_kernel', in_specs=[pl.BlockSpe...  11.3 us
    all_to_all x1, waiting for transfers between devices, body(): got = lax.all_to_all(sent, 'z', 0, 0, tiled=True)  10 us
    all_to_all x1, starting transfers between devices, body(): got = lax.all_to_all(sent, 'z', 0, 0, tiled=True)  8.48 us
    all_to_all x1, starting transfers between devices, body(): got = lax.all_to_all(sent, ('virt', 'y'), 0, 0, tiled=True)  7.45 us
    all_to_all x1, waiting for transfers between devices, body(): got = lax.all_to_all(sent, ('virt', 'y'), 0, 0, tiled=True)  4.77 us
    pallas_call x1, Pallas kernels, body(): pl.pallas_call(out_kernel, name='out_kernel', in_specs=[hbm, hbm, hbm, hb...  2.71 us
  transfers between devices with their start and end apart: 6, of which 2 were waited for; matrix products, arithmetic and copies ran while one was open for 0% of the time, Pallas kernels for 2%

profile of v12, /device:TPU:4, one launch (start us, length us, event | category | flops | bytes accessed | tf_op | source)
XLA Modules:
  0.0 81.3 jit_solution(7142223327372763779)
XLA Ops:
  0.0 0.0 copy-start.2
  0.0 0.0 copy-start.3
  0.0 0.0 copy-start
  0.0 0.0 copy-start.4
  0.0 2.7 %out_kernel.1 = (bf16[8,80,256]{2,1,0:T(8,128)(2,1)}, bf16[4,256,256]{2,1,0:T(8,128)(2,1)}, bf16[4,256,256]{2,1,0:T(8,128)(2,1)}) custom-call(s32[1,1,2]{2,1,0:T(1,128)} %domain_ref.1, bf16[1,1,64,256]{3,2,1,0:T(8,128)(2,1)} %amp_hbm.1, bf16[512,256]{1,0:T(8,128)(2,1)} %bitcast.2, bf16[16,256,256]{2,1,0:T(8,128)(2,1)} %own_ref.1), custom_call_target="tpu_custom_call" | custom-call | tf_op jit(solution)/shard_map/out_kernel/pallas_call | solution.py:194
  2.7 8.5 %all-to-all-start = ((bf16[8,80,256]{2,1,0:T(8,128)(2,1)}), bf16[8,80,256]{2,1,0:T(8,128)(2,1)S(1)}, u32[]{:S(2)}, u32[]{:S(2)}) async-start(bf16[8,80,256]{2,1,0:T(8,128)(2,1)} %get-tuple-element.10), calls=%async_computation | async-start | bytes 655360 | tf_op jit(solution)/shard_map/all_to_all | solution.py:206
  11.2 1.6 %collective-permute-start = (bf16[4,256,256]{2,1,0:T(8,128)(2,1)}, bf16[4,256,256]{2,1,0:T(8,128)(2,1)S(1)}, u32[]{:S(2)}, u32[]{:S(2)}) collective-permute-start(bf16[4,256,256]{2,1,0:T(8,128)(2,1)} %get-tuple-element.11), channel_id=1, source_target_pairs={{0,8},{8,16},{16,24},{24,0},{1,9},{9,17},{17,25},{25,1},{2,10},{10... | collective-permute-start | bytes 1572872 | tf_op jit(solution)/shard_map/ppermute | solution.py:209
  12.8 1.7 %collective-permute-start.1 = (bf16[4,256,256]{2,1,0:T(8,128)(2,1)}, bf16[4,256,256]{2,1,0:T(8,128)(2,1)}, u32[]{:S(2)}, u32[]{:S(2)}) collective-permute-start(bf16[4,256,256]{2,1,0:T(8,128)(2,1)} %get-tuple-element.12), channel_id=1, source_target_pairs={{0,24},{8,0},{16,8},{24,16},{1,25},{9,1},{17,9},{25,17},{2,26},{10... | collective-permute-start | bytes 1572872 | tf_op jit(solution)/shard_map/ppermute | solution.py:210
  14.5 10.0 %all-to-all-done.got_ref = bf16[8,80,256]{2,1,0:T(8,128)(2,1)S(1)} async-done(((bf16[8,80,256]{2,1,0:T(8,128)(2,1)}), bf16[8,80,256]{2,1,0:T(8,128)(2,1)S(1)}, u32[]{:S(2)}, u32[]{:S(2)}) %all-to-all-start) | async-done | bytes 327712 | tf_op jit(solution)/shard_map/all_to_all | solution.py:206
  24.5 0.9 %spread_kernel.1 = bf16[16,72,256]{2,1,0:T(8,128)(2,1)} custom-call(bf16[8,80,256]{2,1,0:T(8,128)(2,1)S(1)} %all-to-all-done.got_ref), custom_call_target="tpu_custom_call" | custom-call | tf_op jit(solution)/shard_map/spread_kernel/pallas_call | solution.py:177
  25.4 7.5 %all-to-all-start.1 = ((bf16[16,72,256]{2,1,0:T(8,128)(2,1)}), bf16[16,72,256]{2,1,0:T(8,128)(2,1)S(1)}, u32[]{:S(2)}, u32[]{:S(2)}) async-start(bf16[16,72,256]{2,1,0:T(8,128)(2,1)} %spread_kernel.1), calls=%async_computation.1 | async-start | bytes 1179648 | tf_op jit(solution)/shard_map/all_to_all | solution.py:212
  32.8 0.0 collective-permute-done.up_hbm
  32.8 0.0 copy-start.5
  32.8 0.1 collective-permute-start.2
  32.9 0.0 collective-permute-done.1.down_hbm
  32.9 0.5 collective-permute-start.3
  34.7 0.0 copy-done.2
  34.7 0.0 copy-done.3
  34.7 0.6 scale_kernel.1.scale_ref
  35.4 0.0 collective-permute-done.2.up2_hbm
  35.4 0.0 copy-start.6
  35.4 0.8 copy-done.6
  36.2 0.0 collective-permute-done.3.down2_hbm
  36.2 4.8 %all-to-all-done.1.rows_ref = bf16[16,72,256]{2,1,0:T(8,128)(2,1)S(1)} async-done(((bf16[16,72,256]{2,1,0:T(8,128)(2,1)}), bf16[16,72,256]{2,1,0:T(8,128)(2,1)S(1)}, u32[]{:S(2)}, u32[]{:S(2)}) %all-to-all-start.1) | async-done | bytes 589856 | tf_op jit(solution)/shard_map/all_to_all | solution.py:212
  41.0 0.0 copy-done.5
  41.0 0.0 copy-done
  41.0 0.0 copy-done.4
  41.0 11.3 %ladder_kernel.1 = bf16[16,72,256]{2,1,0:T(8,128)(2,1)S(1)} custom-call(s32[2,2]{1,0:T(2,128)S(1)} %copy-done.4, bf16[16,72,256]{2,1,0:T(8,128)(2,1)S(1)} %all-to-all-done.1.rows_ref, bf16[16,256,256]{2,1,0:T(8,128)(2,1)S(1)} %copy-done, bf16[4,256,256]{2,1,0:T(8,128)(2,1)} %copy-done.5, bf16[4,256,256]{2,1,0:T(8,128)(2,1)} %collective-permute-done.1.down_hbm, ...), custom_call_target="tpu_custom_call" | custom-call | tf_op jit(solution)/shard_map/ladder_kernel/pallas_call | solution.py:214
  52.3 0.0 copy-start.1
  52.3 14.0 %all_to_all.20.got_ref = bf16[16,72,256]{2,1,0:T(8,128)(2,1)S(1)} all-to-all(bf16[16,72,256]{2,1,0:T(8,128)(2,1)S(1)} %ladder_kernel.1), channel_id=1, replica_groups=mesh['pair'=2,'virt'=4,'y'=4,'z'=8] {'virt','y'}, dimensions={0} | all-to-all | bytes 1179648 | tf_op jit(solution)/shard_map/all_to_all | solution.py:231
  66.3 0.1 sum_kernel.1
  66.4 14.0 %all_to_all.21.got_ref = bf16[8,80,256]{2,1,0:T(8,128)(2,1)S(1)} all-to-all(bf16[8,80,256]{2,1,0:T(8,128)(2,1)S(1)} %sum_kernel.1), channel_id=1, replica_groups=mesh['pair'=2,'virt'=4,'y'=4,'z'=8] {'z'}, dimensions={0} | all-to-all | bytes 655360 | tf_op jit(solution)/shard_map/all_to_all | solution.py:233
  80.4 0.0 copy-done.1
  80.4 0.9 %update_kernel.1 = bf16[1,1,64,256]{3,2,1,0:T(8,128)(2,1)} custom-call(bf16[8,80,256]{2,1,0:T(8,128)(2,1)S(1)} %all_to_all.21.got_ref, bf16[512,256]{1,0:T(8,128)(2,1)S(1)} %bitcast.3, f32[64,256]{1,0:T(8,128)S(1)} %scale_kernel.1.scale_ref), custom_call_target="tpu_custom_call" | custom-call | tf_op jit(solution)/shard_map/update_kernel/pallas_call | solution.py:177
Async XLA Ops:
  0.0 34.7 %copy-start.2 = (s32[1,1,2]{2,1,0:T(1,128)S(1)}, s32[1,1,2]{2,1,0:T(1,128)}, u32[]{:S(2)}) copy-start(s32[1,1,2]{2,1,0:T(1,128)} %domain_ref.1) | copy-start | bytes 28
  0.0 34.7 %copy-start.3 = (f32[256]{0:T(256)S(1)}, f32[256]{0:T(256)}, u32[]{:S(2)}) copy-start(f32[256]{0:T(256)} %param.13) | copy-start | bytes 3076
  0.0 41.0 %copy-start = (bf16[16,256,256]{2,1,0:T(8,128)(2,1)S(1)}, bf16[16,256,256]{2,1,0:T(8,128)(2,1)}, u32[]{:S(2)}) copy-start(bf16[16,256,256]{2,1,0:T(8,128)(2,1)} %own_ref.1) | copy-start | bytes 6291460
  0.0 41.0 %copy-start.4 = (s32[2,2]{1,0:T(2,128)S(1)}, s32[2,2]{1,0:T(2,128)}, u32[]{:S(2)}) copy-start(s32[2,2]{1,0:T(2,128)} %mask_ref.1) | copy-start | bytes 52
  2.7 21.8 %all-to-all-start = ((bf16[8,80,256]{2,1,0:T(8,128)(2,1)}), bf16[8,80,256]{2,1,0:T(8,128)(2,1)S(1)}, u32[]{:S(2)}, u32[]{:S(2)}) async-start(bf16[8,80,256]{2,1,0:T(8,128)(2,1)} %get-tuple-element.10), calls=%async_computation | async-start | bytes 655360 | tf_op jit(solution)/shard_map/all_to_all | solution.py:206
  11.2 21.6 %collective-permute-start = (bf16[4,256,256]{2,1,0:T(8,128)(2,1)}, bf16[4,256,256]{2,1,0:T(8,128)(2,1)S(1)}, u32[]{:S(2)}, u32[]{:S(2)}) collective-permute-start(bf16[4,256,256]{2,1,0:T(8,128)(2,1)} %get-tuple-element.11), channel_id=1, source_target_pairs={{0,8},{8,16},{16,24},{24,0},{1,9},{9,17},{17,25},{25,1},{2,10},{10... | collective-permute-start | bytes 1572872 | tf_op jit(solution)/shard_map/ppermute | solution.py:209
  12.8 20.1 %collective-permute-start.1 = (bf16[4,256,256]{2,1,0:T(8,128)(2,1)}, bf16[4,256,256]{2,1,0:T(8,128)(2,1)}, u32[]{:S(2)}, u32[]{:S(2)}) collective-permute-start(bf16[4,256,256]{2,1,0:T(8,128)(2,1)} %get-tuple-element.12), channel_id=1, source_target_pairs={{0,24},{8,0},{16,8},{24,16},{1,25},{9,1},{17,9},{25,17},{2,26},{10... | collective-permute-start | bytes 1572872 | tf_op jit(solution)/shard_map/ppermute | solution.py:210
  25.4 15.6 %all-to-all-start.1 = ((bf16[16,72,256]{2,1,0:T(8,128)(2,1)}), bf16[16,72,256]{2,1,0:T(8,128)(2,1)S(1)}, u32[]{:S(2)}, u32[]{:S(2)}) async-start(bf16[16,72,256]{2,1,0:T(8,128)(2,1)} %spread_kernel.1), calls=%async_computation.1 | async-start | bytes 1179648 | tf_op jit(solution)/shard_map/all_to_all | solution.py:212
  32.8 8.2 %copy-start.5 = (bf16[4,256,256]{2,1,0:T(8,128)(2,1)}, bf16[4,256,256]{2,1,0:T(8,128)(2,1)S(1)}, u32[]{:S(2)}) copy-start(bf16[4,256,256]{2,1,0:T(8,128)(2,1)S(1)} %collective-permute-done.up_hbm) | copy-start | bytes 1572868
  32.8 2.6 %collective-permute-start.2 = (bf16[4,256,256]{2,1,0:T(8,128)(2,1)S(1)}, bf16[4,256,256]{2,1,0:T(8,128)(2,1)S(1)}, u32[]{:S(2)}, u32[]{:S(2)}) collective-permute-start(bf16[4,256,256]{2,1,0:T(8,128)(2,1)S(1)} %collective-permute-done.up_hbm), channel_id=1, source_target_pairs={{0,128},{128,0},{1,129},{129,1},{2,130},{130,2},{3,131},{131,3},{4... | collective-permute-start | bytes 1572872 | tf_op jit(solution)/shard_map/ppermute | solution.py:211
  32.9 3.3 %collective-permute-start.3 = (bf16[4,256,256]{2,1,0:T(8,128)(2,1)}, bf16[4,256,256]{2,1,0:T(8,128)(2,1)}, u32[]{:S(2)}, u32[]{:S(2)}) collective-permute-start(bf16[4,256,256]{2,1,0:T(8,128)(2,1)} %collective-permute-done.1.down_hbm), channel_id=1, source_target_pairs={{0,128},{128,0},{1,129},{129,1},{2,130},{130,2},{3,131},{131,3},{4... | collective-permute-start | bytes 1572872 | tf_op jit(solution)/shard_map/ppermute | solution.py:211
  35.4 0.8 %copy-start.6 = (bf16[4,256,256]{2,1,0:T(8,128)(2,1)}, bf16[4,256,256]{2,1,0:T(8,128)(2,1)S(1)}, u32[]{:S(2)}) copy-start(bf16[4,256,256]{2,1,0:T(8,128)(2,1)S(1)} %collective-permute-done.2.up2_hbm) | copy-start | bytes 1572868
  52.3 28.1 %copy-start.1 = (bf16[512,1,256]{2,0,1:T(8,128)(2,1)S(1)}, bf16[512,1,256]{2,0,1:T(8,128)(2,1)}, u32[]{:S(2)}) copy-start(bf16[512,1,256]{2,0,1:T(8,128)(2,1)} %param.10) | copy-start | bytes 786436

commit v13 on v12

--- a/solution.py
+++ b/solution.py
@@ -21,20 +21,17 @@
 SHARE = 4
 
 
-def out_kernel(domain_hbm, amp_hbm, ov_hbm, factors_hbm, out_ref, up_ref, down_ref, domain, amp, sems):
+def out_kernel(domain_hbm, amp_hbm, ov_hbm, out_ref, domain, amp, sems):
     x = lax.axis_index("virt")
-    share = lax.axis_index("pair") * SHARE
     copies = [
         pltpu.make_async_copy(domain_hbm.at[0], domain, sems.at[0]),
         pltpu.make_async_copy(amp_hbm.at[0, 0], amp, sems.at[1]),
-        pltpu.make_async_copy(factors_hbm.at[pl.ds(share, SHARE)], up_ref, sems.at[2]),
-        pltpu.make_async_copy(factors_hbm.at[pl.ds(2 * SHARE + share, SHARE)], down_ref, sems.at[3]),
     ]
     for to in range(Z):
         for high in range(2):
             start = pl.multiple_of(((2 * high + x // 2) * Z + to) * AUX + (x % 2) * PART, PART)
             target = out_ref.at[to, pl.ds(ROWS + high * PART, PART)]
-            copies.append(pltpu.make_async_copy(ov_hbm.at[pl.ds(start, PART)], target, sems.at[4 + 2 * to + high]))
+            copies.append(pltpu.make_async_copy(ov_hbm.at[pl.ds(start, PART)], target, sems.at[2 + 2 * to + high]))
     for copy in copies:
         copy.start()
     copies[0].wait()
@@ -50,6 +47,16 @@
         copy.wait()
 
 
+def share_kernel(factors_hbm, up_ref, down_ref, sems):
+    share = lax.axis_index("pair") * SHARE
+    up = pltpu.make_async_copy(factors_hbm.at[pl.ds(share, SHARE)], up_ref, sems.at[0])
+    down = pltpu.make_async_copy(factors_hbm.at[pl.ds(2 * SHARE + share, SHARE)], down_ref, sems.at[1])
+    up.start()
+    down.start()
+    up.wait()
+    down.wait()
+
+
 def spread_kernel(got_ref, out_ref):
     for to_x in range(VIRT):
         for to_y in range(Y):
@@ -78,13 +85,6 @@
                 block = matrix[rows, q * TILE_SIZE : (q + 1) * TILE_SIZE]
                 masked[rows, left : left + TILE_SIZE] = block * keep
 
-    for aux in range(AUX):
-        mask(aux, own_ref.at[aux])
-    for part, copy in enumerate(copies):
-        copy.wait()
-        for aux in range(SHARE):
-            mask(AUX + part * SHARE + aux, factors.at[part, aux])
-
     zeta = jnp.zeros((2 * AUX, COLS), F32)
     for at_y in range(Y):
         amp = jnp.concatenate([rows_ref[at_x * Y + at_y, :ROWS] for at_x in range(VIRT)], axis=0)
@@ -92,9 +92,17 @@
         direct = lax.dot_general(fac, amp, NT, preferred_element_type=F32)
         swapped = jnp.dot(fac, amp, preferred_element_type=F32)
         zeta = zeta + (2.0 * direct - swapped)
+        for aux in range(at_y * SHARE, (at_y + 1) * SHARE):
+            mask(aux, own_ref.at[aux])
+    for copy in copies:
+        copy.wait()
+    for at_y in range(Y):
+        amp = jnp.concatenate([rows_ref[at_x * Y + at_y, :ROWS] for at_x in range(VIRT)], axis=0)
         for slot in range(2 * AUX):
             cols = slice(slot * COLS, (slot + 1) * COLS)
             weighted[:, cols] = jnp.dot(masked[:, cols], amp, preferred_element_type=F32).astype(BF16)
+            if at_y == 0 and slot < AUX:
+                mask(AUX + slot, factors.at[slot // SHARE, slot % SHARE])
         total = lax.dot_general(weighted[...], masked[...], NT, preferred_element_type=F32).astype(BF16)
         for at_x in range(VIRT):
             out_ref[at_x * Y + at_y, :ROWS] = total[at_x * ROWS : (at_x + 1) * ROWS]
@@ -189,20 +197,26 @@
 ):
     ov = ov_factors[:, 0, :]
     hbm = pl.BlockSpec(memory_space=pltpu.HBM)
-    vmem = pl.BlockSpec(memory_space=pltpu.VMEM)
-    share = jax.ShapeDtypeStruct((SHARE, COLS, COLS), BF16)
-    sent, up, down = pl.pallas_call(
+    sent = pl.pallas_call(
         out_kernel,
         name="out_kernel",
-        in_specs=[hbm, hbm, hbm, hbm],
-        out_specs=[vmem, vmem, vmem],
-        out_shape=[jax.ShapeDtypeStruct((Z, ROWS + AUX, COLS), BF16), share, share],
+        in_specs=[hbm, hbm, hbm],
+        out_specs=pl.BlockSpec(memory_space=pltpu.VMEM),
+        out_shape=jax.ShapeDtypeStruct((Z, ROWS + AUX, COLS), BF16),
         scratch_shapes=[
             pltpu.SMEM((1, 2), jnp.int32),
             pltpu.VMEM((ROWS, COLS), BF16),
-            pltpu.SemaphoreType.DMA((4 + 2 * Z,)),
+            pltpu.SemaphoreType.DMA((2 + 2 * Z,)),
         ],
-    )(pair_domain, amplitudes, ov, vv_factors)
+    )(pair_domain, amplitudes, ov)
+    up, down = pl.pallas_call(
+        share_kernel,
+        name="share_kernel",
+        in_specs=[hbm],
+        out_specs=[pl.BlockSpec(memory_space=pltpu.VMEM)] * 2,
+        out_shape=[jax.ShapeDtypeStruct((SHARE, COLS, COLS), BF16)] * 2,
+        scratch_shapes=[pltpu.SemaphoreType.DMA((2,))],
+    )(vv_factors)
     got = lax.all_to_all(sent, "z", 0, 0, tiled=True)
     sent = kernel(spread_kernel, (VIRT * Y, ROWS + PART, COLS), (), (got,))
     swap = [(0, 1), (1, 0)]

time: 82.5 us -> 85.9 us (1.041)
  blocking collectives: 28 us -> 32.3 us
  waiting for transfers between devices: 14.8 us -> 12.3 us
  Pallas kernels: 16.4 us -> 18.2 us
    all_to_all x1, blocking collectives: 14 us -> 18.3 us  [body(): got = lax.all_to_all(sent, 'z', 0, 0, tiled=True)]
    all_to_all x1, waiting for transfers between devices: 10 us -> 7.52 us  [body(): got = lax.all_to_all(sent, 'z', 0, 0, tiled=True)]
    pallas_call x1 -> x2, Pallas kernels: 2.71 us -> 4.13 us  [the longest x1 2.4 us: body(): pl.pallas_call(share_kernel, name='share_kernel', in_specs=[hbm], out_spe...]
  transfers between devices with their start and end apart: 6 -> 6, of which waited for: 2 -> 2; matrix products, arithmetic and copies ran while one was open for 0% -> 0% of each run, Pallas kernels for 2% -> 5%
where the time goes in v13:
time: 85.9 us; the launch traced here: 84.9 us
  blocking collectives  32.3 us (38%)
  starting transfers between devices  19.8 us (23%)
  Pallas kernels  18.2 us (21%)
  waiting for transfers between devices  12.3 us (14%)
  between operations  1.43 us (2%)
    all_to_all x1, blocking collectives, body(): got = lax.all_to_all(sent, 'z', 0, 0, tiled=True)  18.3 us
    all_to_all x1, blocking collectives, body(): got = lax.all_to_all(sent, ('virt', 'y'), 0, 0, tiled=True)  14 us
    pallas_call x1, Pallas kernels, body(): pl.pallas_call(ladder_kernel, name='ladder_kernel', in_specs=[pl.BlockSpe...  11.6 us
    all_to_all x1, starting transfers between devices, body(): got = lax.all_to_all(sent, 'z', 0, 0, tiled=True)  8.48 us
    all_to_all x1, waiting for transfers between devices, body(): got = lax.all_to_all(sent, 'z', 0, 0, tiled=True)  7.52 us
    all_to_all x1, starting transfers between devices, body(): got = lax.all_to_all(sent, ('virt', 'y'), 0, 0, tiled=True)  7.45 us
    all_to_all x1, waiting for transfers between devices, body(): got = lax.all_to_all(sent, ('virt', 'y'), 0, 0, tiled=True)  4.77 us
    pallas_call x4, Pallas kernels, kernel(): return call(*scalars, *arrays)  2.46 us
  transfers between devices with their start and end apart: 6, of which 2 were waited for; matrix products, arithmetic and copies ran while one was open for 0% of the time, Pallas kernels for 5%

profile of v13, /device:TPU:4, one launch (start us, length us, event | category | flops | bytes accessed | tf_op | source)
XLA Modules:
  0.0 84.9 jit_solution(10484271133073331711)
XLA Ops:
  0.0 1.7 %out_kernel.1 = bf16[8,80,256]{2,1,0:T(8,128)(2,1)} custom-call(s32[1,1,2]{2,1,0:T(1,128)} %domain_ref.1, bf16[1,1,64,256]{3,2,1,0:T(8,128)(2,1)} %amp_hbm.1, bf16[512,256]{1,0:T(8,128)(2,1)} %bitcast.2), custom_call_target="tpu_custom_call" | custom-call | tf_op jit(solution)/shard_map/out_kernel/pallas_call | solution.py:200
  1.7 8.5 %all-to-all-start = ((bf16[8,80,256]{2,1,0:T(8,128)(2,1)}), bf16[8,80,256]{2,1,0:T(8,128)(2,1)S(1)}, u32[]{:S(2)}, u32[]{:S(2)}) async-start(bf16[8,80,256]{2,1,0:T(8,128)(2,1)} %out_kernel.1), calls=%async_computation | async-start | bytes 655360 | tf_op jit(solution)/shard_map/all_to_all | solution.py:220
  10.2 0.0 copy-start.2
  10.2 0.0 copy-start.3
  10.2 0.0 copy-start
  10.2 0.0 copy-start.4
  10.3 2.4 %share_kernel.1 = (bf16[4,256,256]{2,1,0:T(8,128)(2,1)}, bf16[4,256,256]{2,1,0:T(8,128)(2,1)}) custom-call(bf16[16,256,256]{2,1,0:T(8,128)(2,1)} %own_ref.1), custom_call_target="tpu_custom_call" | custom-call | tf_op jit(solution)/shard_map/share_kernel/pallas_call | solution.py:212
  12.7 1.7 %collective-permute-start = (bf16[4,256,256]{2,1,0:T(8,128)(2,1)}, bf16[4,256,256]{2,1,0:T(8,128)(2,1)S(1)}, u32[]{:S(2)}, u32[]{:S(2)}) collective-permute-start(bf16[4,256,256]{2,1,0:T(8,128)(2,1)} %get-tuple-element.9), channel_id=1, source_target_pairs={{0,8},{8,16},{16,24},{24,0},{1,9},{9,17},{17,25},{25,1},{2,10},{10... | collective-permute-start | bytes 1572872 | tf_op jit(solution)/shard_map/ppermute | solution.py:223
  14.3 1.7 %collective-permute-start.1 = (bf16[4,256,256]{2,1,0:T(8,128)(2,1)}, bf16[4,256,256]{2,1,0:T(8,128)(2,1)}, u32[]{:S(2)}, u32[]{:S(2)}) collective-permute-start(bf16[4,256,256]{2,1,0:T(8,128)(2,1)} %get-tuple-element.10), channel_id=1, source_target_pairs={{0,24},{8,0},{16,8},{24,16},{1,25},{9,1},{17,9},{25,17},{2,26},{10... | collective-permute-start | bytes 1572872 | tf_op jit(solution)/shard_map/ppermute | solution.py:224
  16.0 7.5 %all-to-all-done.got_ref = bf16[8,80,256]{2,1,0:T(8,128)(2,1)S(1)} async-done(((bf16[8,80,256]{2,1,0:T(8,128)(2,1)}), bf16[8,80,256]{2,1,0:T(8,128)(2,1)S(1)}, u32[]{:S(2)}, u32[]{:S(2)}) %all-to-all-start) | async-done | bytes 327712 | tf_op jit(solution)/shard_map/all_to_all | solution.py:220
  23.5 0.9 %spread_kernel.1 = bf16[16,72,256]{2,1,0:T(8,128)(2,1)} custom-call(bf16[8,80,256]{2,1,0:T(8,128)(2,1)S(1)} %all-to-all-done.got_ref), custom_call_target="tpu_custom_call" | custom-call | tf_op jit(solution)/shard_map/spread_kernel/pallas_call | solution.py:185
  24.4 7.5 %all-to-all-start.1 = ((bf16[16,72,256]{2,1,0:T(8,128)(2,1)}), bf16[16,72,256]{2,1,0:T(8,128)(2,1)S(1)}, u32[]{:S(2)}, u32[]{:S(2)}) async-start(bf16[16,72,256]{2,1,0:T(8,128)(2,1)} %spread_kernel.1), calls=%async_computation.1 | async-start | bytes 1179648 | tf_op jit(solution)/shard_map/all_to_all | solution.py:226
  31.8 0.0 collective-permute-done.up_hbm
  31.8 0.0 copy-start.5
  31.8 0.1 collective-permute-start.2
  31.9 0.0 collective-permute-done.1.down_hbm
  31.9 0.5 collective-permute-start.3
  33.7 0.0 copy-done.2
  33.7 0.0 copy-done.3
  33.7 0.6 scale_kernel.1.scale_ref
  34.4 0.0 collective-permute-done.2.up2_hbm
  34.4 0.0 copy-start.6
  34.4 0.8 copy-done.6
  35.2 0.0 collective-permute-done.3.down2_hbm
  35.2 4.8 %all-to-all-done.1.rows_ref = bf16[16,72,256]{2,1,0:T(8,128)(2,1)S(1)} async-done(((bf16[16,72,256]{2,1,0:T(8,128)(2,1)}), bf16[16,72,256]{2,1,0:T(8,128)(2,1)S(1)}, u32[]{:S(2)}, u32[]{:S(2)}) %all-to-all-start.1) | async-done | bytes 589856 | tf_op jit(solution)/shard_map/all_to_all | solution.py:226
  40.0 0.0 copy-done.5
  40.0 0.0 copy-done
  40.0 0.0 copy-done.4
  40.0 11.6 %ladder_kernel.1 = bf16[16,72,256]{2,1,0:T(8,128)(2,1)S(1)} custom-call(s32[2,2]{1,0:T(2,128)S(1)} %copy-done.4, bf16[16,72,256]{2,1,0:T(8,128)(2,1)S(1)} %all-to-all-done.1.rows_ref, bf16[16,256,256]{2,1,0:T(8,128)(2,1)S(1)} %copy-done, bf16[4,256,256]{2,1,0:T(8,128)(2,1)} %copy-done.5, bf16[4,256,256]{2,1,0:T(8,128)(2,1)} %collective-permute-done.1.down_hbm, ...), custom_call_target="tpu_custom_call" | custom-call | tf_op jit(solution)/shard_map/ladder_kernel/pallas_call | solution.py:228
  51.6 0.0 copy-start.1
  51.6 14.0 %all_to_all.20.got_ref = bf16[16,72,256]{2,1,0:T(8,128)(2,1)S(1)} all-to-all(bf16[16,72,256]{2,1,0:T(8,128)(2,1)S(1)} %ladder_kernel.1), channel_id=1, replica_groups=mesh['pair'=2,'virt'=4,'y'=4,'z'=8] {'virt','y'}, dimensions={0} | all-to-all | bytes 1179648 | tf_op jit(solution)/shard_map/all_to_all | solution.py:245
  65.6 0.1 sum_kernel.1
  65.7 18.3 %all_to_all.21.got_ref = bf16[8,80,256]{2,1,0:T(8,128)(2,1)S(1)} all-to-all(bf16[8,80,256]{2,1,0:T(8,128)(2,1)S(1)} %sum_kernel.1), channel_id=1, replica_groups=mesh['pair'=2,'virt'=4,'y'=4,'z'=8] {'z'}, dimensions={0} | all-to-all | bytes 655360 | tf_op jit(solution)/shard_map/all_to_all | solution.py:247
  84.0 0.0 copy-done.1
  84.0 0.9 %update_kernel.1 = bf16[1,1,64,256]{3,2,1,0:T(8,128)(2,1)} custom-call(bf16[8,80,256]{2,1,0:T(8,128)(2,1)S(1)} %all_to_all.21.got_ref, bf16[512,256]{1,0:T(8,128)(2,1)S(1)} %bitcast.3, f32[64,256]{1,0:T(8,128)S(1)} %scale_kernel.1.scale_ref), custom_call_target="tpu_custom_call" | custom-call | tf_op jit(solution)/shard_map/update_kernel/pallas_call | solution.py:185
Async XLA Ops:
  1.7 21.8 %all-to-all-start = ((bf16[8,80,256]{2,1,0:T(8,128)(2,1)}), bf16[8,80,256]{2,1,0:T(8,128)(2,1)S(1)}, u32[]{:S(2)}, u32[]{:S(2)}) async-start(bf16[8,80,256]{2,1,0:T(8,128)(2,1)} %out_kernel.1), calls=%async_computation | async-start | bytes 655360 | tf_op jit(solution)/shard_map/all_to_all | solution.py:220
  10.2 23.5 %copy-start.2 = (s32[1,1,2]{2,1,0:T(1,128)S(1)}, s32[1,1,2]{2,1,0:T(1,128)}, u32[]{:S(2)}) copy-start(s32[1,1,2]{2,1,0:T(1,128)} %domain_ref.1) | copy-start | bytes 28
  10.2 23.5 %copy-start.3 = (f32[256]{0:T(256)S(1)}, f32[256]{0:T(256)}, u32[]{:S(2)}) copy-start(f32[256]{0:T(256)} %param.13) | copy-start | bytes 3076
  10.2 29.8 %copy-start = (bf16[16,256,256]{2,1,0:T(8,128)(2,1)S(1)}, bf16[16,256,256]{2,1,0:T(8,128)(2,1)}, u32[]{:S(2)}) copy-start(bf16[16,256,256]{2,1,0:T(8,128)(2,1)} %own_ref.1) | copy-start | bytes 6291460
  10.2 29.8 %copy-start.4 = (s32[2,2]{1,0:T(2,128)S(1)}, s32[2,2]{1,0:T(2,128)}, u32[]{:S(2)}) copy-start(s32[2,2]{1,0:T(2,128)} %mask_ref.1) | copy-start | bytes 52
  12.7 19.1 %collective-permute-start = (bf16[4,256,256]{2,1,0:T(8,128)(2,1)}, bf16[4,256,256]{2,1,0:T(8,128)(2,1)S(1)}, u32[]{:S(2)}, u32[]{:S(2)}) collective-permute-start(bf16[4,256,256]{2,1,0:T(8,128)(2,1)} %get-tuple-element.9), channel_id=1, source_target_pairs={{0,8},{8,16},{16,24},{24,0},{1,9},{9,17},{17,25},{25,1},{2,10},{10... | collective-permute-start | bytes 1572872 | tf_op jit(solution)/shard_map/ppermute | solution.py:223
  14.3 17.6 %collective-permute-start.1 = (bf16[4,256,256]{2,1,0:T(8,128)(2,1)}, bf16[4,256,256]{2,1,0:T(8,128)(2,1)}, u32[]{:S(2)}, u32[]{:S(2)}) collective-permute-start(bf16[4,256,256]{2,1,0:T(8,128)(2,1)} %get-tuple-element.10), channel_id=1, source_target_pairs={{0,24},{8,0},{16,8},{24,16},{1,25},{9,1},{17,9},{25,17},{2,26},{10... | collective-permute-start | bytes 1572872 | tf_op jit(solution)/shard_map/ppermute | solution.py:224
  24.4 15.6 %all-to-all-start.1 = ((bf16[16,72,256]{2,1,0:T(8,128)(2,1)}), bf16[16,72,256]{2,1,0:T(8,128)(2,1)S(1)}, u32[]{:S(2)}, u32[]{:S(2)}) async-start(bf16[16,72,256]{2,1,0:T(8,128)(2,1)} %spread_kernel.1), calls=%async_computation.1 | async-start | bytes 1179648 | tf_op jit(solution)/shard_map/all_to_all | solution.py:226
  31.8 8.2 %copy-start.5 = (bf16[4,256,256]{2,1,0:T(8,128)(2,1)}, bf16[4,256,256]{2,1,0:T(8,128)(2,1)S(1)}, u32[]{:S(2)}) copy-start(bf16[4,256,256]{2,1,0:T(8,128)(2,1)S(1)} %collective-permute-done.up_hbm) | copy-start | bytes 1572868
  31.8 2.6 %collective-permute-start.2 = (bf16[4,256,256]{2,1,0:T(8,128)(2,1)S(1)}, bf16[4,256,256]{2,1,0:T(8,128)(2,1)S(1)}, u32[]{:S(2)}, u32[]{:S(2)}) collective-permute-start(bf16[4,256,256]{2,1,0:T(8,128)(2,1)S(1)} %collective-permute-done.up_hbm), channel_id=1, source_target_pairs={{0,128},{128,0},{1,129},{129,1},{2,130},{130,2},{3,131},{131,3},{4... | collective-permute-start | bytes 1572872 | tf_op jit(solution)/shard_map/ppermute | solution.py:225
  31.9 3.3 %collective-permute-start.3 = (bf16[4,256,256]{2,1,0:T(8,128)(2,1)}, bf16[4,256,256]{2,1,0:T(8,128)(2,1)}, u32[]{:S(2)}, u32[]{:S(2)}) collective-permute-start(bf16[4,256,256]{2,1,0:T(8,128)(2,1)} %collective-permute-done.1.down_hbm), channel_id=1, source_target_pairs={{0,128},{128,0},{1,129},{129,1},{2,130},{130,2},{3,131},{131,3},{4... | collective-permute-start | bytes 1572872 | tf_op jit(solution)/shard_map/ppermute | solution.py:225
  34.4 0.8 copy-start.6
  51.6 32.4 %copy-start.1 = (bf16[512,1,256]{2,0,1:T(8,128)(2,1)S(1)}, bf16[512,1,256]{2,0,1:T(8,128)(2,1)}, u32[]{:S(2)}) copy-start(bf16[512,1,256]{2,0,1:T(8,128)(2,1)} %param.10) | copy-start | bytes 786436

commit v14 on v12

--- a/solution.py
+++ b/solution.py
@@ -21,14 +21,14 @@
 SHARE = 4
 
 
-def out_kernel(domain_hbm, amp_hbm, ov_hbm, factors_hbm, out_ref, up_ref, down_ref, domain, amp, sems):
+def out_kernel(domain_hbm, amp_hbm, ov_hbm, factors_hbm, out_ref, up_hbm, down_hbm, domain, amp, shares, sems):
     x = lax.axis_index("virt")
     share = lax.axis_index("pair") * SHARE
     copies = [
         pltpu.make_async_copy(domain_hbm.at[0], domain, sems.at[0]),
         pltpu.make_async_copy(amp_hbm.at[0, 0], amp, sems.at[1]),
-        pltpu.make_async_copy(factors_hbm.at[pl.ds(share, SHARE)], up_ref, sems.at[2]),
-        pltpu.make_async_copy(factors_hbm.at[pl.ds(2 * SHARE + share, SHARE)], down_ref, sems.at[3]),
+        pltpu.make_async_copy(factors_hbm.at[pl.ds(share, SHARE)], shares.at[0], sems.at[2]),
+        pltpu.make_async_copy(factors_hbm.at[pl.ds(2 * SHARE + share, SHARE)], shares.at[1], sems.at[3]),
     ]
     for to in range(Z):
         for high in range(2):
@@ -46,7 +46,12 @@
         rows = (amp[:, cols].astype(F32) * keep).astype(BF16)
         for to in range(Z):
             out_ref[to, :ROWS, cols] = rows
-    for copy in copies[2:]:
+    writes = []
+    for part, target in enumerate((up_hbm, down_hbm)):
+        copies[2 + part].wait()
+        writes.append(pltpu.make_async_copy(shares.at[part], target, sems.at[4 + 2 * Z + part]))
+        writes[-1].start()
+    for copy in copies[4:] + writes:
         copy.wait()
 
 
@@ -195,12 +200,13 @@
         out_kernel,
         name="out_kernel",
         in_specs=[hbm, hbm, hbm, hbm],
-        out_specs=[vmem, vmem, vmem],
+        out_specs=[vmem, hbm, hbm],
         out_shape=[jax.ShapeDtypeStruct((Z, ROWS + AUX, COLS), BF16), share, share],
         scratch_shapes=[
             pltpu.SMEM((1, 2), jnp.int32),
             pltpu.VMEM((ROWS, COLS), BF16),
-            pltpu.SemaphoreType.DMA((4 + 2 * Z,)),
+            pltpu.VMEM((2, SHARE, COLS, COLS), BF16),
+            pltpu.SemaphoreType.DMA((6 + 2 * Z,)),
         ],
     )(pair_domain, amplitudes, ov, vv_factors)
     got = lax.all_to_all(sent, "z", 0, 0, tiled=True)

time: 82.5 us -> 82.9 us (level)
  no operation moved by 1% of the time
where the time goes in v14:
time: 82.9 us; the launch traced here: 81.7 us
  blocking collectives  28 us (34%)
  starting transfers between devices  19.7 us (24%)
  Pallas kernels  16.9 us (20%)
  waiting for transfers between devices  14.8 us (18%)
  between operations  1.41 us (2%)
  local copies, waits for them, and re-layouts  0.83 us (1%)
    all_to_all x1, blocking collectives, body(): got = lax.all_to_all(sent, 'z', 0, 0, tiled=True)  14 us
    all_to_all x1, blocking collectives, body(): got = lax.all_to_all(sent, ('virt', 'y'), 0, 0, tiled=True)  14 us
    pallas_call x1, Pallas kernels, body(): pl.pallas_call(ladder_kernel, name='ladder_kernel', in_specs=[pl.BlockSpe...  11.3 us
    all_to_all x1, waiting for transfers between devices, body(): got = lax.all_to_all(sent, 'z', 0, 0, tiled=True)  10 us
    all_to_all x1, starting transfers between devices, body(): got = lax.all_to_all(sent, 'z', 0, 0, tiled=True)  8.48 us
    all_to_all x1, starting transfers between devices, body(): got = lax.all_to_all(sent, ('virt', 'y'), 0, 0, tiled=True)  7.45 us
    all_to_all x1, waiting for transfers between devices, body(): got = lax.all_to_all(sent, ('virt', 'y'), 0, 0, tiled=True)  4.77 us
    pallas_call x1, Pallas kernels, body(): pl.pallas_call(out_kernel, name='out_kernel', in_specs=[hbm, hbm, hbm, hb...  3.15 us
  transfers between devices with their start and end apart: 6, of which 2 were waited for; matrix products, arithmetic and copies ran while one was open for 0% of the time, Pallas kernels for 2%

profile of v14, /device:TPU:4, one launch (start us, length us, event | category | flops | bytes accessed | tf_op | source)
XLA Modules:
  0.0 81.7 jit_solution(6138369284854368553)
XLA Ops:
  0.0 0.0 copy-start.2
  0.0 0.0 copy-start.3
  0.0 0.0 copy-start
  0.0 0.0 copy-start.4
  0.0 3.1 %out_kernel.1 = (bf16[8,80,256]{2,1,0:T(8,128)(2,1)}, bf16[4,256,256]{2,1,0:T(8,128)(2,1)}, bf16[4,256,256]{2,1,0:T(8,128)(2,1)}) custom-call(s32[1,1,2]{2,1,0:T(1,128)} %domain_ref.1, bf16[1,1,64,256]{3,2,1,0:T(8,128)(2,1)} %amp_hbm.1, bf16[512,256]{1,0:T(8,128)(2,1)} %bitcast.2, bf16[16,256,256]{2,1,0:T(8,128)(2,1)} %own_ref.1), custom_call_target="tpu_custom_call" | custom-call | tf_op jit(solution)/shard_map/out_kernel/pallas_call | solution.py:199
  3.2 8.5 %all-to-all-start = ((bf16[8,80,256]{2,1,0:T(8,128)(2,1)}), bf16[8,80,256]{2,1,0:T(8,128)(2,1)S(1)}, u32[]{:S(2)}, u32[]{:S(2)}) async-start(bf16[8,80,256]{2,1,0:T(8,128)(2,1)} %get-tuple-element.10), calls=%async_computation | async-start | bytes 655360 | tf_op jit(solution)/shard_map/all_to_all | solution.py:212
  11.7 1.6 %collective-permute-start = (bf16[4,256,256]{2,1,0:T(8,128)(2,1)}, bf16[4,256,256]{2,1,0:T(8,128)(2,1)S(1)}, u32[]{:S(2)}, u32[]{:S(2)}) collective-permute-start(bf16[4,256,256]{2,1,0:T(8,128)(2,1)} %get-tuple-element.11), channel_id=1, source_target_pairs={{0,8},{8,16},{16,24},{24,0},{1,9},{9,17},{17,25},{25,1},{2,10},{10... | collective-permute-start | bytes 1572872 | tf_op jit(solution)/shard_map/ppermute | solution.py:215
  13.2 1.7 %collective-permute-start.1 = (bf16[4,256,256]{2,1,0:T(8,128)(2,1)}, bf16[4,256,256]{2,1,0:T(8,128)(2,1)}, u32[]{:S(2)}, u32[]{:S(2)}) collective-permute-start(bf16[4,256,256]{2,1,0:T(8,128)(2,1)} %get-tuple-element.12), channel_id=1, source_target_pairs={{0,24},{8,0},{16,8},{24,16},{1,25},{9,1},{17,9},{25,17},{2,26},{10... | collective-permute-start | bytes 1572872 | tf_op jit(solution)/shard_map/ppermute | solution.py:216
  14.9 10.0 %all-to-all-done.got_ref = bf16[8,80,256]{2,1,0:T(8,128)(2,1)S(1)} async-done(((bf16[8,80,256]{2,1,0:T(8,128)(2,1)}), bf16[8,80,256]{2,1,0:T(8,128)(2,1)S(1)}, u32[]{:S(2)}, u32[]{:S(2)}) %all-to-all-start) | async-done | bytes 327712 | tf_op jit(solution)/shard_map/all_to_all | solution.py:212
  24.9 0.9 %spread_kernel.1 = bf16[16,72,256]{2,1,0:T(8,128)(2,1)} custom-call(bf16[8,80,256]{2,1,0:T(8,128)(2,1)S(1)} %all-to-all-done.got_ref), custom_call_target="tpu_custom_call" | custom-call | tf_op jit(solution)/shard_map/spread_kernel/pallas_call | solution.py:182
  25.8 7.5 %all-to-all-start.1 = ((bf16[16,72,256]{2,1,0:T(8,128)(2,1)}), bf16[16,72,256]{2,1,0:T(8,128)(2,1)S(1)}, u32[]{:S(2)}, u32[]{:S(2)}) async-start(bf16[16,72,256]{2,1,0:T(8,128)(2,1)} %spread_kernel.1), calls=%async_computation.1 | async-start | bytes 1179648 | tf_op jit(solution)/shard_map/all_to_all | solution.py:218
  33.2 0.0 collective-permute-done.up_hbm
  33.3 0.0 copy-start.5
  33.3 0.1 collective-permute-start.2
  33.4 0.0 collective-permute-done.1.down_hbm
  33.4 0.5 collective-permute-start.3
  35.2 0.0 copy-done.2
  35.2 0.0 copy-done.3
  35.2 0.6 scale_kernel.1.scale_ref
  35.8 0.0 collective-permute-done.2.up2_hbm
  35.8 0.0 copy-start.6
  35.9 0.8 copy-done.6
  36.7 0.0 collective-permute-done.3.down2_hbm
  36.7 4.8 %all-to-all-done.1.rows_ref = bf16[16,72,256]{2,1,0:T(8,128)(2,1)S(1)} async-done(((bf16[16,72,256]{2,1,0:T(8,128)(2,1)}), bf16[16,72,256]{2,1,0:T(8,128)(2,1)S(1)}, u32[]{:S(2)}, u32[]{:S(2)}) %all-to-all-start.1) | async-done | bytes 589856 | tf_op jit(solution)/shard_map/all_to_all | solution.py:218
  41.4 0.0 copy-done.5
  41.4 0.0 copy-done
  41.4 0.0 copy-done.4
  41.4 11.3 %ladder_kernel.1 = bf16[16,72,256]{2,1,0:T(8,128)(2,1)S(1)} custom-call(s32[2,2]{1,0:T(2,128)S(1)} %copy-done.4, bf16[16,72,256]{2,1,0:T(8,128)(2,1)S(1)} %all-to-all-done.1.rows_ref, bf16[16,256,256]{2,1,0:T(8,128)(2,1)S(1)} %copy-done, bf16[4,256,256]{2,1,0:T(8,128)(2,1)} %copy-done.5, bf16[4,256,256]{2,1,0:T(8,128)(2,1)} %collective-permute-done.1.down_hbm, ...), custom_call_target="tpu_custom_call" | custom-call | tf_op jit(solution)/shard_map/ladder_kernel/pallas_call | solution.py:220
  52.7 0.0 copy-start.1
  52.7 14.0 %all_to_all.20.got_ref = bf16[16,72,256]{2,1,0:T(8,128)(2,1)S(1)} all-to-all(bf16[16,72,256]{2,1,0:T(8,128)(2,1)S(1)} %ladder_kernel.1), channel_id=1, replica_groups=mesh['pair'=2,'virt'=4,'y'=4,'z'=8] {'virt','y'}, dimensions={0} | all-to-all | bytes 1179648 | tf_op jit(solution)/shard_map/all_to_all | solution.py:237
  66.7 0.1 sum_kernel.1
  66.8 14.0 %all_to_all.21.got_ref = bf16[8,80,256]{2,1,0:T(8,128)(2,1)S(1)} all-to-all(bf16[8,80,256]{2,1,0:T(8,128)(2,1)S(1)} %sum_kernel.1), channel_id=1, replica_groups=mesh['pair'=2,'virt'=4,'y'=4,'z'=8] {'z'}, dimensions={0} | all-to-all | bytes 655360 | tf_op jit(solution)/shard_map/all_to_all | solution.py:239
  80.8 0.0 copy-done.1
  80.8 0.9 %update_kernel.1 = bf16[1,1,64,256]{3,2,1,0:T(8,128)(2,1)} custom-call(bf16[8,80,256]{2,1,0:T(8,128)(2,1)S(1)} %all_to_all.21.got_ref, bf16[512,256]{1,0:T(8,128)(2,1)S(1)} %bitcast.3, f32[64,256]{1,0:T(8,128)S(1)} %scale_kernel.1.scale_ref), custom_call_target="tpu_custom_call" | custom-call | tf_op jit(solution)/shard_map/update_kernel/pallas_call | solution.py:182
Async XLA Ops:
  0.0 35.2 %copy-start.2 = (s32[1,1,2]{2,1,0:T(1,128)S(1)}, s32[1,1,2]{2,1,0:T(1,128)}, u32[]{:S(2)}) copy-start(s32[1,1,2]{2,1,0:T(1,128)} %domain_ref.1) | copy-start | bytes 28
  0.0 35.2 %copy-start.3 = (f32[256]{0:T(256)S(1)}, f32[256]{0:T(256)}, u32[]{:S(2)}) copy-start(f32[256]{0:T(256)} %param.13) | copy-start | bytes 3076
  0.0 41.4 %copy-start = (bf16[16,256,256]{2,1,0:T(8,128)(2,1)S(1)}, bf16[16,256,256]{2,1,0:T(8,128)(2,1)}, u32[]{:S(2)}) copy-start(bf16[16,256,256]{2,1,0:T(8,128)(2,1)} %own_ref.1) | copy-start | bytes 6291460
  0.0 41.4 %copy-start.4 = (s32[2,2]{1,0:T(2,128)S(1)}, s32[2,2]{1,0:T(2,128)}, u32[]{:S(2)}) copy-start(s32[2,2]{1,0:T(2,128)} %mask_ref.1) | copy-start | bytes 52
  3.2 21.8 %all-to-all-start = ((bf16[8,80,256]{2,1,0:T(8,128)(2,1)}), bf16[8,80,256]{2,1,0:T(8,128)(2,1)S(1)}, u32[]{:S(2)}, u32[]{:S(2)}) async-start(bf16[8,80,256]{2,1,0:T(8,128)(2,1)} %get-tuple-element.10), calls=%async_computation | async-start | bytes 655360 | tf_op jit(solution)/shard_map/all_to_all | solution.py:212
  11.7 21.6 %collective-permute-start = (bf16[4,256,256]{2,1,0:T(8,128)(2,1)}, bf16[4,256,256]{2,1,0:T(8,128)(2,1)S(1)}, u32[]{:S(2)}, u32[]{:S(2)}) collective-permute-start(bf16[4,256,256]{2,1,0:T(8,128)(2,1)} %get-tuple-element.11), channel_id=1, source_target_pairs={{0,8},{8,16},{16,24},{24,0},{1,9},{9,17},{17,25},{25,1},{2,10},{10... | collective-permute-start | bytes 1572872 | tf_op jit(solution)/shard_map/ppermute | solution.py:215
  13.2 20.1 %collective-permute-start.1 = (bf16[4,256,256]{2,1,0:T(8,128)(2,1)}, bf16[4,256,256]{2,1,0:T(8,128)(2,1)}, u32[]{:S(2)}, u32[]{:S(2)}) collective-permute-start(bf16[4,256,256]{2,1,0:T(8,128)(2,1)} %get-tuple-element.12), channel_id=1, source_target_pairs={{0,24},{8,0},{16,8},{24,16},{1,25},{9,1},{17,9},{25,17},{2,26},{10... | collective-permute-start | bytes 1572872 | tf_op jit(solution)/shard_map/ppermute | solution.py:216
  25.8 15.6 %all-to-all-start.1 = ((bf16[16,72,256]{2,1,0:T(8,128)(2,1)}), bf16[16,72,256]{2,1,0:T(8,128)(2,1)S(1)}, u32[]{:S(2)}, u32[]{:S(2)}) async-start(bf16[16,72,256]{2,1,0:T(8,128)(2,1)} %spread_kernel.1), calls=%async_computation.1 | async-start | bytes 1179648 | tf_op jit(solution)/shard_map/all_to_all | solution.py:218
  33.3 8.2 %copy-start.5 = (bf16[4,256,256]{2,1,0:T(8,128)(2,1)}, bf16[4,256,256]{2,1,0:T(8,128)(2,1)S(1)}, u32[]{:S(2)}) copy-start(bf16[4,256,256]{2,1,0:T(8,128)(2,1)S(1)} %collective-permute-done.up_hbm) | copy-start | bytes 1572868
  33.3 2.6 %collective-permute-start.2 = (bf16[4,256,256]{2,1,0:T(8,128)(2,1)S(1)}, bf16[4,256,256]{2,1,0:T(8,128)(2,1)S(1)}, u32[]{:S(2)}, u32[]{:S(2)}) collective-permute-start(bf16[4,256,256]{2,1,0:T(8,128)(2,1)S(1)} %collective-permute-done.up_hbm), channel_id=1, source_target_pairs={{0,128},{128,0},{1,129},{129,1},{2,130},{130,2},{3,131},{131,3},{4... | collective-permute-start | bytes 1572872 | tf_op jit(solution)/shard_map/ppermute | solution.py:217
  33.4 3.3 %collective-permute-start.3 = (bf16[4,256,256]{2,1,0:T(8,128)(2,1)}, bf16[4,256,256]{2,1,0:T(8,128)(2,1)}, u32[]{:S(2)}, u32[]{:S(2)}) collective-permute-start(bf16[4,256,256]{2,1,0:T(8,128)(2,1)} %collective-permute-done.1.down_hbm), channel_id=1, source_target_pairs={{0,128},{128,0},{1,129},{129,1},{2,130},{130,2},{3,131},{131,3},{4... | collective-permute-start | bytes 1572872 | tf_op jit(solution)/shard_map/ppermute | solution.py:217
  35.8 0.8 copy-start.6
  52.7 28.1 %copy-start.1 = (bf16[512,1,256]{2,0,1:T(8,128)(2,1)S(1)}, bf16[512,1,256]{2,0,1:T(8,128)(2,1)}, u32[]{:S(2)}) copy-start(bf16[512,1,256]{2,0,1:T(8,128)(2,1)} %param.10) | copy-start | bytes 786436

commit v15 on v12

--- a/solution.py
+++ b/solution.py
@@ -21,20 +21,19 @@
 SHARE = 4
 
 
-def out_kernel(domain_hbm, amp_hbm, ov_hbm, factors_hbm, out_ref, up_ref, down_ref, domain, amp, sems):
+def out_kernel(domain_hbm, amp_hbm, ov_hbm, factors_hbm, out_ref, up_ref, domain, amp, sems):
     x = lax.axis_index("virt")
     share = lax.axis_index("pair") * SHARE
     copies = [
         pltpu.make_async_copy(domain_hbm.at[0], domain, sems.at[0]),
         pltpu.make_async_copy(amp_hbm.at[0, 0], amp, sems.at[1]),
         pltpu.make_async_copy(factors_hbm.at[pl.ds(share, SHARE)], up_ref, sems.at[2]),
-        pltpu.make_async_copy(factors_hbm.at[pl.ds(2 * SHARE + share, SHARE)], down_ref, sems.at[3]),
     ]
     for to in range(Z):
         for high in range(2):
             start = pl.multiple_of(((2 * high + x // 2) * Z + to) * AUX + (x % 2) * PART, PART)
             target = out_ref.at[to, pl.ds(ROWS + high * PART, PART)]
-            copies.append(pltpu.make_async_copy(ov_hbm.at[pl.ds(start, PART)], target, sems.at[4 + 2 * to + high]))
+            copies.append(pltpu.make_async_copy(ov_hbm.at[pl.ds(start, PART)], target, sems.at[3 + 2 * to + high]))
     for copy in copies:
         copy.start()
     copies[0].wait()
@@ -48,6 +47,13 @@
             out_ref[to, :ROWS, cols] = rows
     for copy in copies[2:]:
         copy.wait()
+
+
+def down_kernel(factors_hbm, down_ref, sem):
+    share = lax.axis_index("pair") * SHARE
+    copy = pltpu.make_async_copy(factors_hbm.at[pl.ds(2 * SHARE + share, SHARE)], down_ref, sem)
+    copy.start()
+    copy.wait()
 
 
 def spread_kernel(got_ref, out_ref):
@@ -191,18 +197,26 @@
     hbm = pl.BlockSpec(memory_space=pltpu.HBM)
     vmem = pl.BlockSpec(memory_space=pltpu.VMEM)
     share = jax.ShapeDtypeStruct((SHARE, COLS, COLS), BF16)
-    sent, up, down = pl.pallas_call(
+    sent, up = pl.pallas_call(
         out_kernel,
         name="out_kernel",
         in_specs=[hbm, hbm, hbm, hbm],
-        out_specs=[vmem, vmem, vmem],
-        out_shape=[jax.ShapeDtypeStruct((Z, ROWS + AUX, COLS), BF16), share, share],
+        out_specs=[vmem, vmem],
+        out_shape=[jax.ShapeDtypeStruct((Z, ROWS + AUX, COLS), BF16), share],
         scratch_shapes=[
             pltpu.SMEM((1, 2), jnp.int32),
             pltpu.VMEM((ROWS, COLS), BF16),
-            pltpu.SemaphoreType.DMA((4 + 2 * Z,)),
+            pltpu.SemaphoreType.DMA((3 + 2 * Z,)),
         ],
     )(pair_domain, amplitudes, ov, vv_factors)
+    down = pl.pallas_call(
+        down_kernel,
+        name="down_kernel",
+        in_specs=[hbm],
+        out_specs=vmem,
+        out_shape=share,
+        scratch_shapes=[pltpu.SemaphoreType.DMA],
+    )(vv_factors)
     got = lax.all_to_all(sent, "z", 0, 0, tiled=True)
     sent = kernel(spread_kernel, (VIRT * Y, ROWS + PART, COLS), (), (got,))
     swap = [(0, 1), (1, 0)]

time: 82.5 us -> 83.8 us (1.016)
  waiting for transfers between devices: 14.8 us -> 12.6 us
  blocking collectives: 28 us -> 30.1 us
  Pallas kernels: 16.4 us -> 17.8 us
    all_to_all x1, waiting for transfers between devices: 10 us -> 7.8 us  [body(): got = lax.all_to_all(sent, 'z', 0, 0, tiled=True)]
    all_to_all x1, blocking collectives: 14 us -> 16.1 us  [body(): got = lax.all_to_all(sent, 'z', 0, 0, tiled=True)]
    pallas_call x0 -> x1, Pallas kernels: none -> 1.88 us  [body(): pl.pallas_call(down_kernel, name='down_kernel', in_specs=[hbm], out_specs...]
  transfers between devices with their start and end apart: 6 -> 6, of which waited for: 2 -> 2; matrix products, arithmetic and copies ran while one was open for 0% -> 0% of each run, Pallas kernels for 2% -> 4%
where the time goes in v15:
time: 83.8 us; the launch traced here: 82.8 us
  blocking collectives  30.1 us (36%)
  starting transfers between devices  20.1 us (24%)
  Pallas kernels  17.8 us (21%)
  waiting for transfers between devices  12.6 us (15%)
  between operations  1.43 us (2%)
  local copies, waits for them, and re-layouts  0.85 us (1%)
    all_to_all x1, blocking collectives, body(): got = lax.all_to_all(sent, 'z', 0, 0, tiled=True)  16.1 us
    all_to_all x1, blocking collectives, body(): got = lax.all_to_all(sent, ('virt', 'y'), 0, 0, tiled=True)  14 us
    pallas_call x1, Pallas kernels, body(): pl.pallas_call(ladder_kernel, name='ladder_kernel', in_specs=[pl.BlockSpe...  11.3 us
    all_to_all x1, starting transfers between devices, body(): got = lax.all_to_all(sent, 'z', 0, 0, tiled=True)  8.48 us
    all_to_all x1, waiting for transfers between devices, body(): got = lax.all_to_all(sent, 'z', 0, 0, tiled=True)  7.8 us
    all_to_all x1, starting transfers between devices, body(): got = lax.all_to_all(sent, ('virt', 'y'), 0, 0, tiled=True)  7.45 us
    all_to_all x1, waiting for transfers between devices, body(): got = lax.all_to_all(sent, ('virt', 'y'), 0, 0, tiled=True)  4.75 us
    pallas_call x4, Pallas kernels, kernel(): return call(*scalars, *arrays)  2.46 us
  transfers between devices with their start and end apart: 6, of which 2 were waited for; matrix products, arithmetic and copies ran while one was open for 0% of the time, Pallas kernels for 4%

profile of v15, /device:TPU:4, one launch (start us, length us, event | category | flops | bytes accessed | tf_op | source)
XLA Modules:
  0.0 82.8 jit_solution(7011559741830754613)
XLA Ops:
  0.0 2.2 %out_kernel.1 = (bf16[8,80,256]{2,1,0:T(8,128)(2,1)}, bf16[4,256,256]{2,1,0:T(8,128)(2,1)}) custom-call(s32[1,1,2]{2,1,0:T(1,128)} %domain_ref.1, bf16[1,1,64,256]{3,2,1,0:T(8,128)(2,1)} %amp_hbm.1, bf16[512,256]{1,0:T(8,128)(2,1)} %bitcast.2, bf16[16,256,256]{2,1,0:T(8,128)(2,1)} %own_ref.1), custom_call_target="tpu_custom_call" | custom-call | tf_op jit(solution)/shard_map/out_kernel/pallas_call | solution.py:200
  2.2 8.5 %all-to-all-start = ((bf16[8,80,256]{2,1,0:T(8,128)(2,1)}), bf16[8,80,256]{2,1,0:T(8,128)(2,1)S(1)}, u32[]{:S(2)}, u32[]{:S(2)}) async-start(bf16[8,80,256]{2,1,0:T(8,128)(2,1)} %get-tuple-element.9), calls=%async_computation | async-start | bytes 655360 | tf_op jit(solution)/shard_map/all_to_all | solution.py:220
  10.7 0.0 copy-start.2
  10.7 0.0 copy-start.3
  10.7 0.0 copy-start
  10.7 0.0 copy-start.4
  10.7 1.7 %collective-permute-start = (bf16[4,256,256]{2,1,0:T(8,128)(2,1)}, bf16[4,256,256]{2,1,0:T(8,128)(2,1)S(1)}, u32[]{:S(2)}, u32[]{:S(2)}) collective-permute-start(bf16[4,256,256]{2,1,0:T(8,128)(2,1)} %get-tuple-element.10), channel_id=1, source_target_pairs={{0,8},{8,16},{16,24},{24,0},{1,9},{9,17},{17,25},{25,1},{2,10},{10... | collective-permute-start | bytes 1572872 | tf_op jit(solution)/shard_map/ppermute | solution.py:223
  12.4 1.9 %down_kernel.1 = bf16[4,256,256]{2,1,0:T(8,128)(2,1)} custom-call(bf16[16,256,256]{2,1,0:T(8,128)(2,1)} %own_ref.1), custom_call_target="tpu_custom_call" | custom-call | tf_op jit(solution)/shard_map/down_kernel/pallas_call | solution.py:212
  14.2 1.9 %collective-permute-start.1 = (bf16[4,256,256]{2,1,0:T(8,128)(2,1)}, bf16[4,256,256]{2,1,0:T(8,128)(2,1)}, u32[]{:S(2)}, u32[]{:S(2)}) collective-permute-start(bf16[4,256,256]{2,1,0:T(8,128)(2,1)} %down_kernel.1), channel_id=1, source_target_pairs={{0,24},{8,0},{16,8},{24,16},{1,25},{9,1},{17,9},{25,17},{2,26},{10... | collective-permute-start | bytes 1572872 | tf_op jit(solution)/shard_map/ppermute | solution.py:224
  16.1 7.8 %all-to-all-done.got_ref = bf16[8,80,256]{2,1,0:T(8,128)(2,1)S(1)} async-done(((bf16[8,80,256]{2,1,0:T(8,128)(2,1)}), bf16[8,80,256]{2,1,0:T(8,128)(2,1)S(1)}, u32[]{:S(2)}, u32[]{:S(2)}) %all-to-all-start) | async-done | bytes 327712 | tf_op jit(solution)/shard_map/all_to_all | solution.py:220
  23.9 0.9 %spread_kernel.1 = bf16[16,72,256]{2,1,0:T(8,128)(2,1)} custom-call(bf16[8,80,256]{2,1,0:T(8,128)(2,1)S(1)} %all-to-all-done.got_ref), custom_call_target="tpu_custom_call" | custom-call | tf_op jit(solution)/shard_map/spread_kernel/pallas_call | solution.py:183
  24.8 7.5 %all-to-all-start.1 = ((bf16[16,72,256]{2,1,0:T(8,128)(2,1)}), bf16[16,72,256]{2,1,0:T(8,128)(2,1)S(1)}, u32[]{:S(2)}, u32[]{:S(2)}) async-start(bf16[16,72,256]{2,1,0:T(8,128)(2,1)} %spread_kernel.1), calls=%async_computation.1 | async-start | bytes 1179648 | tf_op jit(solution)/shard_map/all_to_all | solution.py:226
  32.2 0.0 collective-permute-done.up_hbm
  32.3 0.0 copy-start.5
  32.3 0.1 collective-permute-start.2
  32.4 0.0 collective-permute-done.1.down_hbm
  32.4 0.5 collective-permute-start.3
  34.2 0.0 copy-done.2
  34.2 0.0 copy-done.3
  34.2 0.6 scale_kernel.1.scale_ref
  34.8 0.0 collective-permute-done.2.up2_hbm
  34.8 0.0 copy-start.6
  34.9 0.8 copy-done.6
  35.7 0.0 collective-permute-done.3.down2_hbm
  35.7 4.8 %all-to-all-done.1.rows_ref = bf16[16,72,256]{2,1,0:T(8,128)(2,1)S(1)} async-done(((bf16[16,72,256]{2,1,0:T(8,128)(2,1)}), bf16[16,72,256]{2,1,0:T(8,128)(2,1)S(1)}, u32[]{:S(2)}, u32[]{:S(2)}) %all-to-all-start.1) | async-done | bytes 589856 | tf_op jit(solution)/shard_map/all_to_all | solution.py:226
  40.4 0.0 copy-done.5
  40.4 0.0 copy-done
  40.4 0.0 copy-done.4
  40.4 11.3 %ladder_kernel.1 = bf16[16,72,256]{2,1,0:T(8,128)(2,1)S(1)} custom-call(s32[2,2]{1,0:T(2,128)S(1)} %copy-done.4, bf16[16,72,256]{2,1,0:T(8,128)(2,1)S(1)} %all-to-all-done.1.rows_ref, bf16[16,256,256]{2,1,0:T(8,128)(2,1)S(1)} %copy-done, bf16[4,256,256]{2,1,0:T(8,128)(2,1)} %copy-done.5, bf16[4,256,256]{2,1,0:T(8,128)(2,1)} %collective-permute-done.1.down_hbm, ...), custom_call_target="tpu_custom_call" | custom-call | tf_op jit(solution)/shard_map/ladder_kernel/pallas_call | solution.py:228
  51.7 0.0 copy-start.1
  51.7 14.0 %all_to_all.20.got_ref = bf16[16,72,256]{2,1,0:T(8,128)(2,1)S(1)} all-to-all(bf16[16,72,256]{2,1,0:T(8,128)(2,1)S(1)} %ladder_kernel.1), channel_id=1, replica_groups=mesh['pair'=2,'virt'=4,'y'=4,'z'=8] {'virt','y'}, dimensions={0} | all-to-all | bytes 1179648 | tf_op jit(solution)/shard_map/all_to_all | solution.py:245
  65.7 0.1 sum_kernel.1
  65.8 16.1 %all_to_all.21.got_ref = bf16[8,80,256]{2,1,0:T(8,128)(2,1)S(1)} all-to-all(bf16[8,80,256]{2,1,0:T(8,128)(2,1)S(1)} %sum_kernel.1), channel_id=1, replica_groups=mesh['pair'=2,'virt'=4,'y'=4,'z'=8] {'z'}, dimensions={0} | all-to-all | bytes 655360 | tf_op jit(solution)/shard_map/all_to_all | solution.py:247
  82.0 0.0 copy-done.1
  82.0 0.9 %update_kernel.1 = bf16[1,1,64,256]{3,2,1,0:T(8,128)(2,1)} custom-call(bf16[8,80,256]{2,1,0:T(8,128)(2,1)S(1)} %all_to_all.21.got_ref, bf16[512,256]{1,0:T(8,128)(2,1)S(1)} %bitcast.3, f32[64,256]{1,0:T(8,128)S(1)} %scale_kernel.1.scale_ref), custom_call_target="tpu_custom_call" | custom-call | tf_op jit(solution)/shard_map/update_kernel/pallas_call | solution.py:183
Async XLA Ops:
  2.2 21.8 %all-to-all-start = ((bf16[8,80,256]{2,1,0:T(8,128)(2,1)}), bf16[8,80,256]{2,1,0:T(8,128)(2,1)S(1)}, u32[]{:S(2)}, u32[]{:S(2)}) async-start(bf16[8,80,256]{2,1,0:T(8,128)(2,1)} %get-tuple-element.9), calls=%async_computation | async-start | bytes 655360 | tf_op jit(solution)/shard_map/all_to_all | solution.py:220
  10.7 23.5 %copy-start.2 = (s32[1,1,2]{2,1,0:T(1,128)S(1)}, s32[1,1,2]{2,1,0:T(1,128)}, u32[]{:S(2)}) copy-start(s32[1,1,2]{2,1,0:T(1,128)} %domain_ref.1) | copy-start | bytes 28
  10.7 23.5 %copy-start.3 = (f32[256]{0:T(256)S(1)}, f32[256]{0:T(256)}, u32[]{:S(2)}) copy-start(f32[256]{0:T(256)} %param.13) | copy-start | bytes 3076
  10.7 29.8 %copy-start = (bf16[16,256,256]{2,1,0:T(8,128)(2,1)S(1)}, bf16[16,256,256]{2,1,0:T(8,128)(2,1)}, u32[]{:S(2)}) copy-start(bf16[16,256,256]{2,1,0:T(8,128)(2,1)} %own_ref.1) | copy-start | bytes 6291460
  10.7 29.8 %copy-start.4 = (s32[2,2]{1,0:T(2,128)S(1)}, s32[2,2]{1,0:T(2,128)}, u32[]{:S(2)}) copy-start(s32[2,2]{1,0:T(2,128)} %mask_ref.1) | copy-start | bytes 52
  10.7 21.6 %collective-permute-start = (bf16[4,256,256]{2,1,0:T(8,128)(2,1)}, bf16[4,256,256]{2,1,0:T(8,128)(2,1)S(1)}, u32[]{:S(2)}, u32[]{:S(2)}) collective-permute-start(bf16[4,256,256]{2,1,0:T(8,128)(2,1)} %get-tuple-element.10), channel_id=1, source_target_pairs={{0,8},{8,16},{16,24},{24,0},{1,9},{9,17},{17,25},{25,1},{2,10},{10... | collective-permute-start | bytes 1572872 | tf_op jit(solution)/shard_map/ppermute | solution.py:223
  14.2 18.1 %collective-permute-start.1 = (bf16[4,256,256]{2,1,0:T(8,128)(2,1)}, bf16[4,256,256]{2,1,0:T(8,128)(2,1)}, u32[]{:S(2)}, u32[]{:S(2)}) collective-permute-start(bf16[4,256,256]{2,1,0:T(8,128)(2,1)} %down_kernel.1), channel_id=1, source_target_pairs={{0,24},{8,0},{16,8},{24,16},{1,25},{9,1},{17,9},{25,17},{2,26},{10... | collective-permute-start | bytes 1572872 | tf_op jit(solution)/shard_map/ppermute | solution.py:224
  24.8 15.6 %all-to-all-start.1 = ((bf16[16,72,256]{2,1,0:T(8,128)(2,1)}), bf16[16,72,256]{2,1,0:T(8,128)(2,1)S(1)}, u32[]{:S(2)}, u32[]{:S(2)}) async-start(bf16[16,72,256]{2,1,0:T(8,128)(2,1)} %spread_kernel.1), calls=%async_computation.1 | async-start | bytes 1179648 | tf_op jit(solution)/shard_map/all_to_all | solution.py:226
  32.3 8.2 %copy-start.5 = (bf16[4,256,256]{2,1,0:T(8,128)(2,1)}, bf16[4,256,256]{2,1,0:T(8,128)(2,1)S(1)}, u32[]{:S(2)}) copy-start(bf16[4,256,256]{2,1,0:T(8,128)(2,1)S(1)} %collective-permute-done.up_hbm) | copy-start | bytes 1572868
  32.3 2.6 %collective-permute-start.2 = (bf16[4,256,256]{2,1,0:T(8,128)(2,1)S(1)}, bf16[4,256,256]{2,1,0:T(8,128)(2,1)S(1)}, u32[]{:S(2)}, u32[]{:S(2)}) collective-permute-start(bf16[4,256,256]{2,1,0:T(8,128)(2,1)S(1)} %collective-permute-done.up_hbm), channel_id=1, source_target_pairs={{0,128},{128,0},{1,129},{129,1},{2,130},{130,2},{3,131},{131,3},{4... | collective-permute-start | bytes 1572872 | tf_op jit(solution)/shard_map/ppermute | solution.py:225
  32.4 3.3 %collective-permute-start.3 = (bf16[4,256,256]{2,1,0:T(8,128)(2,1)}, bf16[4,256,256]{2,1,0:T(8,128)(2,1)}, u32[]{:S(2)}, u32[]{:S(2)}) collective-permute-start(bf16[4,256,256]{2,1,0:T(8,128)(2,1)} %collective-permute-done.1.down_hbm), channel_id=1, source_target_pairs={{0,128},{128,0},{1,129},{129,1},{2,130},{130,2},{3,131},{131,3},{4... | collective-permute-start | bytes 1572872 | tf_op jit(solution)/shard_map/ppermute | solution.py:225
  34.8 0.8 %copy-start.6 = (bf16[4,256,256]{2,1,0:T(8,128)(2,1)}, bf16[4,256,256]{2,1,0:T(8,128)(2,1)S(1)}, u32[]{:S(2)}) copy-start(bf16[4,256,256]{2,1,0:T(8,128)(2,1)S(1)} %collective-permute-done.2.up2_hbm) | copy-start | bytes 1572868
  51.7 30.2 %copy-start.1 = (bf16[512,1,256]{2,0,1:T(8,128)(2,1)S(1)}, bf16[512,1,256]{2,0,1:T(8,128)(2,1)}, u32[]{:S(2)}) copy-start(bf16[512,1,256]{2,0,1:T(8,128)(2,1)} %param.10) | copy-start | bytes 786436
